TPU v7x, 32 devices: a whole 2x2x4 slice. The times are simulated.
32 devices in a mesh: grp: 2 (over x), tile: 16 (over z, y, core).
Axes of the slice: x: 2, y: 2, z: 4, core: 2. Of those that a mesh axis runs over, the one named last changes fastest.
Arguments:
- mask_params: float32 [64, 64, 128], P(('grp', 'tile')), parts along dimension 0, may hold values from -3 to 3
- target: float32 [64, 64, 128], P(('grp', 'tile')), parts along dimension 0, may hold values from 0 to 1
- weight: float32 [64, 64, 128], P(('grp', 'tile')), parts along dimension 0, may hold values from 0.3 to 3
- kernels: float32 [24, 2, 65, 65], replicated, may hold values from -0.25515518 to 0.25515518
- kernel_weight: float32 [24], replicated, may hold values from 0.05 to 1
- tile_ids: int32 [64], P(('grp', 'tile')), parts along dimension 0, may hold values from -1 to 134, as said below
- tile_links: int32 [64, 2], P(('grp', 'tile')), parts along dimension 0, may hold values from 0 to 1, as said below
Outputs:
- params_out: float32 [64, 64, 128], P(('grp', 'tile')), parts along dimension 0
- resist: float32 [64, 64, 128], P(('grp', 'tile')), parts along dimension 0
There are 2 independent parts, one for each index of `grp`. A program takes and returns all parts, laid end to end along the dimension named above; an argument that names none is the same for every part. Nothing has to cross between parts.
Inputs may be any that keep to these rules, and one draw needn't show every extreme that they name: `tile_ids`: -1 marks an empty slot. Every device holds between 1 and 2 tiles in its first slots and some device holds 2; stripe columns rise strictly in the order of devices and slots, and the last live tile of the stripe holds column 134. `tile_links`: entry 0 is 1 exactly where the stripe column just before the slot's tile holds an active tile (then held by the previous live slot in order), entry 1 likewise for the column just after (the next live slot); both are 0 for empty slots.
All inputs are finite; a program needn't handle non-finite values.
Results may differ from a plain program's by a relative error of at most 0.00011.
Values sent between devices are 32-bit elements; how exact they have to be, the bound alone decides.
No kernel may reach another device: no remote copies, remote signals or barrier semaphores. Data moves between devices by JAX's collectives and lax.ppermute only.
A program may use at most 64 MiB of HBM per device.

v0:
```python
import functools
import math

import jax
import jax.numpy as jnp
import numpy as np
from jax import lax
from jax.experimental import pallas as pl
from jax.experimental.pallas import tpu as pltpu
from jax.sharding import PartitionSpec as P

ITERS = 2
RESIST_SLOPE = 4.0
THRESHOLD = 0.9
STEP_SCALE = 0.04
GROUP = 8
MID = 16
F32 = jnp.float32
BF16 = jnp.bfloat16


def snake_ring(groups, count, step):
    order = []
    for g in range(groups):
        span = range(count) if g % 2 == 0 else range(count - 1, -1, -1)
        order += [g * count + i for i in span]
    total = len(order)
    return [(order[j], order[(j + step) % total]) for j in range(total)]


def split_np(table):
    table = np.asarray(table, np.float32)
    high = table.astype(jnp.bfloat16)
    low = (table - high.astype(np.float32)).astype(jnp.bfloat16)
    return high, low


class Tables:
    def __init__(self, rows, cols, bands):
        half = (bands - 1) // 2
        self.half = half
        area = 1.0 / (rows * cols)
        self.area = area
        pos = np.arange(1, half + 1)
        angle = (np.arange(rows)[:, None] * pos[None, :] % (2 * rows)) * (np.pi / rows)
        ty = np.zeros((rows, 2 * half + MID))
        ty[:, :half] = np.cos(angle)
        ty[:, half] = 1.0
        ty[:, half + MID :] = np.sin(angle)
        freq = np.concatenate([np.arange(-half, 0), np.arange(1, half + 1)])
        self.nf = len(freq)
        period = 3 * cols
        theta = (np.arange(period)[:, None] * freq[None, :] % period) * (2.0 * np.pi / period)
        c, s = np.cos(theta), np.sin(theta)
        co, so = c[cols : 2 * cols].T, s[cols : 2 * cols].T
        forward = np.block([[co, so], [-so, co]])
        adjoint = np.block([[co.T, so.T], [so.T, -co.T]])
        gradient = np.concatenate([c.T, s.T], 0) * (2.0 * area)
        spectrum = np.concatenate([c, -s], 1) * area

        def left(table):
            h, l = split_np(table)
            return np.concatenate([h, h, l], 1)

        def right(table):
            h, l = split_np(table)
            return np.concatenate([h, h, l], 0)

        part = np.arange(2 * self.nf) // (self.nf // 2) % 2
        ones = np.zeros((2 * self.nf, 2 * cols))
        ones[part == 0, :cols] = 1.0
        ones[part == 1, cols:] = 1.0
        sums = np.concatenate([ones.T, ones.T, np.zeros_like(ones.T)], 0).astype(jnp.bfloat16)
        sums[cols : 2 * cols] *= -1
        sums[3 * cols : 4 * cols] *= -1
        picks = np.zeros((self.nf // 2, MID, 2 * self.nf), jnp.bfloat16)
        for k in range(self.nf // 2):
            picks[k, :, k :: self.nf // 2] = 1.0

        def wide(table):
            h, l = split_np(table)
            top = np.concatenate([h, l], 1)
            return np.concatenate([top, np.concatenate([h, np.zeros_like(l)], 1)], 0)

        self.arrays = dict(
            ty=left(ty),
            tyt=left(ty.T),
            fwd=np.concatenate([right(forward), ones.astype(jnp.bfloat16)], 0),
            picks=picks,
            adj=np.concatenate([right(adjoint), sums], 1),
            grad=right(gradient),
            spec=np.stack([wide(spectrum[j * cols : (j + 1) * cols]) for j in range(3)]),
        )
        order = np.zeros((2 * half + 8, 2 * half + 8), jnp.bfloat16)
        for j in range(half):
            order[j, half + 1 + j] = 1.0
            order[half + 8 + j, half - 1 - j] = 1.0
        order[half, half] = 1.0
        self.order = order


def split(v):
    high = v.astype(BF16)
    return high, (v - high.astype(F32)).astype(BF16)


def dot(a, b):
    return jnp.dot(a, b, preferred_element_type=F32)


def lanes3(v):
    high, low = split(v)
    return jnp.concatenate([high, low, high], 1)


def rows3(v):
    high, low = split(v)
    return jnp.concatenate([high, low, high], 0)


def wide_dot(v, table):
    high, low = split(v)
    o = dot(jnp.concatenate([high, low], 1), table)
    n = o.shape[1] // 2
    return o[:, :n] + o[:, n:]


def lane_of(shape):
    return lax.broadcasted_iota(jnp.int32, shape, 1)


def swap(v, block):
    n = v.shape[1]
    if 2 * block == n:
        return pltpu.roll(v, block, 1)
    even = lax.rem(lax.div(lane_of(v.shape), block), 2) == 0
    return jnp.where(even, pltpu.roll(v, n - block, 1), pltpu.roll(v, block, 1))


def conj(v, block):
    even = lax.rem(lax.div(lane_of((1, v.shape[1])), block), 2) == 0
    return v * jnp.where(even, 1.0, -1.0)


def minus_i(v, block):
    return conj(swap(v, block), block)


def fold(half, plus, zero, minus):
    gap = jnp.zeros((MID - 8, plus.shape[1]), F32)
    return jnp.concatenate([plus, zero, gap, minus], 0)


def spread(half, o, block):
    cosine, zero, sine = o[:half], o[half : half + 8], minus_i(o[half + MID :], block)
    return jnp.concatenate([cosine + sine, zero, cosine - sine], 0)


def drive(half, a, b, u):
    p, m = slice(0, half), slice(half + 8, 2 * half + 8)
    d = a * u[0] + b * u[1]
    turned_p = a[p] * u[2][p] + b[p] * u[3][p]
    turned_m = a[m] * u[2][m] + b[m] * u[3][m]
    return fold(half, d[p] + d[m], d[half : half + 8], turned_p - turned_m)


def phases(u, block):
    v = swap(u, block)
    return u, v, -conj(v, block), conj(u, block)


def gather(half, q, a, b, o, block):
    p, z, m = slice(0, half), slice(half, half + 8), slice(half + 8, 2 * half + 8)
    c, zero, s = o[:half], o[half : half + 8], conj(o[half + MID :], block)
    parts = [
        a[p] * c + b[p] * s,
        a[z] * zero,
        a[m] * c - b[m] * s,
        b[p] * c - a[p] * s,
        b[z] * zero,
        b[m] * c + a[m] * s,
    ]
    return parts if q is None else [x + y for x, y in zip(q, parts)]


def back_rows(half, q, block):
    p, z, m = (q[j] - swap(q[j + 3], block) for j in range(3))
    return fold(half, p + m, z, minus_i(p - m, block))


def lane_sum(v):
    return jnp.sum(v, axis=1, keepdims=True)


def core(tb, dom, target, weight, ha_ref, hb_ref, h0, t, e_ref, keep=None):
    half, nf = tb.half, tb.nf
    slots, rows, cols = target.shape
    kcount = ha_ref.shape[0]
    wl = 2 * nf
    zb = wl // (2 * slots)
    ty, tyt = t["ty"], t["tyt"]
    thirds_of = [dom[:, j * cols : (j + 1) * cols] for j in range(3)]
    g = sum(wide_dot(v, t["spec"][j]) for j, v in enumerate(thirds_of))
    gw = jnp.concatenate([g[s * rows : (s + 1) * rows] for s in range(slots)], 1)
    spec = dot(tyt[...], rows3(gw))
    us = [phases(spread(half, spec[:, s * wl : (s + 1) * wl], nf), nf) for s in range(slots)]
    g0 = lane_sum(thirds_of[0] + thirds_of[1] + thirds_of[2]) * tb.area
    block = lax.div(lane_of((rows, wl)), zb)
    g0w = jnp.zeros((rows, wl), F32)
    for s in range(slots):
        g0w = jnp.where(block == 2 * s, g0[s * rows : (s + 1) * rows], g0w)
    u0 = phases(spread(half, dot(tyt[...], rows3(g0w)), zb), zb)
    a0, b0 = h0[0], h0[1]
    r0 = dot(ty[...], rows3(drive(half, a0, b0, u0)))
    r0h, r0l = split(r0)
    r0l = pltpu.roll(r0l.astype(F32), wl // 2, 1)
    r0s = [
        jnp.where(lax.div(block, 2) == s, r0h.astype(F32), r0l).astype(BF16) for s in range(slots)
    ]
    inner = lax.rem(lane_of((rows, wl)), zb)
    groups = [range(k0, min(k0 + GROUP, kcount)) for k0 in range(0, kcount, GROUP)]

    def in_pairs(ks):
        return [ks[i : i + 2] for i in range(0, len(ks), 2)]

    def row_stage(s, ks):
        out, extra = [], []
        for pair in in_pairs(ks):
            w = jnp.concatenate([drive(half, ha_ref[k], hb_ref[k], us[s]) for k in pair], 1)
            r = dot(ty[...], rows3(w))
            for n, k in enumerate(pair):
                out.append(r[:, n * wl : (n + 1) * wl])
                extra += [r0s[s][i : i + MID] * t["picks"][k] for i in range(0, rows, MID)]
        return jnp.concatenate([lanes3(jnp.concatenate(out, 0)), jnp.concatenate(extra, 0)], 1)

    def field_stage(s, ks, ready, inten):
        field = dot(ready, t["fwd"][...])
        for n, k in enumerate(ks):
            e = field[n * rows : (n + 1) * rows]
            e_ref[s, k] = e
            inten = inten + (e[:, :cols] * e[:, :cols] + e[:, cols:] * e[:, cols:])
        return inten

    def slope_of(s, inten):
        resist = jax.nn.sigmoid(RESIST_SLOPE * (inten - THRESHOLD))
        slope = 2.0 * weight[s] * (resist - target[s]) * RESIST_SLOPE * resist * (1.0 - resist)
        return resist, jnp.concatenate([slope, slope], 1)

    def column_stage(s, ks, slope2):
        back = jnp.concatenate([e_ref[s, k] * slope2 for k in ks], 0)
        return dot(lanes3(back), t["adj"][...])

    def sum_stage(s, ks, ready, c0, q):
        for m, pair in enumerate(in_pairs(ks)):
            parts = [ready[(2 * m + n) * rows : (2 * m + n + 1) * rows] for n in range(len(pair))]
            o = dot(tyt[...], rows3(jnp.concatenate([v[:, :wl] for v in parts], 1)))
            for n, k in enumerate(pair):
                c0 = jnp.where(inner == k, parts[n][:, wl:], c0)
                q = gather(half, q, ha_ref[k], hb_ref[k], o[:, n * wl : (n + 1) * wl], nf)
        return c0, q

    def finish(s, c0, q):
        own = lax.div(block, 2) == s
        q0 = gather(half, None, a0, b0, dot(tyt[...], rows3(jnp.where(own, c0, 0.0))), zb)
        ug = dot(ty[...], rows3(back_rows(half, q, nf)))
        ug0 = dot(ty[...], rows3(back_rows(half, q0, zb)))
        flat = lane_sum(jnp.where(block == 2 * s, ug0, 0.0))
        return dot(lanes3(ug), t["grad"][...]) + (2.0 * tb.area) * flat

    grads = []
    slope2 = None
    for s in range(slots + 1):
        forward, backward = s < slots, s > 0
        inten = jnp.zeros((rows, cols), F32)
        c0, q = jnp.zeros((rows, wl), F32), None
        ahead_f = row_stage(s, groups[0]) if forward else None
        ahead_b = column_stage(s - 1, groups[0], slope2) if backward else None
        for j, ks in enumerate(groups):
            now_f, now_b = ahead_f, ahead_b
            more = j + 1 < len(groups)
            if forward and more:
                ahead_f = row_stage(s, groups[j + 1])
            if backward and more:
                ahead_b = column_stage(s - 1, groups[j + 1], slope2)
            if forward:
                inten = field_stage(s, ks, now_f, inten)
            if backward:
                c0, q = sum_stage(s - 1, ks, now_b, c0, q)
        if backward:
            grads.append(finish(s - 1, c0, q))
        if forward:
            resist, slope2 = slope_of(s, inten)
            if keep is not None:
                keep(s, resist)
    return grads


def read_flags(ids, links):
    both = ids[1] >= 0
    even = lax.rem(lax.axis_index("grp"), 2) == 0
    return both, links[0, 0] == 1, links[1, 0] == 1, links[0, 1] == 1, links[1, 1] == 1, even


def in_order(even, first, second):
    return jnp.where(even, first, second), jnp.where(even, second, first)


def domain_of(flags, prev, own0, own1, nxt):
    both, l0, l1, r0, r1, _ = flags
    zero = jnp.zeros_like(own0)
    first = [jnp.where(l0, prev, zero), own0, jnp.where(r0, jnp.where(both, own1, nxt), zero)]
    second = [jnp.where(l1, own0, zero), own1, jnp.where(r1, nxt, zero)]
    return jnp.concatenate([jnp.concatenate(first, 1), jnp.concatenate(second, 1)], 0)


def thirds(flags, dg):
    both, l0, l1, r0, r1, _ = flags
    cols = dg[0].shape[1] // 3
    left0, mid0, right0 = (dg[0][:, j * cols : (j + 1) * cols] for j in range(3))
    left1, mid1, right1 = (dg[1][:, j * cols : (j + 1) * cols] for j in range(3))
    part0 = mid0 + jnp.where(jnp.logical_and(r0, both), left1, 0.0)
    part1 = mid1 + jnp.where(l1, right0, 0.0)
    return part0, part1, jnp.where(both, right1, right0), left0


def own_gradient(flags, part0, part1, from_prev, from_next):
    both, l0, l1, r0, r1, _ = flags
    g0 = part0 + jnp.where(l0, from_prev, 0.0)
    g0 = g0 + jnp.where(jnp.logical_and(r0, jnp.logical_not(both)), from_next, 0.0)
    return g0, part1 + jnp.where(jnp.logical_and(r1, both), from_next, 0.0)


def stepped(step, params, gradient):
    transmit = jnp.tanh(params)
    return params - step * gradient * (1.0 - transmit * transmit)


def kernel_first(tb, names, ids, links, mp, got_a, got_b, target, weight, ha, hb, h0, *rest):
    t = dict(zip(names, rest))
    part, send_a, send_b, e_ref = rest[len(names) :]
    flags = read_flags(ids, links)
    prev, nxt = in_order(flags[5], got_a[...], got_b[...])
    tile = [jnp.tanh(v) for v in (prev, mp[0], mp[1], nxt)]
    dg = core(tb, domain_of(flags, *tile), target, weight, ha, hb, h0, t, e_ref)
    part[0], part[1], to_next, to_prev = thirds(flags, dg)
    send_a[...], send_b[...] = in_order(flags[5], to_next, to_prev)


def kernel_update(step, ids, links, part, params, got_a, got_b, out, send_a, send_b):
    flags = read_flags(ids, links)
    prev, nxt = in_order(flags[5], got_a[...], got_b[...])
    g0, g1 = own_gradient(flags, part[0], part[1], prev, nxt)
    new0 = stepped(step, params[0], g0)
    new1 = jnp.where(flags[0], stepped(step, params[1], g1), params[1])
    out[0], out[1] = new0, new1
    send_a[...], send_b[...] = in_order(flags[5], jnp.where(flags[0], new1, new0), new0)


def kernel_second(tb, names, ids, links, mp, got_a, got_b, target, weight, ha, hb, h0, *rest):
    t = dict(zip(names, rest))
    part, resist_out, send_a, send_b, e_ref, resist_v, sems = rest[len(names) :]
    flags = read_flags(ids, links)
    prev, nxt = in_order(flags[5], got_a[...], got_b[...])
    tile = [jnp.tanh(v) for v in (prev, mp[0], mp[1], nxt)]
    moves = []

    def keep(s, resist):
        resist_v[s] = resist if s == 0 else jnp.where(flags[0], resist, 0.0)
        moves.append(pltpu.make_async_copy(resist_v.at[s], resist_out.at[s], sems.at[s]))
        moves[-1].start()

    dg = core(tb, domain_of(flags, *tile), target, weight, ha, hb, h0, t, e_ref, keep)
    part[0], part[1], to_next, to_prev = thirds(flags, dg)
    send_a[...], send_b[...] = in_order(flags[5], to_next, to_prev)
    for move in moves:
        move.wait()


def kernel_last(step, ids, links, part, params, got_a, got_b, out):
    flags = read_flags(ids, links)
    prev, nxt = in_order(flags[5], got_a[...], got_b[...])
    g0, g1 = own_gradient(flags, part[0], part[1], prev, nxt)
    out[0] = stepped(step, params[0], g0)
    out[1] = jnp.where(flags[0], stepped(step, params[1], g1), params[1])


def kernel_arrange(tb, slots, weights, kernels, order, out_a, out_b, out_0, padded):
    half, nf = tb.half, tb.nf
    frows, wl = 2 * half + 8, 2 * nf
    bands = kernels.shape[3]
    zb = wl // (2 * slots)
    lane = lane_of((frows, wl))
    inner = lax.rem(lane, zb)
    roots = jnp.sqrt(weights[...])
    zeros = [jnp.zeros((frows, wl), F32) for _ in range(2)]
    padded[...] = jnp.zeros(padded.shape, F32)
    for k in range(kernels.shape[0]):
        root = jnp.broadcast_to(roots[:, k : k + 1], (1, bands))
        for part in range(2):
            padded[k, part, :bands, :bands] = kernels[k, part] * root
    for k in range(kernels.shape[0]):
        for part in range(2):
            high, low = split(padded[k, part])
            v = dot(order[...], high) + dot(order[...], low)
            zero = jnp.broadcast_to(v[:, half : half + 1], (frows, wl))
            zeros[part] = jnp.where(inner == k, zero, zeros[part])
            v = jnp.where(lane < half, v, pltpu.roll(v, wl - 1, 1))
            v = jnp.where(lane < nf, v, pltpu.roll(v, nf, 1))
            if part == 0:
                out_a[k] = v
            else:
                out_b[k] = -conj(v, nf)
    out_0[0] = zeros[0]
    out_0[1] = -conj(zeros[1], zb)


def kernel_choose(ids, params, send_a, send_b, ids_s, params_v, sems):
    move_ids = pltpu.make_async_copy(ids, ids_s, sems.at[0])
    move = pltpu.make_async_copy(params, params_v, sems.at[1])
    move_ids.start()
    move.start()
    move_ids.wait()
    move.wait()
    even = lax.rem(lax.axis_index("grp"), 2) == 0
    last = jnp.where(ids_s[1] >= 0, params_v[1], params_v[0])
    send_a[...], send_b[...] = in_order(even, last, params_v[0])


def choose(tile_ids, mask_params):
    tile = mask_params.shape[1:]
    anywhere = pl.BlockSpec(memory_space=pltpu.HBM)
    return pl.pallas_call(
        kernel_choose,
        in_specs=[anywhere] * 2,
        out_specs=[pl.BlockSpec(memory_space=pltpu.VMEM)] * 2,
        out_shape=[jax.ShapeDtypeStruct(tile, F32)] * 2,
        scratch_shapes=[
            pltpu.SMEM(tile_ids.shape, jnp.int32),
            pltpu.VMEM(mask_params.shape, F32),
            pltpu.SemaphoreType.DMA((2,)),
        ],
        compiler_params=pltpu.CompilerParams(vmem_limit_bytes=4 << 20),
    )(*(pltpu.with_memory_space_constraint(v, pltpu.HBM) for v in (tile_ids, mask_params)))


def call(body, ins, outs, scratch=(), scalars=2, limit=32 << 20, moved=()):
    smem = pl.BlockSpec(memory_space=pltpu.SMEM)
    vmem = pl.BlockSpec(memory_space=pltpu.VMEM)
    return pl.pallas_call(
        body,
        in_specs=[smem] * scalars + [vmem] * (len(ins) - scalars),
        out_specs=[
            pl.BlockSpec(memory_space=pltpu.HBM) if i in moved else vmem for i in range(len(outs))
        ],
        out_shape=[jax.ShapeDtypeStruct(s, F32) for s in outs],
        scratch_shapes=list(scratch),
        compiler_params=pltpu.CompilerParams(vmem_limit_bytes=limit),
    )(*ins)


def local(mesh_shape, mask_params, target, weight, kernels, kernel_weight, tile_ids, tile_links):
    slots, rows, cols = mask_params.shape
    bands = kernels.shape[2]
    kcount = kernels.shape[0]
    groups, count = mesh_shape
    step = STEP_SCALE * math.sqrt(rows * cols)
    tb = Tables(rows, cols, bands)
    names = tuple(tb.arrays)
    tables = [jnp.asarray(tb.arrays[n]) for n in names]
    axes = ("grp", "tile")

    ring_a = snake_ring(groups, count, 1)
    ring_b = snake_ring(groups, count, -1)

    def exchange(a, b):
        return lax.ppermute(a, axes, ring_a), lax.ppermute(b, axes, ring_b)

    got = exchange(*choose(tile_ids, mask_params))
    frows = 2 * tb.half + 8
    arranged = call(
        functools.partial(kernel_arrange, tb, slots),
        [kernel_weight[None], kernels, jnp.asarray(tb.order)],
        [(kcount, frows, 2 * tb.nf)] * 2 + [(2, frows, 2 * tb.nf)],
        [pltpu.VMEM((kcount, 2, frows, 2 * tb.nf), F32)],
        scalars=0,
    )
    field = pltpu.VMEM((slots, kcount, rows, 2 * cols), F32)
    whole, tile = mask_params.shape, (rows, cols)
    part, sa, sb = call(
        functools.partial(kernel_first, tb, names),
        [tile_ids, tile_links, mask_params, *got, target, weight, *arranged, *tables],
        [whole, tile, tile],
        [field],
    )
    params, sa, sb = call(
        functools.partial(kernel_update, step),
        [tile_ids, tile_links, part, mask_params, *exchange(sa, sb)],
        [whole, tile, tile],
    )
    part, resist, sa, sb = call(
        functools.partial(kernel_second, tb, names),
        [tile_ids, tile_links, params, *exchange(sa, sb), target, weight, *arranged, *tables],
        [whole, whole, tile, tile],
        [field, pltpu.VMEM(whole, F32), pltpu.SemaphoreType.DMA((slots,))],
        moved=(1,),
    )
    (out,) = call(
        functools.partial(kernel_last, step),
        [tile_ids, tile_links, part, params, *exchange(sa, sb)],
        [whole],
    )
    return (out, resist)


def solution(mesh):
    tiles = P(("grp", "tile"), None, None)
    return jax.shard_map(
        functools.partial(local, (mesh.shape["grp"], mesh.shape["tile"])),
        mesh=mesh,
        in_specs=(tiles, tiles, tiles, P(), P(), P(("grp", "tile")), P(("grp", "tile"), None)),
        out_specs=(tiles, tiles),
        check_vma=False,
    )
```

profile of v0, /device:TPU:21, one launch (start us, length us, event | category | flops | bytes accessed | tf_op | source)
XLA Modules:
  0.0 37.6 jit_solution(9991476279499011778)
XLA Ops:
  0.6 0.0 copy-start.10
  0.6 0.0 copy-start.13
  0.7 0.9 %shard_map.158 = (f32[64,128]{1,0:T(8,128)S(1)}, f32[64,128]{1,0:T(8,128)S(1)}) custom-call(s32[2]{0:T(128)} %ids.9, f32[2,64,128]{2,1,0:T(8,128)} %params.3), custom_call_target="tpu_custom_call" | custom-call | tf_op jit(solution)/shard_map/pallas_call | solution.py:432
  1.5 1.9 %collective-permute-start = (f32[64,128]{1,0:T(8,128)S(1)}, f32[64,128]{1,0:T(8,128)S(1)}, u32[]{:S(2)}, u32[]{:S(2)}) collective-permute-start(f32[64,128]{1,0:T(8,128)S(1)} %get-tuple-element.17), channel_id=1, source_target_pairs={{0,1},{1,2},{2,3},{3,4},{4,5},{5,6},{6,7},{7,8},{8,9},{9,10},{10,1... | collective-permute-start | bytes 98312 | tf_op jit(solution)/shard_map/ppermute | solution.py:476
  3.4 0.0 copy-start
  3.4 0.0 copy-start.1
  3.4 0.0 copy-start.2
  3.4 0.0 copy-start.3
  3.4 0.0 copy-start.4
  3.4 0.0 copy-start.5
  3.4 0.0 copy-start.6
  3.4 0.0 copy-start.7
  3.5 0.0 copy-start.8
  3.5 0.0 copy-start.9
  3.5 0.0 copy-start.11
  3.5 0.0 copy-start.12
  3.5 0.1 collective-permute-start.1
  3.6 1.7 %copy.17.kernels = f32[24,2,65,65]{3,2,1,0:T(8,128)S(1)} copy(f32[24,2,65,65]{3,1,2,0:T(2,128)} %param.18) | data formatting | bytes 1622400 | tf_op args[3]
  5.2 0.0 copy-done.10
  5.2 0.0 copy-done.13
  5.3 2.7 %shard_map.159 = (f32[24,72,128]{2,1,0:T(8,128)S(1)}, f32[24,72,128]{2,1,0:T(8,128)S(1)}, f32[2,72,128]{2,1,0:T(8,128)S(1)}) custom-call(f32[1,24]{1,0:T(1,128)S(1)} %bitcast.1, f32[24,2,65,65]{3,2,1,0:T(8,128)S(1)} %copy.17.kernels, bf16[72,72]{1,0:T(8,128)(2,1)S(1)} %copy-done.10), custom_call_target="tpu_custom_call" | custom-call | tf_op jit(solution)/shard_map/pallas_call | solution.py:449
  8.0 0.0 collective-permute-done.got_a
  8.0 0.0 collective-permute-done.1.got_b
  8.0 0.0 copy-done
  8.0 0.0 copy-done.1
  8.1 0.0 copy-done.2
  8.1 0.0 copy-done.3
  8.1 0.0 copy-done.4
  8.1 0.0 copy-done.5
  8.1 0.0 copy-done.6
  8.1 0.0 copy-done.7
  8.1 0.0 copy-done.8
  8.1 0.0 copy-done.9
  8.1 0.0 copy-done.11
  8.1 0.0 copy-done.12
  8.2 6.0 %shard_map.160 = (f32[2,64,128]{2,1,0:T(8,128)S(1)}, f32[64,128]{1,0:T(8,128)S(1)}, f32[64,128]{1,0:T(8,128)S(1)}) custom-call(s32[2]{0:T(128)S(1)} %copy-done.12, s32[2,2]{1,0:T(2,128)S(1)} %copy-done.11, f32[2,64,128]{2,1,0:T(8,128)S(1)} %copy-done.4, f32[64,128]{1,0:T(8,128)S(1)} %collective-permute-done.got_a, ...), custom_call_target="tpu_custom_call" | custom-call | tf_op jit(solution)/shard_map/pallas_call | solution.py:449
  14.2 2.6 %collective-permute-start.2 = (f32[64,128]{1,0:T(8,128)S(1)}, f32[64,128]{1,0:T(8,128)S(1)}, u32[]{:S(2)}, u32[]{:S(2)}) collective-permute-start(f32[64,128]{1,0:T(8,128)S(1)} %get-tuple-element.23), channel_id=1, source_target_pairs={{0,1},{1,2},{2,3},{3,4},{4,5},{5,6},{6,7},{7,8},{8,9},{9,10},{10,1... | collective-permute-start | bytes 98312 | tf_op jit(solution)/shard_map/ppermute | solution.py:476
  16.8 0.0 collective-permute-start.3
  16.8 1.0 %collective-permute-done.2.got_a = f32[64,128]{1,0:T(8,128)S(1)} collective-permute-done((f32[64,128]{1,0:T(8,128)S(1)}, f32[64,128]{1,0:T(8,128)S(1)}, u32[]{:S(2)}, u32[]{:S(2)}) %collective-permute-start.2) | collective-permute-done | bytes 32800 | tf_op jit(solution)/shard_map/ppermute | solution.py:476
  17.8 3.2 %collective-permute-done.3.got_b = f32[64,128]{1,0:T(8,128)S(1)} collective-permute-done((f32[64,128]{1,0:T(8,128)S(1)}, f32[64,128]{1,0:T(8,128)S(1)}, u32[]{:S(2)}, u32[]{:S(2)}) %collective-permute-start.3) | collective-permute-done | bytes 32800 | tf_op jit(solution)/shard_map/ppermute | solution.py:476
  21.0 0.6 %shard_map.161 = (f32[2,64,128]{2,1,0:T(8,128)S(1)}, f32[64,128]{1,0:T(8,128)S(1)}, f32[64,128]{1,0:T(8,128)S(1)}) custom-call(s32[2]{0:T(128)S(1)} %copy-done.12, s32[2,2]{1,0:T(2,128)S(1)} %copy-done.11, f32[2,64,128]{2,1,0:T(8,128)S(1)} %get-tuple-element.22.part, f32[2,64,128]{2,1,0:T(8,128)S(1)} %copy-done.4, ...), custom_call_target="tpu_custom_call" | custom-call | tf_op jit(solution)/shard_map/pallas_call | solution.py:449
  21.6 0.1 collective-permute-start.4
  21.7 0.5 %collective-permute-start.5 = (f32[64,128]{1,0:T(8,128)S(1)}, f32[64,128]{1,0:T(8,128)S(1)}, u32[]{:S(2)}, u32[]{:S(2)}) collective-permute-start(f32[64,128]{1,0:T(8,128)S(1)} %get-tuple-element.27), channel_id=1, source_target_pairs={{0,16},{1,0},{2,1},{3,2},{4,3},{5,4},{6,5},{7,6},{8,7},{9,8},{10,9... | collective-permute-start | bytes 98312 | tf_op jit(solution)/shard_map/ppermute | solution.py:476
  22.2 0.7 %collective-permute-done.4.got_a = f32[64,128]{1,0:T(8,128)S(1)} collective-permute-done((f32[64,128]{1,0:T(8,128)S(1)}, f32[64,128]{1,0:T(8,128)S(1)}, u32[]{:S(2)}, u32[]{:S(2)}) %collective-permute-start.4) | collective-permute-done | bytes 32800 | tf_op jit(solution)/shard_map/ppermute | solution.py:476
  22.9 3.1 %collective-permute-done.5.got_b = f32[64,128]{1,0:T(8,128)S(1)} collective-permute-done((f32[64,128]{1,0:T(8,128)S(1)}, f32[64,128]{1,0:T(8,128)S(1)}, u32[]{:S(2)}, u32[]{:S(2)}) %collective-permute-start.5) | collective-permute-done | bytes 32800 | tf_op jit(solution)/shard_map/ppermute | solution.py:476
  26.0 6.0 %shard_map.162 = (f32[2,64,128]{2,1,0:T(8,128)S(1)}, f32[2,64,128]{2,1,0:T(8,128)}, f32[64,128]{1,0:T(8,128)S(1)}, f32[64,128]{1,0:T(8,128)S(1)}) custom-call(s32[2]{0:T(128)S(1)} %copy-done.12, s32[2,2]{1,0:T(2,128)S(1)} %copy-done.11, f32[2,64,128]{2,1,0:T(8,128)S(1)} %get-tuple-element.25.mp.params, f32[64,128]{1,0:T(8,128)S(1)} %collective-permute-done.4.got_a, ...), custom_call_target="tpu_custom_call" | custom-call | tf_op jit(solution)/shard_map/pallas_call | solution.py:449
  32.0 0.1 collective-permute-start.6
  32.1 0.5 %collective-permute-start.7 = (f32[64,128]{1,0:T(8,128)S(1)}, f32[64,128]{1,0:T(8,128)S(1)}, u32[]{:S(2)}, u32[]{:S(2)}) collective-permute-start(f32[64,128]{1,0:T(8,128)S(1)} %get-tuple-element.30), channel_id=1, source_target_pairs={{0,16},{1,0},{2,1},{3,2},{4,3},{5,4},{6,5},{7,6},{8,7},{9,8},{10,9... | collective-permute-start | bytes 98312 | tf_op jit(solution)/shard_map/ppermute | solution.py:476
  32.6 0.7 %collective-permute-done.6.got_a = f32[64,128]{1,0:T(8,128)S(1)} collective-permute-done((f32[64,128]{1,0:T(8,128)S(1)}, f32[64,128]{1,0:T(8,128)S(1)}, u32[]{:S(2)}, u32[]{:S(2)}) %collective-permute-start.6) | collective-permute-done | bytes 32800 | tf_op jit(solution)/shard_map/ppermute | solution.py:476
  33.3 3.1 %collective-permute-done.7.got_b = f32[64,128]{1,0:T(8,128)S(1)} collective-permute-done((f32[64,128]{1,0:T(8,128)S(1)}, f32[64,128]{1,0:T(8,128)S(1)}, u32[]{:S(2)}, u32[]{:S(2)}) %collective-permute-start.7) | collective-permute-done | bytes 32800 | tf_op jit(solution)/shard_map/ppermute | solution.py:476
  36.4 1.2 %shard_map.163 = f32[2,64,128]{2,1,0:T(8,128)} custom-call(s32[2]{0:T(128)S(1)} %copy-done.12, s32[2,2]{1,0:T(2,128)S(1)} %copy-done.11, f32[2,64,128]{2,1,0:T(8,128)S(1)} %get-tuple-element.28.part, f32[2,64,128]{2,1,0:T(8,128)S(1)} %get-tuple-element.25.mp.params, f32[64,128]{1,0:T(8,128)S(1)} %collective-permute-done.6.got_a, ...), custom_call_target="tpu_custom_call" | custom-call | tf_op jit(solution)/shard_map/pallas_call | solution.py:449
Async XLA Ops:
  0.6 4.6 %copy-start.10 = (bf16[72,72]{1,0:T(8,128)(2,1)S(1)}, bf16[72,72]{1,0:T(8,128)(2,1)}, u32[]{:S(2)}) copy-start(bf16[72,72]{1,0:T(8,128)(2,1)} %constant.23.clone.order) | copy-start | bytes 31108
  0.6 4.6 %copy-start.13 = (f32[24]{0:T(128)S(1)}, f32[24]{0:T(128)}, u32[]{:S(2)}) copy-start(f32[24]{0:T(128)} %param.19) | copy-start | bytes 292
  1.5 6.5 %collective-permute-start = (f32[64,128]{1,0:T(8,128)S(1)}, f32[64,128]{1,0:T(8,128)S(1)}, u32[]{:S(2)}, u32[]{:S(2)}) collective-permute-start(f32[64,128]{1,0:T(8,128)S(1)} %get-tuple-element.17), channel_id=1, source_target_pairs={{0,1},{1,2},{2,3},{3,4},{4,5},{5,6},{6,7},{7,8},{8,9},{9,10},{10,1... | collective-permute-start | bytes 98312 | tf_op jit(solution)/shard_map/ppermute | solution.py:476
  3.4 4.6 %copy-start = (bf16[768,256]{1,0:T(8,128)(2,1)S(1)}, bf16[768,256]{1,0:T(8,128)(2,1)}, u32[]{:S(2)}) copy-start(bf16[768,256]{1,0:T(8,128)(2,1)} %constant.20.clone.rest_4_) | copy-start | bytes 1179652
  3.4 4.6 %copy-start.1 = (bf16[3,256,256]{2,1,0:T(8,128)(2,1)S(1)}, bf16[3,256,256]{2,1,0:T(8,128)(2,1)}, u32[]{:S(2)}) copy-start(bf16[3,256,256]{2,1,0:T(8,128)(2,1)} %constant.22.clone.rest_6_) | copy-start | bytes 1179652
  3.4 4.7 %copy-start.2 = (bf16[384,384]{1,0:T(8,128)(2,1)S(1)}, bf16[384,384]{1,0:T(8,128)(2,1)}, u32[]{:S(2)}) copy-start(bf16[384,384]{1,0:T(8,128)(2,1)} %constant.21.clone.rest_5_) | copy-start | bytes 884740
  3.4 4.7 %copy-start.3 = (bf16[512,256]{1,0:T(8,128)(2,1)S(1)}, bf16[512,256]{1,0:T(8,128)(2,1)}, u32[]{:S(2)}) copy-start(bf16[512,256]{1,0:T(8,128)(2,1)} %constant.18.clone.rest_2_) | copy-start | bytes 786436
  3.4 4.7 %copy-start.4 = (f32[2,64,128]{2,1,0:T(8,128)S(1)}, f32[2,64,128]{2,1,0:T(8,128)}, u32[]{:S(2)}) copy-start(f32[2,64,128]{2,1,0:T(8,128)} %params.3) | copy-start | bytes 196612
  3.4 4.7 %copy-start.5 = (bf16[32,16,128]{2,1,0:T(8,128)(2,1)S(1)}, bf16[32,16,128]{2,1,0:T(8,128)(2,1)}, u32[]{:S(2)}) copy-start(bf16[32,16,128]{2,1,0:T(8,128)(2,1)} %constant.19.clone.rest_3_) | copy-start | bytes 393220
  3.4 4.7 %copy-start.6 = (f32[2,64,128]{2,1,0:T(8,128)S(1)}, f32[2,64,128]{2,1,0:T(8,128)}, u32[]{:S(2)}) copy-start(f32[2,64,128]{2,1,0:T(8,128)} %target.3) | copy-start | bytes 196612
  3.4 4.7 %copy-start.7 = (f32[2,64,128]{2,1,0:T(8,128)S(1)}, f32[2,64,128]{2,1,0:T(8,128)}, u32[]{:S(2)}) copy-start(f32[2,64,128]{2,1,0:T(8,128)} %weight.3) | copy-start | bytes 196612
  3.5 4.7 %copy-start.8 = (bf16[80,192]{1,0:T(8,128)(2,1)S(1)}, bf16[80,192]{1,0:T(8,128)(2,1)}, u32[]{:S(2)}) copy-start(bf16[80,192]{1,0:T(8,128)(2,1)} %constant.17.clone.rest_1_) | copy-start | bytes 92164
  3.5 4.7 %copy-start.9 = (bf16[64,240]{1,0:T(8,128)(2,1)S(1)}, bf16[64,240]{1,0:T(8,128)(2,1)}, u32[]{:S(2)}) copy-start(bf16[64,240]{1,0:T(8,128)(2,1)} %constant.16.clone.rest_0_) | copy-start | bytes 92164
  3.5 4.7 %copy-start.11 = (s32[2,2]{1,0:T(2,128)S(1)}, s32[2,2]{1,0:T(2,128)}, u32[]{:S(2)}) copy-start(s32[2,2]{1,0:T(2,128)} %links.7) | copy-start | bytes 52
  3.5 4.7 %copy-start.12 = (s32[2]{0:T(128)S(1)}, s32[2]{0:T(128)}, u32[]{:S(2)}) copy-start(s32[2]{0:T(128)} %ids.9) | copy-start | bytes 28
  3.5 4.5 %collective-permute-start.1 = (f32[64,128]{1,0:T(8,128)S(1)}, f32[64,128]{1,0:T(8,128)S(1)}, u32[]{:S(2)}, u32[]{:S(2)}) collective-permute-start(f32[64,128]{1,0:T(8,128)S(1)} %get-tuple-element.18), channel_id=1, source_target_pairs={{0,16},{1,0},{2,1},{3,2},{4,3},{5,4},{6,5},{7,6},{8,7},{9,8},{10,9... | collective-permute-start | bytes 98312 | tf_op jit(solution)/shard_map/ppermute | solution.py:476
  14.2 3.6 %collective-permute-start.2 = (f32[64,128]{1,0:T(8,128)S(1)}, f32[64,128]{1,0:T(8,128)S(1)}, u32[]{:S(2)}, u32[]{:S(2)}) collective-permute-start(f32[64,128]{1,0:T(8,128)S(1)} %get-tuple-element.23), channel_id=1, source_target_pairs={{0,1},{1,2},{2,3},{3,4},{4,5},{5,6},{6,7},{7,8},{8,9},{9,10},{10,1... | collective-permute-start | bytes 98312 | tf_op jit(solution)/shard_map/ppermute | solution.py:476
  16.8 4.2 %collective-permute-start.3 = (f32[64,128]{1,0:T(8,128)S(1)}, f32[64,128]{1,0:T(8,128)S(1)}, u32[]{:S(2)}, u32[]{:S(2)}) collective-permute-start(f32[64,128]{1,0:T(8,128)S(1)} %get-tuple-element.24), channel_id=1, source_target_pairs={{0,16},{1,0},{2,1},{3,2},{4,3},{5,4},{6,5},{7,6},{8,7},{9,8},{10,9... | collective-permute-start | bytes 98312 | tf_op jit(solution)/shard_map/ppermute | solution.py:476
  21.6 1.3 %collective-permute-start.4 = (f32[64,128]{1,0:T(8,128)S(1)}, f32[64,128]{1,0:T(8,128)S(1)}, u32[]{:S(2)}, u32[]{:S(2)}) collective-permute-start(f32[64,128]{1,0:T(8,128)S(1)} %get-tuple-element.26), channel_id=1, source_target_pairs={{0,1},{1,2},{2,3},{3,4},{4,5},{5,6},{6,7},{7,8},{8,9},{9,10},{10,1... | collective-permute-start | bytes 98312 | tf_op jit(solution)/shard_map/ppermute | solution.py:476
  21.7 4.3 %collective-permute-start.5 = (f32[64,128]{1,0:T(8,128)S(1)}, f32[64,128]{1,0:T(8,128)S(1)}, u32[]{:S(2)}, u32[]{:S(2)}) collective-permute-start(f32[64,128]{1,0:T(8,128)S(1)} %get-tuple-element.27), channel_id=1, source_target_pairs={{0,16},{1,0},{2,1},{3,2},{4,3},{5,4},{6,5},{7,6},{8,7},{9,8},{10,9... | collective-permute-start | bytes 98312 | tf_op jit(solution)/shard_map/ppermute | solution.py:476
  32.0 1.3 %collective-permute-start.6 = (f32[64,128]{1,0:T(8,128)S(1)}, f32[64,128]{1,0:T(8,128)S(1)}, u32[]{:S(2)}, u32[]{:S(2)}) collective-permute-start(f32[64,128]{1,0:T(8,128)S(1)} %get-tuple-element.29), channel_id=1, source_target_pairs={{0,1},{1,2},{2,3},{3,4},{4,5},{5,6},{6,7},{7,8},{8,9},{9,10},{10,1... | collective-permute-start | bytes 98312 | tf_op jit(solution)/shard_map/ppermute | solution.py:476
  32.1 4.3 %collective-permute-start.7 = (f32[64,128]{1,0:T(8,128)S(1)}, f32[64,128]{1,0:T(8,128)S(1)}, u32[]{:S(2)}, u32[]{:S(2)}) collective-permute-start(f32[64,128]{1,0:T(8,128)S(1)} %get-tuple-element.30), channel_id=1, source_target_pairs={{0,16},{1,0},{2,1},{3,2},{4,3},{5,4},{6,5},{7,6},{8,7},{9,8},{10,9... | collective-permute-start | bytes 98312 | tf_op jit(solution)/shard_map/ppermute | solution.py:476
where the time goes:
time: 37.8 us; the launch traced here: 37.6 us
  Pallas kernels  17.5 us (46%)
  waiting for transfers between devices  11.8 us (31%)
  starting transfers between devices  5.63 us (15%)
  local copies, waits for them, and re-layouts  1.73 us (5%)
  between operations  0.91 us (2%)
    pallas_call x5, Pallas kernels, call(): pl.pallas_call(body, in_specs=[smem] * scalars + [vmem] * (len(ins) - sca...  16.6 us
    ppermute x8, waiting for transfers between devices, exchange(): return (lax.ppermute(a, axes, ring_a), lax.ppermute(b, axes, ring_b))  11.8 us
    ppermute x8, starting transfers between devices, exchange(): return (lax.ppermute(a, axes, ring_a), lax.ppermute(b, axes, ring_b))  5.63 us
    unnamed x29, local copies, waits for them, and re-layouts  1.73 us
    pallas_call x1, Pallas kernels, choose(): pl.pallas_call(kernel_choose, in_specs=[anywhere] * 2, out_specs=[pl.Bloc...  0.88 us
  transfers between devices with their start and end apart: 8, of which 6 were waited for; matrix products, arithmetic and copies ran while one was open for 4% of the time, Pallas kernels for 7%

commit v1 on v0

--- a/solution.py
+++ b/solution.py
@@ -14,6 +14,7 @@
 THRESHOLD = 0.9
 STEP_SCALE = 0.04
 GROUP = 8
+FIRST = 6
 MID = 16
 F32 = jnp.float32
 BF16 = jnp.bfloat16
@@ -192,10 +193,25 @@
     return jnp.sum(v, axis=1, keepdims=True)
 
 
-def core(tb, dom, target, weight, ha_ref, hb_ref, h0, t, e_ref, keep=None):
+class Spectra:
+    def __init__(self, refs):
+        self.runs = (refs[:2], refs[3:5])
+        self.zeros = (refs[2], refs[5])
+        self.count = sum(run[0].shape[0] for run in self.runs)
+
+    def __getitem__(self, k):
+        first = self.runs[0][0].shape[0]
+        run, k = (self.runs[0], k) if k < first else (self.runs[1], k - first)
+        return run[0][k], run[1][k]
+
+    def at_zero(self):
+        return [self.zeros[0][i] + self.zeros[1][i] for i in range(2)]
+
+
+def core(tb, dom, target, weight, spectra, t, e_ref, keep=None):
     half, nf = tb.half, tb.nf
     slots, rows, cols = target.shape
-    kcount = ha_ref.shape[0]
+    kcount = spectra.count
     wl = 2 * nf
     zb = wl // (2 * slots)
     ty, tyt = t["ty"], t["tyt"]
@@ -210,7 +226,7 @@
     for s in range(slots):
         g0w = jnp.where(block == 2 * s, g0[s * rows : (s + 1) * rows], g0w)
     u0 = phases(spread(half, dot(tyt[...], rows3(g0w)), zb), zb)
-    a0, b0 = h0[0], h0[1]
+    a0, b0 = spectra.at_zero()
     r0 = dot(ty[...], rows3(drive(half, a0, b0, u0)))
     r0h, r0l = split(r0)
     r0l = pltpu.roll(r0l.astype(F32), wl // 2, 1)
@@ -226,7 +242,7 @@
     def row_stage(s, ks):
         out, extra = [], []
         for pair in in_pairs(ks):
-            w = jnp.concatenate([drive(half, ha_ref[k], hb_ref[k], us[s]) for k in pair], 1)
+            w = jnp.concatenate([drive(half, *spectra[k], us[s]) for k in pair], 1)
             r = dot(ty[...], rows3(w))
             for n, k in enumerate(pair):
                 out.append(r[:, n * wl : (n + 1) * wl])
@@ -256,7 +272,7 @@
             o = dot(tyt[...], rows3(jnp.concatenate([v[:, :wl] for v in parts], 1)))
             for n, k in enumerate(pair):
                 c0 = jnp.where(inner == k, parts[n][:, wl:], c0)
-                q = gather(half, q, ha_ref[k], hb_ref[k], o[:, n * wl : (n + 1) * wl], nf)
+                q = gather(half, q, *spectra[k], o[:, n * wl : (n + 1) * wl], nf)
         return c0, q
 
     def finish(s, c0, q):
@@ -295,10 +311,8 @@
     return grads
 
 
-def read_flags(ids, links):
-    both = ids[1] >= 0
-    even = lax.rem(lax.axis_index("grp"), 2) == 0
-    return both, links[0, 0] == 1, links[1, 0] == 1, links[0, 1] == 1, links[1, 1] == 1, even
+def read_flags(flags, shape):
+    return tuple(jnp.broadcast_to(flags[i : i + 1], shape) > 0.5 for i in range(6))
 
 
 def in_order(even, first, second):
@@ -335,19 +349,20 @@
     return params - step * gradient * (1.0 - transmit * transmit)
 
 
-def kernel_first(tb, names, ids, links, mp, got_a, got_b, target, weight, ha, hb, h0, *rest):
+def kernel_first(tb, names, marks, mp, got_a, got_b, target, weight, *rest):
+    spectra, rest = Spectra(rest[:6]), rest[6:]
     t = dict(zip(names, rest))
     part, send_a, send_b, e_ref = rest[len(names) :]
-    flags = read_flags(ids, links)
+    flags = read_flags(marks, got_a.shape)
     prev, nxt = in_order(flags[5], got_a[...], got_b[...])
     tile = [jnp.tanh(v) for v in (prev, mp[0], mp[1], nxt)]
-    dg = core(tb, domain_of(flags, *tile), target, weight, ha, hb, h0, t, e_ref)
+    dg = core(tb, domain_of(flags, *tile), target, weight, spectra, t, e_ref)
     part[0], part[1], to_next, to_prev = thirds(flags, dg)
     send_a[...], send_b[...] = in_order(flags[5], to_next, to_prev)
 
 
-def kernel_update(step, ids, links, part, params, got_a, got_b, out, send_a, send_b):
-    flags = read_flags(ids, links)
+def kernel_update(step, marks, part, params, got_a, got_b, out, send_a, send_b):
+    flags = read_flags(marks, got_a.shape)
     prev, nxt = in_order(flags[5], got_a[...], got_b[...])
     g0, g1 = own_gradient(flags, part[0], part[1], prev, nxt)
     new0 = stepped(step, params[0], g0)
@@ -356,10 +371,11 @@
     send_a[...], send_b[...] = in_order(flags[5], jnp.where(flags[0], new1, new0), new0)
 
 
-def kernel_second(tb, names, ids, links, mp, got_a, got_b, target, weight, ha, hb, h0, *rest):
+def kernel_second(tb, names, marks, mp, got_a, got_b, target, weight, *rest):
+    spectra, rest = Spectra(rest[:6]), rest[6:]
     t = dict(zip(names, rest))
     part, resist_out, send_a, send_b, e_ref, resist_v, sems = rest[len(names) :]
-    flags = read_flags(ids, links)
+    flags = read_flags(marks, got_a.shape)
     prev, nxt = in_order(flags[5], got_a[...], got_b[...])
     tile = [jnp.tanh(v) for v in (prev, mp[0], mp[1], nxt)]
     moves = []
@@ -369,22 +385,22 @@
         moves.append(pltpu.make_async_copy(resist_v.at[s], resist_out.at[s], sems.at[s]))
         moves[-1].start()
 
-    dg = core(tb, domain_of(flags, *tile), target, weight, ha, hb, h0, t, e_ref, keep)
+    dg = core(tb, domain_of(flags, *tile), target, weight, spectra, t, e_ref, keep)
     part[0], part[1], to_next, to_prev = thirds(flags, dg)
     send_a[...], send_b[...] = in_order(flags[5], to_next, to_prev)
     for move in moves:
         move.wait()
 
 
-def kernel_last(step, ids, links, part, params, got_a, got_b, out):
-    flags = read_flags(ids, links)
+def kernel_last(step, marks, part, params, got_a, got_b, out):
+    flags = read_flags(marks, got_a.shape)
     prev, nxt = in_order(flags[5], got_a[...], got_b[...])
     g0, g1 = own_gradient(flags, part[0], part[1], prev, nxt)
     out[0] = stepped(step, params[0], g0)
     out[1] = jnp.where(flags[0], stepped(step, params[1], g1), params[1])
 
 
-def kernel_arrange(tb, slots, weights, kernels, order, out_a, out_b, out_0, padded):
+def kernel_arrange(tb, slots, span, weights, kernels, order, carried, out_a, out_b, out_0, passed, padded):
     half, nf = tb.half, tb.nf
     frows, wl = 2 * half + 8, 2 * nf
     bands = kernels.shape[3]
@@ -394,61 +410,72 @@
     roots = jnp.sqrt(weights[...])
     zeros = [jnp.zeros((frows, wl), F32) for _ in range(2)]
     padded[...] = jnp.zeros(padded.shape, F32)
-    for k in range(kernels.shape[0]):
+    for n, k in enumerate(span):
         root = jnp.broadcast_to(roots[:, k : k + 1], (1, bands))
         for part in range(2):
-            padded[k, part, :bands, :bands] = kernels[k, part] * root
-    for k in range(kernels.shape[0]):
+            padded[n, part, :bands, :bands] = kernels[k, part] * root
+    for n, k in enumerate(span):
         for part in range(2):
-            high, low = split(padded[k, part])
+            high, low = split(padded[n, part])
             v = dot(order[...], high) + dot(order[...], low)
             zero = jnp.broadcast_to(v[:, half : half + 1], (frows, wl))
             zeros[part] = jnp.where(inner == k, zero, zeros[part])
             v = jnp.where(lane < half, v, pltpu.roll(v, wl - 1, 1))
             v = jnp.where(lane < nf, v, pltpu.roll(v, nf, 1))
             if part == 0:
-                out_a[k] = v
+                out_a[n] = v
             else:
-                out_b[k] = -conj(v, nf)
+                out_b[n] = -conj(v, nf)
     out_0[0] = zeros[0]
     out_0[1] = -conj(zeros[1], zb)
-
-
-def kernel_choose(ids, params, send_a, send_b, ids_s, params_v, sems):
-    move_ids = pltpu.make_async_copy(ids, ids_s, sems.at[0])
-    move = pltpu.make_async_copy(params, params_v, sems.at[1])
-    move_ids.start()
-    move.start()
-    move_ids.wait()
-    move.wait()
+    passed[...] = carried[...]
+
+
+def kernel_choose(ids, links, params, marks, send_a, send_b, ids_s, links_s, params_v, sems):
+    moves = [
+        pltpu.make_async_copy(source, target, sems.at[i])
+        for i, (source, target) in enumerate(((ids, ids_s), (links, links_s), (params, params_v)))
+    ]
+    for move in moves:
+        move.start()
+    for move in moves:
+        move.wait()
+    both = ids_s[1] >= 0
     even = lax.rem(lax.axis_index("grp"), 2) == 0
-    last = jnp.where(ids_s[1] >= 0, params_v[1], params_v[0])
+    last = jnp.where(both, params_v[1], params_v[0])
     send_a[...], send_b[...] = in_order(even, last, params_v[0])
-
-
-def choose(tile_ids, mask_params):
+    flags = [both] + [links_s[s, side] == 1 for side in range(2) for s in range(2)] + [even]
+    row = lax.broadcasted_iota(jnp.int32, marks.shape, 0)
+    out = jnp.zeros(marks.shape, F32)
+    for i, flag in enumerate(flags):
+        out = jnp.where(row == i, jnp.where(flag, 1.0, 0.0), out)
+    marks[...] = out
+
+
+def choose(*ins):
+    tile_ids, tile_links, mask_params = ins
     tile = mask_params.shape[1:]
-    anywhere = pl.BlockSpec(memory_space=pltpu.HBM)
+    far = pl.BlockSpec(memory_space=pltpu.HBM)
     return pl.pallas_call(
         kernel_choose,
-        in_specs=[anywhere] * 2,
-        out_specs=[pl.BlockSpec(memory_space=pltpu.VMEM)] * 2,
-        out_shape=[jax.ShapeDtypeStruct(tile, F32)] * 2,
+        in_specs=[far] * 3,
+        out_specs=[pl.BlockSpec(memory_space=pltpu.VMEM)] * 3,
+        out_shape=[jax.ShapeDtypeStruct(s, F32) for s in ((8, tile[1]), tile, tile)],
         scratch_shapes=[
             pltpu.SMEM(tile_ids.shape, jnp.int32),
+            pltpu.SMEM(tile_links.shape, jnp.int32),
             pltpu.VMEM(mask_params.shape, F32),
-            pltpu.SemaphoreType.DMA((2,)),
+            pltpu.SemaphoreType.DMA((3,)),
         ],
         compiler_params=pltpu.CompilerParams(vmem_limit_bytes=4 << 20),
-    )(*(pltpu.with_memory_space_constraint(v, pltpu.HBM) for v in (tile_ids, mask_params)))
-
-
-def call(body, ins, outs, scratch=(), scalars=2, limit=32 << 20, moved=()):
-    smem = pl.BlockSpec(memory_space=pltpu.SMEM)
+    )(*(pltpu.with_memory_space_constraint(v, pltpu.HBM) for v in ins))
+
+
+def call(body, ins, outs, scratch=(), limit=32 << 20, moved=()):
     vmem = pl.BlockSpec(memory_space=pltpu.VMEM)
     return pl.pallas_call(
         body,
-        in_specs=[smem] * scalars + [vmem] * (len(ins) - scalars),
+        in_specs=[vmem] * len(ins),
         out_specs=[
             pl.BlockSpec(memory_space=pltpu.HBM) if i in moved else vmem for i in range(len(outs))
         ],
@@ -475,38 +502,44 @@
     def exchange(a, b):
         return lax.ppermute(a, axes, ring_a), lax.ppermute(b, axes, ring_b)
 
-    got = exchange(*choose(tile_ids, mask_params))
     frows = 2 * tb.half + 8
-    arranged = call(
-        functools.partial(kernel_arrange, tb, slots),
-        [kernel_weight[None], kernels, jnp.asarray(tb.order)],
-        [(kcount, frows, 2 * tb.nf)] * 2 + [(2, frows, 2 * tb.nf)],
-        [pltpu.VMEM((kcount, 2, frows, 2 * tb.nf), F32)],
-        scalars=0,
-    )
+    whole, tile = mask_params.shape, (rows, cols)
+
+    def arrange(span, carried):
+        return call(
+            functools.partial(kernel_arrange, tb, slots, span),
+            [kernel_weight[None], kernels, jnp.asarray(tb.order), carried],
+            [(len(span), frows, 2 * tb.nf)] * 2 + [(2, frows, 2 * tb.nf), carried.shape],
+            [pltpu.VMEM((len(span), 2, frows, 2 * tb.nf), F32)],
+        )
+
+    marks, sa, sb = choose(tile_ids, tile_links, mask_params)
+    *early, sb = arrange(range(FIRST), sb)
+    *late, marks = arrange(range(FIRST, kcount), marks)
+    got = exchange(sa, sb)
+    arranged = early + late
     field = pltpu.VMEM((slots, kcount, rows, 2 * cols), F32)
-    whole, tile = mask_params.shape, (rows, cols)
     part, sa, sb = call(
         functools.partial(kernel_first, tb, names),
-        [tile_ids, tile_links, mask_params, *got, target, weight, *arranged, *tables],
+        [marks, mask_params, *got, target, weight, *arranged, *tables],
         [whole, tile, tile],
         [field],
     )
     params, sa, sb = call(
         functools.partial(kernel_update, step),
-        [tile_ids, tile_links, part, mask_params, *exchange(sa, sb)],
+        [marks, part, mask_params, *exchange(sa, sb)],
         [whole, tile, tile],
     )
     part, resist, sa, sb = call(
         functools.partial(kernel_second, tb, names),
-        [tile_ids, tile_links, params, *exchange(sa, sb), target, weight, *arranged, *tables],
+        [marks, params, *exchange(sa, sb), target, weight, *arranged, *tables],
         [whole, whole, tile, tile],
         [field, pltpu.VMEM(whole, F32), pltpu.SemaphoreType.DMA((slots,))],
         moved=(1,),
     )
     (out,) = call(
         functools.partial(kernel_last, step),
-        [tile_ids, tile_links, part, params, *exchange(sa, sb)],
+        [marks, part, params, *exchange(sa, sb)],
         [whole],
     )
     return (out, resist)

time: 37.8 us -> 35.2 us (0.931)
  Pallas kernels: 17.5 us -> 14.9 us
  waiting for transfers between devices: 11.8 us -> 14 us
  starting transfers between devices: 5.63 us -> 3.61 us
    pallas_call x6 -> x7, Pallas kernels: 17.5 us -> 14.9 us  [the longest x6 14 us: call(): pl.pallas_call(body, in_specs=[vmem] * len(ins), out_specs=[pl.BlockSpec(...]
    ppermute x8, waiting for transfers between devices: 11.8 us -> 14 us  [exchange(): return (lax.ppermute(a, axes, ring_a), lax.ppermute(b, axes, ring_b))]
    ppermute x8, starting transfers between devices: 5.63 us -> 3.61 us  [exchange(): return (lax.ppermute(a, axes, ring_a), lax.ppermute(b, axes, ring_b))]
    unnamed x29 -> x25, local copies, waits for them, and re-layouts: 1.73 us -> 1.64 us
  transfers between devices with their start and end apart: 8 -> 8, of which waited for: 6 -> 7; matrix products, arithmetic and copies ran while one was open for 4% -> 4% of each run, Pallas kernels for 7% -> 7%
where the time goes in v1:
time: 35.2 us; the launch traced here: 35 us
  Pallas kernels  14.9 us (42%)
  waiting for transfers between devices  14 us (40%)
  starting transfers between devices  3.61 us (10%)
  local copies, waits for them, and re-layouts  1.64 us (5%)
  between operations  0.88 us (2%)
    pallas_call x6, Pallas kernels, call(): pl.pallas_call(body, in_specs=[vmem] * len(ins), out_specs=[pl.BlockSpec(...  14 us
    ppermute x8, waiting for transfers between devices, exchange(): return (lax.ppermute(a, axes, ring_a), lax.ppermute(b, axes, ring_b))  14 us
    ppermute x8, starting transfers between devices, exchange(): return (lax.ppermute(a, axes, ring_a), lax.ppermute(b, axes, ring_b))  3.61 us
    unnamed x25, local copies, waits for them, and re-layouts  1.64 us
    pallas_call x1, Pallas kernels, choose(): pl.pallas_call(kernel_choose, in_specs=[far] * 3, out_specs=[pl.BlockSpec...  0.89 us
  transfers between devices with their start and end apart: 8, of which 7 were waited for; matrix products, arithmetic and copies ran while one was open for 4% of the time, Pallas kernels for 7%

profile of v1, /device:TPU:21, one launch (start us, length us, event | category | flops | bytes accessed | tf_op | source)
XLA Modules:
  0.0 35.0 jit_solution(7190856122266043760)
XLA Ops:
  0.6 0.0 copy-start.10
  0.6 0.0 copy-start.11
  0.7 0.9 %shard_map.158 = (f32[8,128]{1,0:T(8,128)S(1)}, f32[64,128]{1,0:T(8,128)S(1)}, f32[64,128]{1,0:T(8,128)S(1)}) custom-call(s32[2]{0:T(128)} %ids.1, s32[2,2]{1,0:T(2,128)} %links.1, f32[2,64,128]{2,1,0:T(8,128)} %params.3), custom_call_target="tpu_custom_call" | custom-call | tf_op jit(solution)/shard_map/pallas_call | solution.py:459
  1.6 1.9 %collective-permute-start = (f32[64,128]{1,0:T(8,128)S(1)}, f32[64,128]{1,0:T(8,128)S(1)}, u32[]{:S(2)}, u32[]{:S(2)}) collective-permute-start(f32[64,128]{1,0:T(8,128)S(1)} %get-tuple-element.25), channel_id=1, source_target_pairs={{0,1},{1,2},{2,3},{3,4},{4,5},{5,6},{6,7},{7,8},{8,9},{9,10},{10,1... | collective-permute-start | bytes 98312 | tf_op jit(solution)/shard_map/ppermute | solution.py:503
  3.4 1.6 %copy.17.kernels = f32[24,2,65,65]{3,2,1,0:T(8,128)S(1)} copy(f32[24,2,65,65]{3,1,2,0:T(2,128)} %param.18) | data formatting | bytes 1622400 | tf_op args[3]
  5.0 0.0 copy-done.10
  5.0 0.0 copy-done.11
  5.0 0.0 copy-start
  5.0 0.0 copy-start.1
  5.0 0.0 copy-start.2
  5.0 0.0 copy-start.3
  5.0 0.0 copy-start.4
  5.1 0.0 copy-start.5
  5.1 0.0 copy-start.6
  5.1 0.0 copy-start.7
  5.1 0.0 copy-start.8
  5.1 0.0 copy-start.9
  5.1 0.7 %shard_map.160 = (f32[6,72,128]{2,1,0:T(8,128)S(1)}, f32[6,72,128]{2,1,0:T(8,128)S(1)}, f32[2,72,128]{2,1,0:T(8,128)S(1)}, f32[64,128]{1,0:T(8,128)S(1)}) custom-call(f32[1,24]{1,0:T(1,128)S(1)} %bitcast.1, f32[24,2,65,65]{3,2,1,0:T(8,128)S(1)} %copy.17.kernels, bf16[72,72]{1,0:T(8,128)(2,1)S(1)} %copy-done.10, f32[64,128]{1,0:T(8,128)S(1)} %get-tuple-element.26.carried), custom_call_target="tpu_custom_call" | custom-call | tf_op jit(solution)/shard_map/pallas_call | solution.py:476
  5.8 0.1 collective-permute-start.1
  5.9 1.6 %shard_map.159 = (f32[18,72,128]{2,1,0:T(8,128)S(1)}, f32[18,72,128]{2,1,0:T(8,128)S(1)}, f32[2,72,128]{2,1,0:T(8,128)S(1)}, f32[8,128]{1,0:T(8,128)S(1)}) custom-call(f32[1,24]{1,0:T(1,128)S(1)} %bitcast.2, f32[24,2,65,65]{3,2,1,0:T(8,128)S(1)} %copy.17.kernels, bf16[72,72]{1,0:T(8,128)(2,1)S(1)} %copy-done.10, f32[8,128]{1,0:T(8,128)S(1)} %get-tuple-element.23.carried), custom_call_target="tpu_custom_call" | custom-call | tf_op jit(solution)/shard_map/pallas_call | solution.py:476
  7.5 0.0 collective-permute-done.got_a
  7.5 2.6 %collective-permute-done.1.got_b = f32[64,128]{1,0:T(8,128)S(1)} collective-permute-done((f32[64,128]{1,0:T(8,128)S(1)}, f32[64,128]{1,0:T(8,128)S(1)}, u32[]{:S(2)}, u32[]{:S(2)}) %collective-permute-start.1) | collective-permute-done | bytes 32800 | tf_op jit(solution)/shard_map/ppermute | solution.py:503
  10.1 0.0 copy-done
  10.1 0.0 copy-done.1
  10.1 0.0 copy-done.2
  10.1 0.0 copy-done.3
  10.2 0.0 copy-done.4
  10.2 0.0 copy-done.5
  10.2 0.0 copy-done.6
  10.2 0.0 copy-done.7
  10.2 0.0 copy-done.8
  10.2 0.0 copy-done.9
  10.2 5.4 %shard_map.161 = (f32[2,64,128]{2,1,0:T(8,128)S(1)}, f32[64,128]{1,0:T(8,128)S(1)}, f32[64,128]{1,0:T(8,128)S(1)}) custom-call(f32[8,128]{1,0:T(8,128)S(1)} %get-tuple-element.24.marks, f32[2,64,128]{2,1,0:T(8,128)S(1)} %copy-done.4, f32[64,128]{1,0:T(8,128)S(1)} %collective-permute-done.got_a, f32[64,128]{1,0:T(8,128)S(1)} %collective-permute-done.1.got_b, ...), custom_call_target="tpu_custom_call" | custom-call | tf_op jit(solution)/shard_map/pallas_call | solution.py:476
  15.6 0.1 collective-permute-start.2
  15.7 0.5 %collective-permute-start.3 = (f32[64,128]{1,0:T(8,128)S(1)}, f32[64,128]{1,0:T(8,128)S(1)}, u32[]{:S(2)}, u32[]{:S(2)}) collective-permute-start(f32[64,128]{1,0:T(8,128)S(1)} %get-tuple-element.36), channel_id=1, source_target_pairs={{0,16},{1,0},{2,1},{3,2},{4,3},{5,4},{6,5},{7,6},{8,7},{9,8},{10,9... | collective-permute-start | bytes 98312 | tf_op jit(solution)/shard_map/ppermute | solution.py:503
  16.2 0.7 %collective-permute-done.2.got_a = f32[64,128]{1,0:T(8,128)S(1)} collective-permute-done((f32[64,128]{1,0:T(8,128)S(1)}, f32[64,128]{1,0:T(8,128)S(1)}, u32[]{:S(2)}, u32[]{:S(2)}) %collective-permute-start.2) | collective-permute-done | bytes 32800 | tf_op jit(solution)/shard_map/ppermute | solution.py:503
  16.9 3.1 %collective-permute-done.3.got_b = f32[64,128]{1,0:T(8,128)S(1)} collective-permute-done((f32[64,128]{1,0:T(8,128)S(1)}, f32[64,128]{1,0:T(8,128)S(1)}, u32[]{:S(2)}, u32[]{:S(2)}) %collective-permute-start.3) | collective-permute-done | bytes 32800 | tf_op jit(solution)/shard_map/ppermute | solution.py:503
  20.0 0.1 collective-permute-start.4
  20.1 0.5 %collective-permute-start.5 = (f32[64,128]{1,0:T(8,128)S(1)}, f32[64,128]{1,0:T(8,128)S(1)}, u32[]{:S(2)}, u32[]{:S(2)}) collective-permute-start(f32[64,128]{1,0:T(8,128)S(1)} %get-tuple-element.39), channel_id=1, source_target_pairs={{0,16},{1,0},{2,1},{3,2},{4,3},{5,4},{6,5},{7,6},{8,7},{9,8},{10,9... | collective-permute-start | bytes 98312 | tf_op jit(solution)/shard_map/ppermute | solution.py:503
  20.6 0.7 %collective-permute-done.4.got_a = f32[64,128]{1,0:T(8,128)S(1)} collective-permute-done((f32[64,128]{1,0:T(8,128)S(1)}, f32[64,128]{1,0:T(8,128)S(1)}, u32[]{:S(2)}, u32[]{:S(2)}) %collective-permute-start.4) | collective-permute-done | bytes 32800 | tf_op jit(solution)/shard_map/ppermute | solution.py:503
  21.3 3.1 %collective-permute-done.5.got_b = f32[64,128]{1,0:T(8,128)S(1)} collective-permute-done((f32[64,128]{1,0:T(8,128)S(1)}, f32[64,128]{1,0:T(8,128)S(1)}, u32[]{:S(2)}, u32[]{:S(2)}) %collective-permute-start.5) | collective-permute-done | bytes 32800 | tf_op jit(solution)/shard_map/ppermute | solution.py:503
  24.4 5.6 %shard_map.163 = (f32[2,64,128]{2,1,0:T(8,128)S(1)}, f32[2,64,128]{2,1,0:T(8,128)}, f32[64,128]{1,0:T(8,128)S(1)}, f32[64,128]{1,0:T(8,128)S(1)}) custom-call(f32[8,128]{1,0:T(8,128)S(1)} %get-tuple-element.24.marks, f32[2,64,128]{2,1,0:T(8,128)S(1)} %get-tuple-element.37.mp.params, f32[64,128]{1,0:T(8,128)S(1)} %collective-permute-done.4.got_a, ...), custom_call_target="tpu_custom_call" | custom-call | tf_op jit(solution)/shard_map/pallas_call | solution.py:476
  30.0 0.1 collective-permute-start.6
  30.0 0.5 %collective-permute-start.7 = (f32[64,128]{1,0:T(8,128)S(1)}, f32[64,128]{1,0:T(8,128)S(1)}, u32[]{:S(2)}, u32[]{:S(2)}) collective-permute-start(f32[64,128]{1,0:T(8,128)S(1)} %get-tuple-element.42), channel_id=1, source_target_pairs={{0,16},{1,0},{2,1},{3,2},{4,3},{5,4},{6,5},{7,6},{8,7},{9,8},{10,9... | collective-permute-start | bytes 98312 | tf_op jit(solution)/shard_map/ppermute | solution.py:503
  30.5 0.7 %collective-permute-done.6.got_a = f32[64,128]{1,0:T(8,128)S(1)} collective-permute-done((f32[64,128]{1,0:T(8,128)S(1)}, f32[64,128]{1,0:T(8,128)S(1)}, u32[]{:S(2)}, u32[]{:S(2)}) %collective-permute-start.6) | collective-permute-done | bytes 32800 | tf_op jit(solution)/shard_map/ppermute | solution.py:503
  31.2 3.1 %collective-permute-done.7.got_b = f32[64,128]{1,0:T(8,128)S(1)} collective-permute-done((f32[64,128]{1,0:T(8,128)S(1)}, f32[64,128]{1,0:T(8,128)S(1)}, u32[]{:S(2)}, u32[]{:S(2)}) %collective-permute-start.7) | collective-permute-done | bytes 32800 | tf_op jit(solution)/shard_map/ppermute | solution.py:503
  34.3 0.7 %shard_map.164 = f32[2,64,128]{2,1,0:T(8,128)} custom-call(f32[8,128]{1,0:T(8,128)S(1)} %get-tuple-element.24.marks, f32[2,64,128]{2,1,0:T(8,128)S(1)} %get-tuple-element.40.part, f32[2,64,128]{2,1,0:T(8,128)S(1)} %get-tuple-element.37.mp.params, f32[64,128]{1,0:T(8,128)S(1)} %collective-permute-done.6.got_a, f32[64,128]{1,0:T(8,128)S(1)} %collective-permute-done.7.got_b), custom_call_target="tpu_custom_call" | custom-call | tf_op jit(solution)/shard_map/pallas_call | solution.py:476
  (1 shorter events, 0.0 us)
Async XLA Ops:
  0.6 4.3 %copy-start.10 = (bf16[72,72]{1,0:T(8,128)(2,1)S(1)}, bf16[72,72]{1,0:T(8,128)(2,1)}, u32[]{:S(2)}) copy-start(bf16[72,72]{1,0:T(8,128)(2,1)} %constant.23.clone.order) | copy-start | bytes 31108
  0.6 4.3 %copy-start.11 = (f32[24]{0:T(128)S(1)}, f32[24]{0:T(128)}, u32[]{:S(2)}) copy-start(f32[24]{0:T(128)} %param.19) | copy-start | bytes 292
  1.6 6.0 %collective-permute-start = (f32[64,128]{1,0:T(8,128)S(1)}, f32[64,128]{1,0:T(8,128)S(1)}, u32[]{:S(2)}, u32[]{:S(2)}) collective-permute-start(f32[64,128]{1,0:T(8,128)S(1)} %get-tuple-element.25), channel_id=1, source_target_pairs={{0,1},{1,2},{2,3},{3,4},{4,5},{5,6},{6,7},{7,8},{8,9},{9,10},{10,1... | collective-permute-start | bytes 98312 | tf_op jit(solution)/shard_map/ppermute | solution.py:503
  5.0 5.1 %copy-start = (bf16[3,256,256]{2,1,0:T(8,128)(2,1)S(1)}, bf16[3,256,256]{2,1,0:T(8,128)(2,1)}, u32[]{:S(2)}) copy-start(bf16[3,256,256]{2,1,0:T(8,128)(2,1)} %constant.22.clone.rest_12_) | copy-start | bytes 1179652
  5.0 5.1 %copy-start.1 = (bf16[768,256]{1,0:T(8,128)(2,1)S(1)}, bf16[768,256]{1,0:T(8,128)(2,1)}, u32[]{:S(2)}) copy-start(bf16[768,256]{1,0:T(8,128)(2,1)} %constant.20.clone.rest_10_) | copy-start | bytes 1179652
  5.0 5.1 %copy-start.2 = (bf16[384,384]{1,0:T(8,128)(2,1)S(1)}, bf16[384,384]{1,0:T(8,128)(2,1)}, u32[]{:S(2)}) copy-start(bf16[384,384]{1,0:T(8,128)(2,1)} %constant.21.clone.rest_11_) | copy-start | bytes 884740
  5.0 5.1 %copy-start.3 = (bf16[512,256]{1,0:T(8,128)(2,1)S(1)}, bf16[512,256]{1,0:T(8,128)(2,1)}, u32[]{:S(2)}) copy-start(bf16[512,256]{1,0:T(8,128)(2,1)} %constant.18.clone.rest_8_) | copy-start | bytes 786436
  5.0 5.1 %copy-start.4 = (f32[2,64,128]{2,1,0:T(8,128)S(1)}, f32[2,64,128]{2,1,0:T(8,128)}, u32[]{:S(2)}) copy-start(f32[2,64,128]{2,1,0:T(8,128)} %params.3) | copy-start | bytes 196612
  5.1 5.1 %copy-start.5 = (bf16[32,16,128]{2,1,0:T(8,128)(2,1)S(1)}, bf16[32,16,128]{2,1,0:T(8,128)(2,1)}, u32[]{:S(2)}) copy-start(bf16[32,16,128]{2,1,0:T(8,128)(2,1)} %constant.19.clone.rest_9_) | copy-start | bytes 393220
  5.1 5.1 %copy-start.6 = (f32[2,64,128]{2,1,0:T(8,128)S(1)}, f32[2,64,128]{2,1,0:T(8,128)}, u32[]{:S(2)}) copy-start(f32[2,64,128]{2,1,0:T(8,128)} %target.3) | copy-start | bytes 196612
  5.1 5.1 %copy-start.7 = (f32[2,64,128]{2,1,0:T(8,128)S(1)}, f32[2,64,128]{2,1,0:T(8,128)}, u32[]{:S(2)}) copy-start(f32[2,64,128]{2,1,0:T(8,128)} %weight.3) | copy-start | bytes 196612
  5.1 5.1 %copy-start.8 = (bf16[80,192]{1,0:T(8,128)(2,1)S(1)}, bf16[80,192]{1,0:T(8,128)(2,1)}, u32[]{:S(2)}) copy-start(bf16[80,192]{1,0:T(8,128)(2,1)} %constant.17.clone.rest_7_) | copy-start | bytes 92164
  5.1 5.1 %copy-start.9 = (bf16[64,240]{1,0:T(8,128)(2,1)S(1)}, bf16[64,240]{1,0:T(8,128)(2,1)}, u32[]{:S(2)}) copy-start(bf16[64,240]{1,0:T(8,128)(2,1)} %constant.16.clone.rest_6_) | copy-start | bytes 92164
  5.8 4.3 %collective-permute-start.1 = (f32[64,128]{1,0:T(8,128)S(1)}, f32[64,128]{1,0:T(8,128)S(1)}, u32[]{:S(2)}, u32[]{:S(2)}) collective-permute-start(f32[64,128]{1,0:T(8,128)S(1)} %get-tuple-element.27), channel_id=1, source_target_pairs={{0,16},{1,0},{2,1},{3,2},{4,3},{5,4},{6,5},{7,6},{8,7},{9,8},{10,9... | collective-permute-start | bytes 98312 | tf_op jit(solution)/shard_map/ppermute | solution.py:503
  15.6 1.3 %collective-permute-start.2 = (f32[64,128]{1,0:T(8,128)S(1)}, f32[64,128]{1,0:T(8,128)S(1)}, u32[]{:S(2)}, u32[]{:S(2)}) collective-permute-start(f32[64,128]{1,0:T(8,128)S(1)} %get-tuple-element.35), channel_id=1, source_target_pairs={{0,1},{1,2},{2,3},{3,4},{4,5},{5,6},{6,7},{7,8},{8,9},{9,10},{10,1... | collective-permute-start | bytes 98312 | tf_op jit(solution)/shard_map/ppermute | solution.py:503
  15.7 4.2 %collective-permute-start.3 = (f32[64,128]{1,0:T(8,128)S(1)}, f32[64,128]{1,0:T(8,128)S(1)}, u32[]{:S(2)}, u32[]{:S(2)}) collective-permute-start(f32[64,128]{1,0:T(8,128)S(1)} %get-tuple-element.36), channel_id=1, source_target_pairs={{0,16},{1,0},{2,1},{3,2},{4,3},{5,4},{6,5},{7,6},{8,7},{9,8},{10,9... | collective-permute-start | bytes 98312 | tf_op jit(solution)/shard_map/ppermute | solution.py:503
  20.0 1.3 %collective-permute-start.4 = (f32[64,128]{1,0:T(8,128)S(1)}, f32[64,128]{1,0:T(8,128)S(1)}, u32[]{:S(2)}, u32[]{:S(2)}) collective-permute-start(f32[64,128]{1,0:T(8,128)S(1)} %get-tuple-element.38), channel_id=1, source_target_pairs={{0,1},{1,2},{2,3},{3,4},{4,5},{5,6},{6,7},{7,8},{8,9},{9,10},{10,1... | collective-permute-start | bytes 98312 | tf_op jit(solution)/shard_map/ppermute | solution.py:503
  20.1 4.3 %collective-permute-start.5 = (f32[64,128]{1,0:T(8,128)S(1)}, f32[64,128]{1,0:T(8,128)S(1)}, u32[]{:S(2)}, u32[]{:S(2)}) collective-permute-start(f32[64,128]{1,0:T(8,128)S(1)} %get-tuple-element.39), channel_id=1, source_target_pairs={{0,16},{1,0},{2,1},{3,2},{4,3},{5,4},{6,5},{7,6},{8,7},{9,8},{10,9... | collective-permute-start | bytes 98312 | tf_op jit(solution)/shard_map/ppermute | solution.py:503
  30.0 1.3 %collective-permute-start.6 = (f32[64,128]{1,0:T(8,128)S(1)}, f32[64,128]{1,0:T(8,128)S(1)}, u32[]{:S(2)}, u32[]{:S(2)}) collective-permute-start(f32[64,128]{1,0:T(8,128)S(1)} %get-tuple-element.41), channel_id=1, source_target_pairs={{0,1},{1,2},{2,3},{3,4},{4,5},{5,6},{6,7},{7,8},{8,9},{9,10},{10,1... | collective-permute-start | bytes 98312 | tf_op jit(solution)/shard_map/ppermute | solution.py:503
  30.0 4.3 %collective-permute-start.7 = (f32[64,128]{1,0:T(8,128)S(1)}, f32[64,128]{1,0:T(8,128)S(1)}, u32[]{:S(2)}, u32[]{:S(2)}) collective-permute-start(f32[64,128]{1,0:T(8,128)S(1)} %get-tuple-element.42), channel_id=1, source_target_pairs={{0,16},{1,0},{2,1},{3,2},{4,3},{5,4},{6,5},{7,6},{8,7},{9,8},{10,9... | collective-permute-start | bytes 98312 | tf_op jit(solution)/shard_map/ppermute | solution.py:503

commit v2 on v1

--- a/solution.py
+++ b/solution.py
@@ -14,7 +14,7 @@
 THRESHOLD = 0.9
 STEP_SCALE = 0.04
 GROUP = 8
-FIRST = 6
+RUN = 4
 MID = 16
 F32 = jnp.float32
 BF16 = jnp.bfloat16
@@ -92,12 +92,27 @@
             grad=right(gradient),
             spec=np.stack([wide(spectrum[j * cols : (j + 1) * cols]) for j in range(3)]),
         )
-        order = np.zeros((2 * half + 8, 2 * half + 8), jnp.bfloat16)
-        for j in range(half):
-            order[j, half + 1 + j] = 1.0
-            order[half + 8 + j, half - 1 - j] = 1.0
-        order[half, half] = 1.0
-        self.order = order
+        chunk = RUN * 2 * bands
+        frows = 2 * half + 8
+        self.window = 2 * frows
+        order = np.zeros((RUN, 2 * frows, self.window), jnp.bfloat16)
+        self.starts = []
+        for j in range(RUN):
+            start = min(2 * bands * j // 8 * 8, chunk - self.window)
+            self.starts.append(start)
+            for part in range(2):
+                first = 2 * bands * j - start + part
+                base = part * frows
+                for f in range(half):
+                    order[j, base + f, first + 2 * (half + 1 + f)] = 1.0
+                    order[j, base + half + 8 + f, first + 2 * (half - 1 - f)] = 1.0
+                order[j, base + half, first + 2 * half] = 1.0
+        self.order = np.concatenate([order, order], 2)
+        lanes = np.zeros((2 * self.nf, 4 * self.nf), jnp.bfloat16)
+        for j, g in enumerate([*range(half), *range(half + 1, bands)]):
+            lanes[g, j] = lanes[g, self.nf + j] = 1.0
+        lanes[half, 2 * self.nf :] = 1.0
+        self.lanes = np.concatenate([lanes, lanes], 0)
 
 
 def split(v):
@@ -194,18 +209,15 @@
 
 
 class Spectra:
-    def __init__(self, refs):
-        self.runs = (refs[:2], refs[3:5])
-        self.zeros = (refs[2], refs[5])
-        self.count = sum(run[0].shape[0] for run in self.runs)
+    def __init__(self, real, imag, at_zero):
+        self.real, self.imag, self.zero = real, imag, at_zero
+        self.count = real.shape[0]
 
     def __getitem__(self, k):
-        first = self.runs[0][0].shape[0]
-        run, k = (self.runs[0], k) if k < first else (self.runs[1], k - first)
-        return run[0][k], run[1][k]
+        return self.real[k], self.imag[k]
 
     def at_zero(self):
-        return [self.zeros[0][i] + self.zeros[1][i] for i in range(2)]
+        return self.zero[0], self.zero[1]
 
 
 def core(tb, dom, target, weight, spectra, t, e_ref, keep=None):
@@ -350,7 +362,7 @@
 
 
 def kernel_first(tb, names, marks, mp, got_a, got_b, target, weight, *rest):
-    spectra, rest = Spectra(rest[:6]), rest[6:]
+    spectra, rest = Spectra(*rest[:3]), rest[3:]
     t = dict(zip(names, rest))
     part, send_a, send_b, e_ref = rest[len(names) :]
     flags = read_flags(marks, got_a.shape)
@@ -372,7 +384,7 @@
 
 
 def kernel_second(tb, names, marks, mp, got_a, got_b, target, weight, *rest):
-    spectra, rest = Spectra(rest[:6]), rest[6:]
+    spectra, rest = Spectra(*rest[:3]), rest[3:]
     t = dict(zip(names, rest))
     part, resist_out, send_a, send_b, e_ref, resist_v, sems = rest[len(names) :]
     flags = read_flags(marks, got_a.shape)
@@ -400,45 +412,76 @@
     out[1] = jnp.where(flags[0], stepped(step, params[1], g1), params[1])
 
 
-def kernel_arrange(tb, slots, span, weights, kernels, order, carried, out_a, out_b, out_0, passed, padded):
+def kernel_arrange(tb, slots, kernels, weights, order, lanes, out_a, out_b, out_0, padded):
     half, nf = tb.half, tb.nf
     frows, wl = 2 * half + 8, 2 * nf
-    bands = kernels.shape[3]
+    bands = kernels.shape[1]
+    kcount = out_a.shape[0]
     zb = wl // (2 * slots)
-    lane = lane_of((frows, wl))
-    inner = lax.rem(lane, zb)
+    chunk = RUN * 2 * bands
+    padded[...] = jnp.zeros(padded.shape, F32)
+    inner = lax.rem(lane_of((frows, wl)), zb)
+    sign = jnp.where(lane_of((1, wl)) < nf, -1.0, 1.0)
+    zeros = [jnp.zeros((frows, wl), F32) for _ in range(2)]
     roots = jnp.sqrt(weights[...])
-    zeros = [jnp.zeros((frows, wl), F32) for _ in range(2)]
-    padded[...] = jnp.zeros(padded.shape, F32)
-    for n, k in enumerate(span):
-        root = jnp.broadcast_to(roots[:, k : k + 1], (1, bands))
-        for part in range(2):
-            padded[n, part, :bands, :bands] = kernels[k, part] * root
-    for n, k in enumerate(span):
-        for part in range(2):
-            high, low = split(padded[n, part])
-            v = dot(order[...], high) + dot(order[...], low)
-            zero = jnp.broadcast_to(v[:, half : half + 1], (frows, wl))
-            zeros[part] = jnp.where(inner == k, zero, zeros[part])
-            v = jnp.where(lane < half, v, pltpu.roll(v, wl - 1, 1))
-            v = jnp.where(lane < nf, v, pltpu.roll(v, nf, 1))
-            if part == 0:
-                out_a[n] = v
-            else:
-                out_b[n] = -conj(v, nf)
+
+    def order_rows(i):
+        found = {}
+        for j in range(RUN):
+            ks = (i * RUN + j, (i + 1) * RUN + j)
+            for n, k in enumerate(ks):
+                window = pl.ds((i + n) * chunk + tb.starts[j], tb.window)
+                padded[k, :, :bands] = kernels[window, :]
+            high, low = split(jnp.concatenate([padded[k] for k in ks], 1))
+            v = dot(order[j], jnp.concatenate([high, low], 0))
+            for n, k in enumerate(ks):
+                root = jnp.broadcast_to(roots[:, k : k + 1], (1, wl))
+                found[k] = v[:, n * wl : (n + 1) * wl] * root
+        return found
+
+    def order_lanes(found):
+        ks = sorted(found)
+        high, low = split(jnp.concatenate([found[k] for k in ks], 0))
+        v = dot(jnp.concatenate([high, low], 1), lanes[...])
+        for n, k in enumerate(ks):
+            real = v[2 * n * frows : (2 * n + 1) * frows]
+            imag = v[(2 * n + 1) * frows : (2 * n + 2) * frows]
+            out_a[k] = real[:, :wl]
+            out_b[k] = imag[:, :wl] * sign
+            zeros[0] = jnp.where(inner == k, real[:, wl:], zeros[0])
+            zeros[1] = jnp.where(inner == k, imag[:, wl:], zeros[1])
+
+    waiting = None
+    for i in range(0, kcount // RUN, 2):
+        found = order_rows(i)
+        if waiting is not None:
+            order_lanes(waiting)
+        waiting = found
+    order_lanes(waiting)
     out_0[0] = zeros[0]
     out_0[1] = -conj(zeros[1], zb)
-    passed[...] = carried[...]
-
-
-def kernel_choose(ids, links, params, marks, send_a, send_b, ids_s, links_s, params_v, sems):
-    moves = [
-        pltpu.make_async_copy(source, target, sems.at[i])
-        for i, (source, target) in enumerate(((ids, ids_s), (links, links_s), (params, params_v)))
-    ]
+
+
+def arrange(tb, slots, parts, ins):
+    bands, kcount = ins[0].shape[1], ins[1].shape[1]
+    frows, wl = 2 * tb.half + 8, 2 * tb.nf
+    return call(
+        functools.partial(kernel_arrange, tb, slots),
+        list(ins),
+        [(kcount, frows, wl)] * 2 + [(2, frows, wl)],
+        [pltpu.VMEM((kcount, parts * frows, wl), F32)],
+    )
+
+
+def kernel_choose(ids, links, params, *refs):
+    count = (len(refs) - 7) // 2
+    far, (marks, send_a, send_b) = refs[:count], refs[count : count + 3]
+    near, (ids_s, links_s, params_v, sems) = refs[count + 3 : 2 * count + 3], refs[2 * count + 3 :]
+    pairs = [(ids, ids_s), (links, links_s), (params, params_v), *zip(far, near)]
+    moves = [pltpu.make_async_copy(*pair, sems.at[i]) for i, pair in enumerate(pairs)]
     for move in moves:
         move.start()
-    for move in moves:
+    for move in moves[:3]:
         move.wait()
     both = ids_s[1] >= 0
     even = lax.rem(lax.axis_index("grp"), 2) == 0
@@ -450,24 +493,27 @@
     for i, flag in enumerate(flags):
         out = jnp.where(row == i, jnp.where(flag, 1.0, 0.0), out)
     marks[...] = out
-
-
-def choose(*ins):
-    tile_ids, tile_links, mask_params = ins
+    for move in moves[3:]:
+        move.wait()
+
+
+def choose(tile_ids, tile_links, mask_params, far):
     tile = mask_params.shape[1:]
-    far = pl.BlockSpec(memory_space=pltpu.HBM)
+    ins = (tile_ids, tile_links, mask_params, *far)
+    shapes = [jax.ShapeDtypeStruct(s, F32) for s in ((8, tile[1]), tile, tile)]
+    shapes += [jax.ShapeDtypeStruct(v.shape, v.dtype) for v in far]
     return pl.pallas_call(
         kernel_choose,
-        in_specs=[far] * 3,
-        out_specs=[pl.BlockSpec(memory_space=pltpu.VMEM)] * 3,
-        out_shape=[jax.ShapeDtypeStruct(s, F32) for s in ((8, tile[1]), tile, tile)],
+        in_specs=[pl.BlockSpec(memory_space=pltpu.HBM)] * len(ins),
+        out_specs=[pl.BlockSpec(memory_space=pltpu.VMEM)] * len(shapes),
+        out_shape=shapes,
         scratch_shapes=[
             pltpu.SMEM(tile_ids.shape, jnp.int32),
             pltpu.SMEM(tile_links.shape, jnp.int32),
             pltpu.VMEM(mask_params.shape, F32),
-            pltpu.SemaphoreType.DMA((3,)),
+            pltpu.SemaphoreType.DMA((len(ins),)),
         ],
-        compiler_params=pltpu.CompilerParams(vmem_limit_bytes=4 << 20),
+        compiler_params=pltpu.CompilerParams(vmem_limit_bytes=8 << 20),
     )(*(pltpu.with_memory_space_constraint(v, pltpu.HBM) for v in ins))
 
 
@@ -502,22 +548,13 @@
     def exchange(a, b):
         return lax.ppermute(a, axes, ring_a), lax.ppermute(b, axes, ring_b)
 
-    frows = 2 * tb.half + 8
     whole, tile = mask_params.shape, (rows, cols)
 
-    def arrange(span, carried):
-        return call(
-            functools.partial(kernel_arrange, tb, slots, span),
-            [kernel_weight[None], kernels, jnp.asarray(tb.order), carried],
-            [(len(span), frows, 2 * tb.nf)] * 2 + [(2, frows, 2 * tb.nf), carried.shape],
-            [pltpu.VMEM((len(span), 2, frows, 2 * tb.nf), F32)],
-        )
-
-    marks, sa, sb = choose(tile_ids, tile_links, mask_params)
-    *early, sb = arrange(range(FIRST), sb)
-    *late, marks = arrange(range(FIRST, kcount), marks)
+    flat = jnp.swapaxes(kernels, 1, 2).reshape(-1, bands)
+    far = (flat, kernel_weight[None], jnp.asarray(tb.order), jnp.asarray(tb.lanes))
+    marks, sa, sb, *near = choose(tile_ids, tile_links, mask_params, far)
     got = exchange(sa, sb)
-    arranged = early + late
+    arranged = arrange(tb, slots, kernels.shape[1], near)
     field = pltpu.VMEM((slots, kcount, rows, 2 * cols), F32)
     part, sa, sb = call(
         functools.partial(kernel_first, tb, names),

time: 35.2 us -> 33.7 us (0.957)
  local copies, waits for them, and re-layouts: 1.64 us -> 0.07 us
    unnamed x25 -> x20, local copies, waits for them, and re-layouts: 1.64 us -> 0.07 us
    pallas_call x6 -> x5, Pallas kernels: 14 us -> 13.1 us  [call(): pl.pallas_call(body, in_specs=[vmem] * len(ins), out_specs=[pl.BlockSpec(...]
    pallas_call x1, Pallas kernels: 0.89 us -> 1.64 us  [choose(): pl.pallas_call(kernel_choose, in_specs=[pl.BlockSpec(memory_space=pltpu.H...]
  transfers between devices with their start and end apart: 8 -> 8, of which waited for: 7 -> 7; matrix products, arithmetic and copies ran while one was open for 4% -> 0% of each run, Pallas kernels for 7% -> 4%
where the time goes in v2:
time: 33.7 us; the launch traced here: 33.5 us
  Pallas kernels  14.8 us (44%)
  waiting for transfers between devices  14.3 us (42%)
  starting transfers between devices  3.53 us (10%)
  between operations  0.84 us (2%)
    ppermute x8, waiting for transfers between devices, exchange(): return (lax.ppermute(a, axes, ring_a), lax.ppermute(b, axes, ring_b))  14.3 us
    pallas_call x5, Pallas kernels, call(): pl.pallas_call(body, in_specs=[vmem] * len(ins), out_specs=[pl.BlockSpec(...  13.1 us
    ppermute x8, starting transfers between devices, exchange(): return (lax.ppermute(a, axes, ring_a), lax.ppermute(b, axes, ring_b))  3.53 us
    pallas_call x1, Pallas kernels, choose(): pl.pallas_call(kernel_choose, in_specs=[pl.BlockSpec(memory_space=pltpu.H...  1.64 us
  transfers between devices with their start and end apart: 8, of which 7 were waited for; matrix products, arithmetic and copies ran while one was open for 0% of the time, Pallas kernels for 4%

profile of v2, /device:TPU:21, one launch (start us, length us, event | category | flops | bytes accessed | tf_op | source)
XLA Modules:
  0.0 33.5 jit_solution(11170753411548606692)
XLA Ops:
  0.6 1.6 %shard_map.167 = (f32[8,128]{1,0:T(8,128)S(1)}, f32[64,128]{1,0:T(8,128)S(1)}, f32[64,128]{1,0:T(8,128)S(1)}, f32[3120,65]{1,0:T(8,128)S(1)}, f32[1,24]{1,0:T(1,...) custom-call(s32[2]{0:T(128)} %ids.1, s32[2,2]{1,0:T(2,128)} %links.1, f32[2,64,128]{2,1,0:T(8,128)} %params.3, ...), custom_call_target="tpu_custom_call" | custom-call | tf_op jit(solution)/shard_map/pallas_call | solution.py:505
  2.3 0.0 copy-start
  2.3 0.0 copy-start.1
  2.3 0.0 copy-start.2
  2.3 0.0 copy-start.3
  2.3 0.0 copy-start.4
  2.3 0.0 copy-start.5
  2.4 0.0 copy-start.6
  2.4 0.0 copy-start.7
  2.4 0.0 copy-start.8
  2.4 0.0 copy-start.9
  2.4 1.9 %collective-permute-start = (f32[64,128]{1,0:T(8,128)S(1)}, f32[64,128]{1,0:T(8,128)S(1)}, u32[]{:S(2)}, u32[]{:S(2)}) collective-permute-start(f32[64,128]{1,0:T(8,128)S(1)} %get-tuple-element.23), channel_id=1, source_target_pairs={{0,1},{1,2},{2,3},{3,4},{4,5},{5,6},{6,7},{7,8},{8,9},{9,10},{10,1... | collective-permute-start | bytes 98312 | tf_op jit(solution)/shard_map/ppermute | solution.py:549
  4.3 0.0 collective-permute-start.1
  4.3 1.3 %shard_map.168 = (f32[24,72,128]{2,1,0:T(8,128)S(1)}, f32[24,72,128]{2,1,0:T(8,128)S(1)}, f32[2,72,128]{2,1,0:T(8,128)S(1)}) custom-call(f32[3120,65]{1,0:T(8,128)S(1)} %get-tuple-element.25.kernels, f32[1,24]{1,0:T(1,128)S(1)} %get-tuple-element.26.weights, bf16[4,144,288]{2,1,0:T(8,128)(2,1)S(1)} %get-tuple-element.27.order, ...), custom_call_target="tpu_custom_call" | custom-call | tf_op jit(solution)/shard_map/pallas_call | solution.py:522
  5.6 0.0 collective-permute-done.got_a
  5.6 2.9 %collective-permute-done.1.got_b = f32[64,128]{1,0:T(8,128)S(1)} collective-permute-done((f32[64,128]{1,0:T(8,128)S(1)}, f32[64,128]{1,0:T(8,128)S(1)}, u32[]{:S(2)}, u32[]{:S(2)}) %collective-permute-start.1) | collective-permute-done | bytes 32800 | tf_op jit(solution)/shard_map/ppermute | solution.py:549
  8.5 0.0 copy-done
  8.5 0.0 copy-done.1
  8.5 0.0 copy-done.2
  8.5 0.0 copy-done.3
  8.5 0.0 copy-done.4
  8.5 0.0 copy-done.5
  8.5 0.0 copy-done.6
  8.5 0.0 copy-done.7
  8.6 0.0 copy-done.8
  8.6 0.0 copy-done.9
  8.6 5.4 %shard_map.169 = (f32[2,64,128]{2,1,0:T(8,128)S(1)}, f32[64,128]{1,0:T(8,128)S(1)}, f32[64,128]{1,0:T(8,128)S(1)}) custom-call(f32[8,128]{1,0:T(8,128)S(1)} %get-tuple-element.22.marks, f32[2,64,128]{2,1,0:T(8,128)S(1)} %copy-done.4, f32[64,128]{1,0:T(8,128)S(1)} %collective-permute-done.got_a, f32[64,128]{1,0:T(8,128)S(1)} %collective-permute-done.1.got_b, ...), custom_call_target="tpu_custom_call" | custom-call | tf_op jit(solution)/shard_map/pallas_call | solution.py:522
  14.0 0.1 collective-permute-start.2
  14.1 0.5 %collective-permute-start.3 = (f32[64,128]{1,0:T(8,128)S(1)}, f32[64,128]{1,0:T(8,128)S(1)}, u32[]{:S(2)}, u32[]{:S(2)}) collective-permute-start(f32[64,128]{1,0:T(8,128)S(1)} %get-tuple-element.34), channel_id=1, source_target_pairs={{0,16},{1,0},{2,1},{3,2},{4,3},{5,4},{6,5},{7,6},{8,7},{9,8},{10,9... | collective-permute-start | bytes 98312 | tf_op jit(solution)/shard_map/ppermute | solution.py:549
  14.6 0.7 %collective-permute-done.2.got_a = f32[64,128]{1,0:T(8,128)S(1)} collective-permute-done((f32[64,128]{1,0:T(8,128)S(1)}, f32[64,128]{1,0:T(8,128)S(1)}, u32[]{:S(2)}, u32[]{:S(2)}) %collective-permute-start.2) | collective-permute-done | bytes 32800 | tf_op jit(solution)/shard_map/ppermute | solution.py:549
  15.3 3.1 %collective-permute-done.3.got_b = f32[64,128]{1,0:T(8,128)S(1)} collective-permute-done((f32[64,128]{1,0:T(8,128)S(1)}, f32[64,128]{1,0:T(8,128)S(1)}, u32[]{:S(2)}, u32[]{:S(2)}) %collective-permute-start.3) | collective-permute-done | bytes 32800 | tf_op jit(solution)/shard_map/ppermute | solution.py:549
  18.4 0.1 collective-permute-start.4
  18.5 0.5 %collective-permute-start.5 = (f32[64,128]{1,0:T(8,128)S(1)}, f32[64,128]{1,0:T(8,128)S(1)}, u32[]{:S(2)}, u32[]{:S(2)}) collective-permute-start(f32[64,128]{1,0:T(8,128)S(1)} %get-tuple-element.37), channel_id=1, source_target_pairs={{0,16},{1,0},{2,1},{3,2},{4,3},{5,4},{6,5},{7,6},{8,7},{9,8},{10,9... | collective-permute-start | bytes 98312 | tf_op jit(solution)/shard_map/ppermute | solution.py:549
  19.0 0.7 %collective-permute-done.4.got_a = f32[64,128]{1,0:T(8,128)S(1)} collective-permute-done((f32[64,128]{1,0:T(8,128)S(1)}, f32[64,128]{1,0:T(8,128)S(1)}, u32[]{:S(2)}, u32[]{:S(2)}) %collective-permute-start.4) | collective-permute-done | bytes 32800 | tf_op jit(solution)/shard_map/ppermute | solution.py:549
  19.7 3.1 %collective-permute-done.5.got_b = f32[64,128]{1,0:T(8,128)S(1)} collective-permute-done((f32[64,128]{1,0:T(8,128)S(1)}, f32[64,128]{1,0:T(8,128)S(1)}, u32[]{:S(2)}, u32[]{:S(2)}) %collective-permute-start.5) | collective-permute-done | bytes 32800 | tf_op jit(solution)/shard_map/ppermute | solution.py:549
  22.8 5.7 %shard_map.171 = (f32[2,64,128]{2,1,0:T(8,128)S(1)}, f32[2,64,128]{2,1,0:T(8,128)}, f32[64,128]{1,0:T(8,128)S(1)}, f32[64,128]{1,0:T(8,128)S(1)}) custom-call(f32[8,128]{1,0:T(8,128)S(1)} %get-tuple-element.22.marks, f32[2,64,128]{2,1,0:T(8,128)S(1)} %get-tuple-element.35.mp.params, f32[64,128]{1,0:T(8,128)S(1)} %collective-permute-done.4.got_a, ...), custom_call_target="tpu_custom_call" | custom-call | tf_op jit(solution)/shard_map/pallas_call | solution.py:522
  28.5 0.1 collective-permute-start.6
  28.6 0.5 %collective-permute-start.7 = (f32[64,128]{1,0:T(8,128)S(1)}, f32[64,128]{1,0:T(8,128)S(1)}, u32[]{:S(2)}, u32[]{:S(2)}) collective-permute-start(f32[64,128]{1,0:T(8,128)S(1)} %get-tuple-element.40), channel_id=1, source_target_pairs={{0,16},{1,0},{2,1},{3,2},{4,3},{5,4},{6,5},{7,6},{8,7},{9,8},{10,9... | collective-permute-start | bytes 98312 | tf_op jit(solution)/shard_map/ppermute | solution.py:549
  29.1 0.7 %collective-permute-done.6.got_a = f32[64,128]{1,0:T(8,128)S(1)} collective-permute-done((f32[64,128]{1,0:T(8,128)S(1)}, f32[64,128]{1,0:T(8,128)S(1)}, u32[]{:S(2)}, u32[]{:S(2)}) %collective-permute-start.6) | collective-permute-done | bytes 32800 | tf_op jit(solution)/shard_map/ppermute | solution.py:549
  29.8 3.1 %collective-permute-done.7.got_b = f32[64,128]{1,0:T(8,128)S(1)} collective-permute-done((f32[64,128]{1,0:T(8,128)S(1)}, f32[64,128]{1,0:T(8,128)S(1)}, u32[]{:S(2)}, u32[]{:S(2)}) %collective-permute-start.7) | collective-permute-done | bytes 32800 | tf_op jit(solution)/shard_map/ppermute | solution.py:549
  32.9 0.7 %shard_map.172 = f32[2,64,128]{2,1,0:T(8,128)} custom-call(f32[8,128]{1,0:T(8,128)S(1)} %get-tuple-element.22.marks, f32[2,64,128]{2,1,0:T(8,128)S(1)} %get-tuple-element.38.part, f32[2,64,128]{2,1,0:T(8,128)S(1)} %get-tuple-element.35.mp.params, f32[64,128]{1,0:T(8,128)S(1)} %collective-permute-done.6.got_a, f32[64,128]{1,0:T(8,128)S(1)} %collective-permute-done.7.got_b), custom_call_target="tpu_custom_call" | custom-call | tf_op jit(solution)/shard_map/pallas_call | solution.py:522
  (1 shorter events, 0.0 us)
Async XLA Ops:
  2.3 6.2 %copy-start = (bf16[3,256,256]{2,1,0:T(8,128)(2,1)S(1)}, bf16[3,256,256]{2,1,0:T(8,128)(2,1)}, u32[]{:S(2)}) copy-start(bf16[3,256,256]{2,1,0:T(8,128)(2,1)} %constant.24.clone.rest_9_) | copy-start | bytes 1179652
  2.3 6.2 %copy-start.1 = (bf16[768,256]{1,0:T(8,128)(2,1)S(1)}, bf16[768,256]{1,0:T(8,128)(2,1)}, u32[]{:S(2)}) copy-start(bf16[768,256]{1,0:T(8,128)(2,1)} %constant.22.clone.rest_7_) | copy-start | bytes 1179652
  2.3 6.2 %copy-start.2 = (bf16[384,384]{1,0:T(8,128)(2,1)S(1)}, bf16[384,384]{1,0:T(8,128)(2,1)}, u32[]{:S(2)}) copy-start(bf16[384,384]{1,0:T(8,128)(2,1)} %constant.23.clone.rest_8_) | copy-start | bytes 884740
  2.3 6.2 %copy-start.3 = (bf16[512,256]{1,0:T(8,128)(2,1)S(1)}, bf16[512,256]{1,0:T(8,128)(2,1)}, u32[]{:S(2)}) copy-start(bf16[512,256]{1,0:T(8,128)(2,1)} %constant.20.clone.rest_5_) | copy-start | bytes 786436
  2.3 6.2 %copy-start.4 = (f32[2,64,128]{2,1,0:T(8,128)S(1)}, f32[2,64,128]{2,1,0:T(8,128)}, u32[]{:S(2)}) copy-start(f32[2,64,128]{2,1,0:T(8,128)} %params.3) | copy-start | bytes 196612
  2.3 6.2 %copy-start.5 = (bf16[32,16,128]{2,1,0:T(8,128)(2,1)S(1)}, bf16[32,16,128]{2,1,0:T(8,128)(2,1)}, u32[]{:S(2)}) copy-start(bf16[32,16,128]{2,1,0:T(8,128)(2,1)} %constant.21.clone.rest_6_) | copy-start | bytes 393220
  2.4 6.2 %copy-start.6 = (f32[2,64,128]{2,1,0:T(8,128)S(1)}, f32[2,64,128]{2,1,0:T(8,128)}, u32[]{:S(2)}) copy-start(f32[2,64,128]{2,1,0:T(8,128)} %target.3) | copy-start | bytes 196612
  2.4 6.2 %copy-start.7 = (f32[2,64,128]{2,1,0:T(8,128)S(1)}, f32[2,64,128]{2,1,0:T(8,128)}, u32[]{:S(2)}) copy-start(f32[2,64,128]{2,1,0:T(8,128)} %weight.3) | copy-start | bytes 196612
  2.4 6.2 %copy-start.8 = (bf16[80,192]{1,0:T(8,128)(2,1)S(1)}, bf16[80,192]{1,0:T(8,128)(2,1)}, u32[]{:S(2)}) copy-start(bf16[80,192]{1,0:T(8,128)(2,1)} %constant.19.clone.rest_4_) | copy-start | bytes 92164
  2.4 6.2 %copy-start.9 = (bf16[64,240]{1,0:T(8,128)(2,1)S(1)}, bf16[64,240]{1,0:T(8,128)(2,1)}, u32[]{:S(2)}) copy-start(bf16[64,240]{1,0:T(8,128)(2,1)} %constant.18.clone.rest_3_) | copy-start | bytes 92164
  2.4 3.2 %collective-permute-start = (f32[64,128]{1,0:T(8,128)S(1)}, f32[64,128]{1,0:T(8,128)S(1)}, u32[]{:S(2)}, u32[]{:S(2)}) collective-permute-start(f32[64,128]{1,0:T(8,128)S(1)} %get-tuple-element.23), channel_id=1, source_target_pairs={{0,1},{1,2},{2,3},{3,4},{4,5},{5,6},{6,7},{7,8},{8,9},{9,10},{10,1... | collective-permute-start | bytes 98312 | tf_op jit(solution)/shard_map/ppermute | solution.py:549
  4.3 4.2 %collective-permute-start.1 = (f32[64,128]{1,0:T(8,128)S(1)}, f32[64,128]{1,0:T(8,128)S(1)}, u32[]{:S(2)}, u32[]{:S(2)}) collective-permute-start(f32[64,128]{1,0:T(8,128)S(1)} %get-tuple-element.24), channel_id=1, source_target_pairs={{0,16},{1,0},{2,1},{3,2},{4,3},{5,4},{6,5},{7,6},{8,7},{9,8},{10,9... | collective-permute-start | bytes 98312 | tf_op jit(solution)/shard_map/ppermute | solution.py:549
  14.0 1.3 %collective-permute-start.2 = (f32[64,128]{1,0:T(8,128)S(1)}, f32[64,128]{1,0:T(8,128)S(1)}, u32[]{:S(2)}, u32[]{:S(2)}) collective-permute-start(f32[64,128]{1,0:T(8,128)S(1)} %get-tuple-element.33), channel_id=1, source_target_pairs={{0,1},{1,2},{2,3},{3,4},{4,5},{5,6},{6,7},{7,8},{8,9},{9,10},{10,1... | collective-permute-start | bytes 98312 | tf_op jit(solution)/shard_map/ppermute | solution.py:549
  14.1 4.3 %collective-permute-start.3 = (f32[64,128]{1,0:T(8,128)S(1)}, f32[64,128]{1,0:T(8,128)S(1)}, u32[]{:S(2)}, u32[]{:S(2)}) collective-permute-start(f32[64,128]{1,0:T(8,128)S(1)} %get-tuple-element.34), channel_id=1, source_target_pairs={{0,16},{1,0},{2,1},{3,2},{4,3},{5,4},{6,5},{7,6},{8,7},{9,8},{10,9... | collective-permute-start | bytes 98312 | tf_op jit(solution)/shard_map/ppermute | solution.py:549
  18.4 1.3 %collective-permute-start.4 = (f32[64,128]{1,0:T(8,128)S(1)}, f32[64,128]{1,0:T(8,128)S(1)}, u32[]{:S(2)}, u32[]{:S(2)}) collective-permute-start(f32[64,128]{1,0:T(8,128)S(1)} %get-tuple-element.36), channel_id=1, source_target_pairs={{0,1},{1,2},{2,3},{3,4},{4,5},{5,6},{6,7},{7,8},{8,9},{9,10},{10,1... | collective-permute-start | bytes 98312 | tf_op jit(solution)/shard_map/ppermute | solution.py:549
  18.5 4.3 %collective-permute-start.5 = (f32[64,128]{1,0:T(8,128)S(1)}, f32[64,128]{1,0:T(8,128)S(1)}, u32[]{:S(2)}, u32[]{:S(2)}) collective-permute-start(f32[64,128]{1,0:T(8,128)S(1)} %get-tuple-element.37), channel_id=1, source_target_pairs={{0,16},{1,0},{2,1},{3,2},{4,3},{5,4},{6,5},{7,6},{8,7},{9,8},{10,9... | collective-permute-start | bytes 98312 | tf_op jit(solution)/shard_map/ppermute | solution.py:549
  28.5 1.3 %collective-permute-start.6 = (f32[64,128]{1,0:T(8,128)S(1)}, f32[64,128]{1,0:T(8,128)S(1)}, u32[]{:S(2)}, u32[]{:S(2)}) collective-permute-start(f32[64,128]{1,0:T(8,128)S(1)} %get-tuple-element.39), channel_id=1, source_target_pairs={{0,1},{1,2},{2,3},{3,4},{4,5},{5,6},{6,7},{7,8},{8,9},{9,10},{10,1... | collective-permute-start | bytes 98312 | tf_op jit(solution)/shard_map/ppermute | solution.py:549
  28.6 4.3 %collective-permute-start.7 = (f32[64,128]{1,0:T(8,128)S(1)}, f32[64,128]{1,0:T(8,128)S(1)}, u32[]{:S(2)}, u32[]{:S(2)}) collective-permute-start(f32[64,128]{1,0:T(8,128)S(1)} %get-tuple-element.40), channel_id=1, source_target_pairs={{0,16},{1,0},{2,1},{3,2},{4,3},{5,4},{6,5},{7,6},{8,7},{9,8},{10,9... | collective-permute-start | bytes 98312 | tf_op jit(solution)/shard_map/ppermute | solution.py:549

commit v3 on v2

--- a/solution.py
+++ b/solution.py
@@ -88,7 +88,7 @@
             tyt=left(ty.T),
             fwd=np.concatenate([right(forward), ones.astype(jnp.bfloat16)], 0),
             picks=picks,
-            adj=np.concatenate([right(adjoint), sums], 1),
+            adj=wide(adjoint),
             grad=right(gradient),
             spec=np.stack([wide(spectrum[j * cols : (j + 1) * cols]) for j in range(3)]),
         )
@@ -167,11 +167,6 @@
     return jnp.concatenate([plus, zero, gap, minus], 0)
 
 
-def spread(half, o, block):
-    cosine, zero, sine = o[:half], o[half : half + 8], minus_i(o[half + MID :], block)
-    return jnp.concatenate([cosine + sine, zero, cosine - sine], 0)
-
-
 def drive(half, a, b, u):
     p, m = slice(0, half), slice(half + 8, 2 * half + 8)
     d = a * u[0] + b * u[1]
@@ -180,8 +175,12 @@
     return fold(half, d[p] + d[m], d[half : half + 8], turned_p - turned_m)
 
 
-def phases(u, block):
-    v = swap(u, block)
+def phases(half, o, block):
+    cosine, zero, sine = o[:half], o[half : half + 8], o[half + MID :]
+    turned = conj(swap(sine, block), block)
+    u = jnp.concatenate([cosine + turned, zero, cosine - turned], 0)
+    other, back = swap(o[: half + 8], block), conj(sine, block)
+    v = jnp.concatenate([other[:half] - back, other[half:], other[:half] + back], 0)
     return u, v, -conj(v, block), conj(u, block)
 
 
@@ -200,8 +199,10 @@
 
 
 def back_rows(half, q, block):
-    p, z, m = (q[j] - swap(q[j + 3], block) for j in range(3))
-    return fold(half, p + m, z, minus_i(p - m, block))
+    plus = q[0] + q[2] - swap(q[3] + q[5], block)
+    zero = q[1] - swap(q[4], block)
+    turned = conj(swap(q[0] - q[2], block) - (q[3] - q[5]), block)
+    return fold(half, plus, zero, turned)
 
 
 def lane_sum(v):
@@ -231,13 +232,13 @@
     g = sum(wide_dot(v, t["spec"][j]) for j, v in enumerate(thirds_of))
     gw = jnp.concatenate([g[s * rows : (s + 1) * rows] for s in range(slots)], 1)
     spec = dot(tyt[...], rows3(gw))
-    us = [phases(spread(half, spec[:, s * wl : (s + 1) * wl], nf), nf) for s in range(slots)]
+    us = [phases(half, spec[:, s * wl : (s + 1) * wl], nf) for s in range(slots)]
     g0 = lane_sum(thirds_of[0] + thirds_of[1] + thirds_of[2]) * tb.area
     block = lax.div(lane_of((rows, wl)), zb)
     g0w = jnp.zeros((rows, wl), F32)
     for s in range(slots):
         g0w = jnp.where(block == 2 * s, g0[s * rows : (s + 1) * rows], g0w)
-    u0 = phases(spread(half, dot(tyt[...], rows3(g0w)), zb), zb)
+    u0 = phases(half, dot(tyt[...], rows3(g0w)), zb)
     a0, b0 = spectra.at_zero()
     r0 = dot(ty[...], rows3(drive(half, a0, b0, u0)))
     r0h, r0l = split(r0)
@@ -275,15 +276,19 @@
         return resist, jnp.concatenate([slope, slope], 1)
 
     def column_stage(s, ks, slope2):
-        back = jnp.concatenate([e_ref[s, k] * slope2 for k in ks], 0)
-        return dot(lanes3(back), t["adj"][...])
+        back = [e_ref[s, k] * slope2 for k in ks]
+        flat = [(lane_sum(v[:, :cols]), -lane_sum(v[:, cols:])) for v in back]
+        return wide_dot(jnp.concatenate(back, 0), t["adj"][...]), flat
 
     def sum_stage(s, ks, ready, c0, q):
         for m, pair in enumerate(in_pairs(ks)):
-            parts = [ready[(2 * m + n) * rows : (2 * m + n + 1) * rows] for n in range(len(pair))]
+            parts = [
+                ready[0][(2 * m + n) * rows : (2 * m + n + 1) * rows] for n in range(len(pair))
+            ]
             o = dot(tyt[...], rows3(jnp.concatenate([v[:, :wl] for v in parts], 1)))
             for n, k in enumerate(pair):
-                c0 = jnp.where(inner == k, parts[n][:, wl:], c0)
+                zr, zi = ready[1][2 * m + n]
+                c0 = jnp.where(inner == k, jnp.where(lax.rem(block, 2) == 0, zr, zi), c0)
                 q = gather(half, q, *spectra[k], o[:, n * wl : (n + 1) * wl], nf)
         return c0, q
 
@@ -386,22 +391,22 @@
 def kernel_second(tb, names, marks, mp, got_a, got_b, target, weight, *rest):
     spectra, rest = Spectra(*rest[:3]), rest[3:]
     t = dict(zip(names, rest))
-    part, resist_out, send_a, send_b, e_ref, resist_v, sems = rest[len(names) :]
+    part, resist_out, send_a, send_b, e_ref = rest[len(names) :]
     flags = read_flags(marks, got_a.shape)
     prev, nxt = in_order(flags[5], got_a[...], got_b[...])
     tile = [jnp.tanh(v) for v in (prev, mp[0], mp[1], nxt)]
-    moves = []
-
     def keep(s, resist):
-        resist_v[s] = resist if s == 0 else jnp.where(flags[0], resist, 0.0)
-        moves.append(pltpu.make_async_copy(resist_v.at[s], resist_out.at[s], sems.at[s]))
-        moves[-1].start()
+        resist_out[s] = resist if s == 0 else jnp.where(flags[0], resist, 0.0)
 
     dg = core(tb, domain_of(flags, *tile), target, weight, spectra, t, e_ref, keep)
     part[0], part[1], to_next, to_prev = thirds(flags, dg)
     send_a[...], send_b[...] = in_order(flags[5], to_next, to_prev)
-    for move in moves:
-        move.wait()
+
+
+def kernel_store(image, out, sem):
+    move = pltpu.make_async_copy(image, out, sem)
+    move.start()
+    move.wait()
 
 
 def kernel_last(step, marks, part, params, got_a, got_b, out):
@@ -571,12 +576,13 @@
         functools.partial(kernel_second, tb, names),
         [marks, params, *exchange(sa, sb), target, weight, *arranged, *tables],
         [whole, whole, tile, tile],
-        [field, pltpu.VMEM(whole, F32), pltpu.SemaphoreType.DMA((slots,))],
-        moved=(1,),
+        [field],
     )
+    got = exchange(sa, sb)
+    (resist,) = call(kernel_store, [resist], [whole], [pltpu.SemaphoreType.DMA], moved=(0,))
     (out,) = call(
         functools.partial(kernel_last, step),
-        [marks, part, params, *exchange(sa, sb)],
+        [marks, part, params, *got],
         [whole],
     )
     return (out, resist)

time: 33.7 us -> 32 us (0.950)
  Pallas kernels: 14.8 us -> 13.7 us
  waiting for transfers between devices: 14.3 us -> 13.7 us
    pallas_call x5 -> x6, Pallas kernels: 13.1 us -> 12.1 us  [call(): pl.pallas_call(body, in_specs=[vmem] * len(ins), out_specs=[pl.BlockSpec(...]
    ppermute x8, waiting for transfers between devices: 14.3 us -> 13.7 us  [exchange(): return (lax.ppermute(a, axes, ring_a), lax.ppermute(b, axes, ring_b))]
  transfers between devices with their start and end apart: 8 -> 8, of which waited for: 7 -> 7; matrix products, arithmetic and copies ran while one was open for 0% -> 0% of each run, Pallas kernels for 4% -> 6%
where the time goes in v3:
time: 32 us; the launch traced here: 31.8 us
  Pallas kernels  13.7 us (43%)
  waiting for transfers between devices  13.7 us (43%)
  starting transfers between devices  3.54 us (11%)
  between operations  0.84 us (3%)
    ppermute x8, waiting for transfers between devices, exchange(): return (lax.ppermute(a, axes, ring_a), lax.ppermute(b, axes, ring_b))  13.7 us
    pallas_call x6, Pallas kernels, call(): pl.pallas_call(body, in_specs=[vmem] * len(ins), out_specs=[pl.BlockSpec(...  12.1 us
    ppermute x8, starting transfers between devices, exchange(): return (lax.ppermute(a, axes, ring_a), lax.ppermute(b, axes, ring_b))  3.54 us
    pallas_call x1, Pallas kernels, choose(): pl.pallas_call(kernel_choose, in_specs=[pl.BlockSpec(memory_space=pltpu.H...  1.64 us
  transfers between devices with their start and end apart: 8, of which 7 were waited for; matrix products, arithmetic and copies ran while one was open for 0% of the time, Pallas kernels for 6%

profile of v3, /device:TPU:21, one launch (start us, length us, event | category | flops | bytes accessed | tf_op | source)
XLA Modules:
  0.0 31.8 jit_solution(8288575663574161660)
XLA Ops:
  0.6 1.6 %shard_map.167 = (f32[8,128]{1,0:T(8,128)S(1)}, f32[64,128]{1,0:T(8,128)S(1)}, f32[64,128]{1,0:T(8,128)S(1)}, f32[3120,65]{1,0:T(8,128)S(1)}, f32[1,24]{1,0:T(1,...) custom-call(s32[2]{0:T(128)} %ids.1, s32[2,2]{1,0:T(2,128)} %links.1, f32[2,64,128]{2,1,0:T(8,128)} %params.3, ...), custom_call_target="tpu_custom_call" | custom-call | tf_op jit(solution)/shard_map/pallas_call | solution.py:510
  2.3 0.0 copy-start
  2.3 0.0 copy-start.1
  2.3 0.0 copy-start.2
  2.3 0.0 copy-start.3
  2.3 0.0 copy-start.4
  2.3 0.0 copy-start.5
  2.4 0.0 copy-start.6
  2.4 0.0 copy-start.7
  2.4 0.0 copy-start.8
  2.4 0.0 copy-start.9
  2.4 1.9 %collective-permute-start = (f32[64,128]{1,0:T(8,128)S(1)}, f32[64,128]{1,0:T(8,128)S(1)}, u32[]{:S(2)}, u32[]{:S(2)}) collective-permute-start(f32[64,128]{1,0:T(8,128)S(1)} %get-tuple-element.23), channel_id=1, source_target_pairs={{0,1},{1,2},{2,3},{3,4},{4,5},{5,6},{6,7},{7,8},{8,9},{9,10},{10,1... | collective-permute-start | bytes 98312 | tf_op jit(solution)/shard_map/ppermute | solution.py:554
  4.3 0.0 collective-permute-start.1
  4.3 1.3 %shard_map.168 = (f32[24,72,128]{2,1,0:T(8,128)S(1)}, f32[24,72,128]{2,1,0:T(8,128)S(1)}, f32[2,72,128]{2,1,0:T(8,128)S(1)}) custom-call(f32[3120,65]{1,0:T(8,128)S(1)} %get-tuple-element.25.kernels, f32[1,24]{1,0:T(1,128)S(1)} %get-tuple-element.26.weights, bf16[4,144,288]{2,1,0:T(8,128)(2,1)S(1)} %get-tuple-element.27.order, ...), custom_call_target="tpu_custom_call" | custom-call | tf_op jit(solution)/shard_map/pallas_call | solution.py:527
  5.6 0.0 collective-permute-done.got_a
  5.6 2.9 %collective-permute-done.1.got_b = f32[64,128]{1,0:T(8,128)S(1)} collective-permute-done((f32[64,128]{1,0:T(8,128)S(1)}, f32[64,128]{1,0:T(8,128)S(1)}, u32[]{:S(2)}, u32[]{:S(2)}) %collective-permute-start.1) | collective-permute-done | bytes 32800 | tf_op jit(solution)/shard_map/ppermute | solution.py:554
  8.5 0.0 copy-done
  8.5 0.0 copy-done.1
  8.5 0.0 copy-done.2
  8.5 0.0 copy-done.3
  8.5 0.0 copy-done.4
  8.5 0.0 copy-done.5
  8.5 0.0 copy-done.6
  8.5 0.0 copy-done.7
  8.6 0.0 copy-done.8
  8.6 0.0 copy-done.9
  8.6 4.7 %shard_map.169 = (f32[2,64,128]{2,1,0:T(8,128)S(1)}, f32[64,128]{1,0:T(8,128)S(1)}, f32[64,128]{1,0:T(8,128)S(1)}) custom-call(f32[8,128]{1,0:T(8,128)S(1)} %get-tuple-element.22.marks, f32[2,64,128]{2,1,0:T(8,128)S(1)} %copy-done.4, f32[64,128]{1,0:T(8,128)S(1)} %collective-permute-done.got_a, f32[64,128]{1,0:T(8,128)S(1)} %collective-permute-done.1.got_b, ...), custom_call_target="tpu_custom_call" | custom-call | tf_op jit(solution)/shard_map/pallas_call | solution.py:527
  13.3 0.1 collective-permute-start.2
  13.4 0.5 %collective-permute-start.3 = (f32[64,128]{1,0:T(8,128)S(1)}, f32[64,128]{1,0:T(8,128)S(1)}, u32[]{:S(2)}, u32[]{:S(2)}) collective-permute-start(f32[64,128]{1,0:T(8,128)S(1)} %get-tuple-element.34), channel_id=1, source_target_pairs={{0,16},{1,0},{2,1},{3,2},{4,3},{5,4},{6,5},{7,6},{8,7},{9,8},{10,9... | collective-permute-start | bytes 98312 | tf_op jit(solution)/shard_map/ppermute | solution.py:554
  13.9 0.7 %collective-permute-done.2.got_a = f32[64,128]{1,0:T(8,128)S(1)} collective-permute-done((f32[64,128]{1,0:T(8,128)S(1)}, f32[64,128]{1,0:T(8,128)S(1)}, u32[]{:S(2)}, u32[]{:S(2)}) %collective-permute-start.2) | collective-permute-done | bytes 32800 | tf_op jit(solution)/shard_map/ppermute | solution.py:554
  14.6 3.1 %collective-permute-done.3.got_b = f32[64,128]{1,0:T(8,128)S(1)} collective-permute-done((f32[64,128]{1,0:T(8,128)S(1)}, f32[64,128]{1,0:T(8,128)S(1)}, u32[]{:S(2)}, u32[]{:S(2)}) %collective-permute-start.3) | collective-permute-done | bytes 32800 | tf_op jit(solution)/shard_map/ppermute | solution.py:554
  17.7 0.1 collective-permute-start.4
  17.8 0.5 %collective-permute-start.5 = (f32[64,128]{1,0:T(8,128)S(1)}, f32[64,128]{1,0:T(8,128)S(1)}, u32[]{:S(2)}, u32[]{:S(2)}) collective-permute-start(f32[64,128]{1,0:T(8,128)S(1)} %get-tuple-element.37), channel_id=1, source_target_pairs={{0,16},{1,0},{2,1},{3,2},{4,3},{5,4},{6,5},{7,6},{8,7},{9,8},{10,9... | collective-permute-start | bytes 98312 | tf_op jit(solution)/shard_map/ppermute | solution.py:554
  18.3 0.7 %collective-permute-done.4.got_a = f32[64,128]{1,0:T(8,128)S(1)} collective-permute-done((f32[64,128]{1,0:T(8,128)S(1)}, f32[64,128]{1,0:T(8,128)S(1)}, u32[]{:S(2)}, u32[]{:S(2)}) %collective-permute-start.4) | collective-permute-done | bytes 32800 | tf_op jit(solution)/shard_map/ppermute | solution.py:554
  19.0 3.1 %collective-permute-done.5.got_b = f32[64,128]{1,0:T(8,128)S(1)} collective-permute-done((f32[64,128]{1,0:T(8,128)S(1)}, f32[64,128]{1,0:T(8,128)S(1)}, u32[]{:S(2)}, u32[]{:S(2)}) %collective-permute-start.5) | collective-permute-done | bytes 32800 | tf_op jit(solution)/shard_map/ppermute | solution.py:554
  22.1 4.7 %shard_map.171 = (f32[2,64,128]{2,1,0:T(8,128)S(1)}, f32[2,64,128]{2,1,0:T(8,128)S(1)}, f32[64,128]{1,0:T(8,128)S(1)}, f32[64,128]{1,0:T(8,128)S(1)}) custom-call(f32[8,128]{1,0:T(8,128)S(1)} %get-tuple-element.22.marks, f32[2,64,128]{2,1,0:T(8,128)S(1)} %get-tuple-element.35.mp.params, f32[64,128]{1,0:T(8,128)S(1)} %collective-permute-done.4.got_a, ...), custom_call_target="tpu_custom_call" | custom-call | tf_op jit(solution)/shard_map/pallas_call | solution.py:527
  26.8 0.1 collective-permute-start.6
  26.8 0.5 %collective-permute-start.7 = (f32[64,128]{1,0:T(8,128)S(1)}, f32[64,128]{1,0:T(8,128)S(1)}, u32[]{:S(2)}, u32[]{:S(2)}) collective-permute-start(f32[64,128]{1,0:T(8,128)S(1)} %get-tuple-element.40), channel_id=1, source_target_pairs={{0,16},{1,0},{2,1},{3,2},{4,3},{5,4},{6,5},{7,6},{8,7},{9,8},{10,9... | collective-permute-start | bytes 98312 | tf_op jit(solution)/shard_map/ppermute | solution.py:554
  27.3 0.6 %shard_map.173 = f32[2,64,128]{2,1,0:T(8,128)} custom-call(f32[2,64,128]{2,1,0:T(8,128)S(1)} %get-tuple-element.41.image), custom_call_target="tpu_custom_call" | custom-call | tf_op jit(solution)/shard_map/pallas_call | solution.py:527
  28.0 0.1 collective-permute-done.6.got_a
  28.0 3.1 %collective-permute-done.7.got_b = f32[64,128]{1,0:T(8,128)S(1)} collective-permute-done((f32[64,128]{1,0:T(8,128)S(1)}, f32[64,128]{1,0:T(8,128)S(1)}, u32[]{:S(2)}, u32[]{:S(2)}) %collective-permute-start.7) | collective-permute-done | bytes 32800 | tf_op jit(solution)/shard_map/ppermute | solution.py:554
  31.1 0.7 %shard_map.172 = f32[2,64,128]{2,1,0:T(8,128)} custom-call(f32[8,128]{1,0:T(8,128)S(1)} %get-tuple-element.22.marks, f32[2,64,128]{2,1,0:T(8,128)S(1)} %get-tuple-element.38.part, f32[2,64,128]{2,1,0:T(8,128)S(1)} %get-tuple-element.35.mp.params, f32[64,128]{1,0:T(8,128)S(1)} %collective-permute-done.6.got_a, f32[64,128]{1,0:T(8,128)S(1)} %collective-permute-done.7.got_b), custom_call_target="tpu_custom_call" | custom-call | tf_op jit(solution)/shard_map/pallas_call | solution.py:527
  (1 shorter events, 0.0 us)
Async XLA Ops:
  2.3 6.2 %copy-start = (bf16[3,256,256]{2,1,0:T(8,128)(2,1)S(1)}, bf16[3,256,256]{2,1,0:T(8,128)(2,1)}, u32[]{:S(2)}) copy-start(bf16[3,256,256]{2,1,0:T(8,128)(2,1)} %constant.24.clone.rest_9_) | copy-start | bytes 1179652
  2.3 6.2 %copy-start.1 = (bf16[384,384]{1,0:T(8,128)(2,1)S(1)}, bf16[384,384]{1,0:T(8,128)(2,1)}, u32[]{:S(2)}) copy-start(bf16[384,384]{1,0:T(8,128)(2,1)} %constant.23.clone.rest_8_) | copy-start | bytes 884740
  2.3 6.2 %copy-start.2 = (bf16[512,256]{1,0:T(8,128)(2,1)S(1)}, bf16[512,256]{1,0:T(8,128)(2,1)}, u32[]{:S(2)}) copy-start(bf16[512,256]{1,0:T(8,128)(2,1)} %constant.22.clone.rest_7_) | copy-start | bytes 786436
  2.3 6.2 %copy-start.3 = (bf16[512,256]{1,0:T(8,128)(2,1)S(1)}, bf16[512,256]{1,0:T(8,128)(2,1)}, u32[]{:S(2)}) copy-start(bf16[512,256]{1,0:T(8,128)(2,1)} %constant.20.clone.rest_5_) | copy-start | bytes 786436
  2.3 6.2 %copy-start.4 = (f32[2,64,128]{2,1,0:T(8,128)S(1)}, f32[2,64,128]{2,1,0:T(8,128)}, u32[]{:S(2)}) copy-start(f32[2,64,128]{2,1,0:T(8,128)} %params.3) | copy-start | bytes 196612
  2.3 6.2 %copy-start.5 = (bf16[32,16,128]{2,1,0:T(8,128)(2,1)S(1)}, bf16[32,16,128]{2,1,0:T(8,128)(2,1)}, u32[]{:S(2)}) copy-start(bf16[32,16,128]{2,1,0:T(8,128)(2,1)} %constant.21.clone.rest_6_) | copy-start | bytes 393220
  2.4 6.2 %copy-start.6 = (f32[2,64,128]{2,1,0:T(8,128)S(1)}, f32[2,64,128]{2,1,0:T(8,128)}, u32[]{:S(2)}) copy-start(f32[2,64,128]{2,1,0:T(8,128)} %target.3) | copy-start | bytes 196612
  2.4 6.2 %copy-start.7 = (f32[2,64,128]{2,1,0:T(8,128)S(1)}, f32[2,64,128]{2,1,0:T(8,128)}, u32[]{:S(2)}) copy-start(f32[2,64,128]{2,1,0:T(8,128)} %weight.3) | copy-start | bytes 196612
  2.4 6.2 %copy-start.8 = (bf16[80,192]{1,0:T(8,128)(2,1)S(1)}, bf16[80,192]{1,0:T(8,128)(2,1)}, u32[]{:S(2)}) copy-start(bf16[80,192]{1,0:T(8,128)(2,1)} %constant.19.clone.rest_4_) | copy-start | bytes 92164
  2.4 6.2 %copy-start.9 = (bf16[64,240]{1,0:T(8,128)(2,1)S(1)}, bf16[64,240]{1,0:T(8,128)(2,1)}, u32[]{:S(2)}) copy-start(bf16[64,240]{1,0:T(8,128)(2,1)} %constant.18.clone.rest_3_) | copy-start | bytes 92164
  2.4 3.2 %collective-permute-start = (f32[64,128]{1,0:T(8,128)S(1)}, f32[64,128]{1,0:T(8,128)S(1)}, u32[]{:S(2)}, u32[]{:S(2)}) collective-permute-start(f32[64,128]{1,0:T(8,128)S(1)} %get-tuple-element.23), channel_id=1, source_target_pairs={{0,1},{1,2},{2,3},{3,4},{4,5},{5,6},{6,7},{7,8},{8,9},{9,10},{10,1... | collective-permute-start | bytes 98312 | tf_op jit(solution)/shard_map/ppermute | solution.py:554
  4.3 4.2 %collective-permute-start.1 = (f32[64,128]{1,0:T(8,128)S(1)}, f32[64,128]{1,0:T(8,128)S(1)}, u32[]{:S(2)}, u32[]{:S(2)}) collective-permute-start(f32[64,128]{1,0:T(8,128)S(1)} %get-tuple-element.24), channel_id=1, source_target_pairs={{0,16},{1,0},{2,1},{3,2},{4,3},{5,4},{6,5},{7,6},{8,7},{9,8},{10,9... | collective-permute-start | bytes 98312 | tf_op jit(solution)/shard_map/ppermute | solution.py:554
  13.3 1.3 %collective-permute-start.2 = (f32[64,128]{1,0:T(8,128)S(1)}, f32[64,128]{1,0:T(8,128)S(1)}, u32[]{:S(2)}, u32[]{:S(2)}) collective-permute-start(f32[64,128]{1,0:T(8,128)S(1)} %get-tuple-element.33), channel_id=1, source_target_pairs={{0,1},{1,2},{2,3},{3,4},{4,5},{5,6},{6,7},{7,8},{8,9},{9,10},{10,1... | collective-permute-start | bytes 98312 | tf_op jit(solution)/shard_map/ppermute | solution.py:554
  13.4 4.3 %collective-permute-start.3 = (f32[64,128]{1,0:T(8,128)S(1)}, f32[64,128]{1,0:T(8,128)S(1)}, u32[]{:S(2)}, u32[]{:S(2)}) collective-permute-start(f32[64,128]{1,0:T(8,128)S(1)} %get-tuple-element.34), channel_id=1, source_target_pairs={{0,16},{1,0},{2,1},{3,2},{4,3},{5,4},{6,5},{7,6},{8,7},{9,8},{10,9... | collective-permute-start | bytes 98312 | tf_op jit(solution)/shard_map/ppermute | solution.py:554
  17.7 1.3 %collective-permute-start.4 = (f32[64,128]{1,0:T(8,128)S(1)}, f32[64,128]{1,0:T(8,128)S(1)}, u32[]{:S(2)}, u32[]{:S(2)}) collective-permute-start(f32[64,128]{1,0:T(8,128)S(1)} %get-tuple-element.36), channel_id=1, source_target_pairs={{0,1},{1,2},{2,3},{3,4},{4,5},{5,6},{6,7},{7,8},{8,9},{9,10},{10,1... | collective-permute-start | bytes 98312 | tf_op jit(solution)/shard_map/ppermute | solution.py:554
  17.8 4.3 %collective-permute-start.5 = (f32[64,128]{1,0:T(8,128)S(1)}, f32[64,128]{1,0:T(8,128)S(1)}, u32[]{:S(2)}, u32[]{:S(2)}) collective-permute-start(f32[64,128]{1,0:T(8,128)S(1)} %get-tuple-element.37), channel_id=1, source_target_pairs={{0,16},{1,0},{2,1},{3,2},{4,3},{5,4},{6,5},{7,6},{8,7},{9,8},{10,9... | collective-permute-start | bytes 98312 | tf_op jit(solution)/shard_map/ppermute | solution.py:554
  26.8 1.3 %collective-permute-start.6 = (f32[64,128]{1,0:T(8,128)S(1)}, f32[64,128]{1,0:T(8,128)S(1)}, u32[]{:S(2)}, u32[]{:S(2)}) collective-permute-start(f32[64,128]{1,0:T(8,128)S(1)} %get-tuple-element.39), channel_id=1, source_target_pairs={{0,1},{1,2},{2,3},{3,4},{4,5},{5,6},{6,7},{7,8},{8,9},{9,10},{10,1... | collective-permute-start | bytes 98312 | tf_op jit(solution)/shard_map/ppermute | solution.py:554
  26.8 4.3 %collective-permute-start.7 = (f32[64,128]{1,0:T(8,128)S(1)}, f32[64,128]{1,0:T(8,128)S(1)}, u32[]{:S(2)}, u32[]{:S(2)}) collective-permute-start(f32[64,128]{1,0:T(8,128)S(1)} %get-tuple-element.40), channel_id=1, source_target_pairs={{0,16},{1,0},{2,1},{3,2},{4,3},{5,4},{6,5},{7,6},{8,7},{9,8},{10,9... | collective-permute-start | bytes 98312 | tf_op jit(solution)/shard_map/ppermute | solution.py:554

commit v4 on v3

--- a/solution.py
+++ b/solution.py
@@ -20,13 +20,16 @@
 BF16 = jnp.bfloat16
 
 
-def snake_ring(groups, count, step):
-    order = []
+def swap_pairs(groups, count, first):
+    pairs = []
     for g in range(groups):
-        span = range(count) if g % 2 == 0 else range(count - 1, -1, -1)
-        order += [g * count + i for i in span]
-    total = len(order)
-    return [(order[j], order[(j + step) % total]) for j in range(total)]
+        for i in range(count):
+            j = i + 1 if (i - first) % 2 == 0 else i - 1
+            other = g
+            if not 0 <= j < count:
+                j, other = i, g ^ 1 if groups % 2 == 0 else g
+            pairs.append((g * count + i, other * count + j))
+    return pairs
 
 
 def split_np(table):
@@ -371,7 +374,7 @@
     t = dict(zip(names, rest))
     part, send_a, send_b, e_ref = rest[len(names) :]
     flags = read_flags(marks, got_a.shape)
-    prev, nxt = in_order(flags[5], got_a[...], got_b[...])
+    prev, nxt = in_order(flags[5], got_b[...], got_a[...])
     tile = [jnp.tanh(v) for v in (prev, mp[0], mp[1], nxt)]
     dg = core(tb, domain_of(flags, *tile), target, weight, spectra, t, e_ref)
     part[0], part[1], to_next, to_prev = thirds(flags, dg)
@@ -380,7 +383,7 @@
 
 def kernel_update(step, marks, part, params, got_a, got_b, out, send_a, send_b):
     flags = read_flags(marks, got_a.shape)
-    prev, nxt = in_order(flags[5], got_a[...], got_b[...])
+    prev, nxt = in_order(flags[5], got_b[...], got_a[...])
     g0, g1 = own_gradient(flags, part[0], part[1], prev, nxt)
     new0 = stepped(step, params[0], g0)
     new1 = jnp.where(flags[0], stepped(step, params[1], g1), params[1])
@@ -393,7 +396,7 @@
     t = dict(zip(names, rest))
     part, resist_out, send_a, send_b, e_ref = rest[len(names) :]
     flags = read_flags(marks, got_a.shape)
-    prev, nxt = in_order(flags[5], got_a[...], got_b[...])
+    prev, nxt = in_order(flags[5], got_b[...], got_a[...])
     tile = [jnp.tanh(v) for v in (prev, mp[0], mp[1], nxt)]
     def keep(s, resist):
         resist_out[s] = resist if s == 0 else jnp.where(flags[0], resist, 0.0)
@@ -411,7 +414,7 @@
 
 def kernel_last(step, marks, part, params, got_a, got_b, out):
     flags = read_flags(marks, got_a.shape)
-    prev, nxt = in_order(flags[5], got_a[...], got_b[...])
+    prev, nxt = in_order(flags[5], got_b[...], got_a[...])
     g0, g1 = own_gradient(flags, part[0], part[1], prev, nxt)
     out[0] = stepped(step, params[0], g0)
     out[1] = jnp.where(flags[0], stepped(step, params[1], g1), params[1])
@@ -489,7 +492,7 @@
     for move in moves[:3]:
         move.wait()
     both = ids_s[1] >= 0
-    even = lax.rem(lax.axis_index("grp"), 2) == 0
+    even = lax.rem(lax.axis_index("tile"), 2) == 0
     last = jnp.where(both, params_v[1], params_v[0])
     send_a[...], send_b[...] = in_order(even, last, params_v[0])
     flags = [both] + [links_s[s, side] == 1 for side in range(2) for s in range(2)] + [even]
@@ -547,11 +550,11 @@
     tables = [jnp.asarray(tb.arrays[n]) for n in names]
     axes = ("grp", "tile")
 
-    ring_a = snake_ring(groups, count, 1)
-    ring_b = snake_ring(groups, count, -1)
+    inner = swap_pairs(groups, count, 0)
+    outer = swap_pairs(groups, count, 1)
 
     def exchange(a, b):
-        return lax.ppermute(a, axes, ring_a), lax.ppermute(b, axes, ring_b)
+        return lax.ppermute(a, axes, inner), lax.ppermute(b, axes, outer)
 
     whole, tile = mask_params.shape, (rows, cols)
 

time: 32 us -> 30.9 us (0.966)
  waiting for transfers between devices: 13.7 us -> 9.78 us
  starting transfers between devices: 3.54 us -> 6.34 us
    ppermute x8, waiting for transfers between devices: 13.7 us -> 9.78 us  [exchange(): return (lax.ppermute(a, axes, inner), lax.ppermute(b, axes, outer))]
    ppermute x8, starting transfers between devices: 3.54 us -> 6.34 us  [exchange(): return (lax.ppermute(a, axes, inner), lax.ppermute(b, axes, outer))]
  transfers between devices with their start and end apart: 8 -> 8, of which waited for: 7 -> 4; matrix products, arithmetic and copies ran while one was open for 0% -> 0% of each run, Pallas kernels for 6% -> 6%
where the time goes in v4:
time: 30.9 us; the launch traced here: 30.8 us
  Pallas kernels  13.7 us (44%)
  waiting for transfers between devices  9.78 us (32%)
  starting transfers between devices  6.34 us (21%)
  between operations  0.86 us (3%)
    pallas_call x6, Pallas kernels, call(): pl.pallas_call(body, in_specs=[vmem] * len(ins), out_specs=[pl.BlockSpec(...  12.1 us
    ppermute x8, waiting for transfers between devices, exchange(): return (lax.ppermute(a, axes, inner), lax.ppermute(b, axes, outer))  9.78 us
    ppermute x8, starting transfers between devices, exchange(): return (lax.ppermute(a, axes, inner), lax.ppermute(b, axes, outer))  6.34 us
    pallas_call x1, Pallas kernels, choose(): pl.pallas_call(kernel_choose, in_specs=[pl.BlockSpec(memory_space=pltpu.H...  1.64 us
  transfers between devices with their start and end apart: 8, of which 4 were waited for; matrix products, arithmetic and copies ran while one was open for 0% of the time, Pallas kernels for 6%

profile of v4, /device:TPU:21, one launch (start us, length us, event | category | flops | bytes accessed | tf_op | source)
XLA Modules:
  0.0 30.8 jit_solution(16763750138233878994)
XLA Ops:
  0.6 1.6 %shard_map.167 = (f32[8,128]{1,0:T(8,128)S(1)}, f32[64,128]{1,0:T(8,128)S(1)}, f32[64,128]{1,0:T(8,128)S(1)}, f32[3120,65]{1,0:T(8,128)S(1)}, f32[1,24]{1,0:T(1,...) custom-call(s32[2]{0:T(128)} %ids.1, s32[2,2]{1,0:T(2,128)} %links.1, f32[2,64,128]{2,1,0:T(8,128)} %params.3, ...), custom_call_target="tpu_custom_call" | custom-call | tf_op jit(solution)/shard_map/pallas_call | solution.py:513
  2.3 0.0 copy-start
  2.3 0.0 copy-start.1
  2.3 0.0 copy-start.2
  2.3 0.0 copy-start.3
  2.3 0.0 copy-start.4
  2.3 0.0 copy-start.5
  2.4 0.0 copy-start.6
  2.4 0.0 copy-start.7
  2.4 0.0 copy-start.8
  2.4 0.0 copy-start.9
  2.4 0.7 %collective-permute-start = (f32[64,128]{1,0:T(8,128)S(1)}, f32[64,128]{1,0:T(8,128)S(1)}, u32[]{:S(2)}, u32[]{:S(2)}) collective-permute-start(f32[64,128]{1,0:T(8,128)S(1)} %get-tuple-element.23), channel_id=1, source_target_pairs={{0,1},{1,0},{2,3},{3,2},{4,5},{5,4},{6,7},{7,6},{8,9},{9,8},{10,11... | collective-permute-start | bytes 98312 | tf_op jit(solution)/shard_map/ppermute | solution.py:557
  3.1 1.2 %collective-permute-start.1 = (f32[64,128]{1,0:T(8,128)S(1)}, f32[64,128]{1,0:T(8,128)S(1)}, u32[]{:S(2)}, u32[]{:S(2)}) collective-permute-start(f32[64,128]{1,0:T(8,128)S(1)} %get-tuple-element.24), channel_id=1, source_target_pairs={{0,16},{1,2},{2,1},{3,4},{4,3},{5,6},{6,5},{7,8},{8,7},{9,10},{10,... | collective-permute-start | bytes 98312 | tf_op jit(solution)/shard_map/ppermute | solution.py:557
  4.3 1.3 %shard_map.168 = (f32[24,72,128]{2,1,0:T(8,128)S(1)}, f32[24,72,128]{2,1,0:T(8,128)S(1)}, f32[2,72,128]{2,1,0:T(8,128)S(1)}) custom-call(f32[3120,65]{1,0:T(8,128)S(1)} %get-tuple-element.25.kernels, f32[1,24]{1,0:T(1,128)S(1)} %get-tuple-element.26.weights, bf16[4,144,288]{2,1,0:T(8,128)(2,1)S(1)} %get-tuple-element.27.order, ...), custom_call_target="tpu_custom_call" | custom-call | tf_op jit(solution)/shard_map/pallas_call | solution.py:530
  5.7 0.0 collective-permute-done.got_a
  5.7 1.7 %collective-permute-done.1.got_b = f32[64,128]{1,0:T(8,128)S(1)} collective-permute-done((f32[64,128]{1,0:T(8,128)S(1)}, f32[64,128]{1,0:T(8,128)S(1)}, u32[]{:S(2)}, u32[]{:S(2)}) %collective-permute-start.1) | collective-permute-done | bytes 32800 | tf_op jit(solution)/shard_map/ppermute | solution.py:557
  7.4 0.0 copy-done
  7.4 0.0 copy-done.1
  7.4 0.0 copy-done.2
  7.4 0.0 copy-done.3
  7.4 0.0 copy-done.4
  7.4 0.0 copy-done.5
  7.4 0.0 copy-done.6
  7.4 0.0 copy-done.7
  7.4 0.0 copy-done.8
  7.5 0.0 copy-done.9
  7.5 4.7 %shard_map.169 = (f32[2,64,128]{2,1,0:T(8,128)S(1)}, f32[64,128]{1,0:T(8,128)S(1)}, f32[64,128]{1,0:T(8,128)S(1)}) custom-call(f32[8,128]{1,0:T(8,128)S(1)} %get-tuple-element.22.marks, f32[2,64,128]{2,1,0:T(8,128)S(1)} %copy-done.4, f32[64,128]{1,0:T(8,128)S(1)} %collective-permute-done.got_a, f32[64,128]{1,0:T(8,128)S(1)} %collective-permute-done.1.got_b, ...), custom_call_target="tpu_custom_call" | custom-call | tf_op jit(solution)/shard_map/pallas_call | solution.py:530
  12.2 0.1 collective-permute-start.2
  12.3 1.3 %collective-permute-start.3 = (f32[64,128]{1,0:T(8,128)S(1)}, f32[64,128]{1,0:T(8,128)S(1)}, u32[]{:S(2)}, u32[]{:S(2)}) collective-permute-start(f32[64,128]{1,0:T(8,128)S(1)} %get-tuple-element.34), channel_id=1, source_target_pairs={{0,16},{1,2},{2,1},{3,4},{4,3},{5,6},{6,5},{7,8},{8,7},{9,10},{10,... | collective-permute-start | bytes 98312 | tf_op jit(solution)/shard_map/ppermute | solution.py:557
  13.6 0.0 collective-permute-done.2.got_a
  13.6 3.0 %collective-permute-done.3.got_b = f32[64,128]{1,0:T(8,128)S(1)} collective-permute-done((f32[64,128]{1,0:T(8,128)S(1)}, f32[64,128]{1,0:T(8,128)S(1)}, u32[]{:S(2)}, u32[]{:S(2)}) %collective-permute-start.3) | collective-permute-done | bytes 32800 | tf_op jit(solution)/shard_map/ppermute | solution.py:557
  16.6 0.1 collective-permute-start.4
  16.7 1.4 %collective-permute-start.5 = (f32[64,128]{1,0:T(8,128)S(1)}, f32[64,128]{1,0:T(8,128)S(1)}, u32[]{:S(2)}, u32[]{:S(2)}) collective-permute-start(f32[64,128]{1,0:T(8,128)S(1)} %get-tuple-element.37), channel_id=1, source_target_pairs={{0,16},{1,2},{2,1},{3,4},{4,3},{5,6},{6,5},{7,8},{8,7},{9,10},{10,... | collective-permute-start | bytes 98312 | tf_op jit(solution)/shard_map/ppermute | solution.py:557
  18.1 0.0 collective-permute-done.4.got_a
  18.1 2.9 %collective-permute-done.5.got_b = f32[64,128]{1,0:T(8,128)S(1)} collective-permute-done((f32[64,128]{1,0:T(8,128)S(1)}, f32[64,128]{1,0:T(8,128)S(1)}, u32[]{:S(2)}, u32[]{:S(2)}) %collective-permute-start.5) | collective-permute-done | bytes 32800 | tf_op jit(solution)/shard_map/ppermute | solution.py:557
  21.0 4.7 %shard_map.171 = (f32[2,64,128]{2,1,0:T(8,128)S(1)}, f32[2,64,128]{2,1,0:T(8,128)S(1)}, f32[64,128]{1,0:T(8,128)S(1)}, f32[64,128]{1,0:T(8,128)S(1)}) custom-call(f32[8,128]{1,0:T(8,128)S(1)} %get-tuple-element.22.marks, f32[2,64,128]{2,1,0:T(8,128)S(1)} %get-tuple-element.35.mp.params, f32[64,128]{1,0:T(8,128)S(1)} %collective-permute-done.4.got_a, ...), custom_call_target="tpu_custom_call" | custom-call | tf_op jit(solution)/shard_map/pallas_call | solution.py:530
  25.7 0.1 collective-permute-start.6
  25.8 1.5 %collective-permute-start.7 = (f32[64,128]{1,0:T(8,128)S(1)}, f32[64,128]{1,0:T(8,128)S(1)}, u32[]{:S(2)}, u32[]{:S(2)}) collective-permute-start(f32[64,128]{1,0:T(8,128)S(1)} %get-tuple-element.40), channel_id=1, source_target_pairs={{0,16},{1,2},{2,1},{3,4},{4,3},{5,6},{6,5},{7,8},{8,7},{9,10},{10,... | collective-permute-start | bytes 98312 | tf_op jit(solution)/shard_map/ppermute | solution.py:557
  27.2 0.6 %shard_map.173 = f32[2,64,128]{2,1,0:T(8,128)} custom-call(f32[2,64,128]{2,1,0:T(8,128)S(1)} %get-tuple-element.41.image), custom_call_target="tpu_custom_call" | custom-call | tf_op jit(solution)/shard_map/pallas_call | solution.py:530
  27.9 0.0 collective-permute-done.6.got_a
  27.9 2.2 %collective-permute-done.7.got_b = f32[64,128]{1,0:T(8,128)S(1)} collective-permute-done((f32[64,128]{1,0:T(8,128)S(1)}, f32[64,128]{1,0:T(8,128)S(1)}, u32[]{:S(2)}, u32[]{:S(2)}) %collective-permute-start.7) | collective-permute-done | bytes 32800 | tf_op jit(solution)/shard_map/ppermute | solution.py:557
  30.1 0.7 %shard_map.172 = f32[2,64,128]{2,1,0:T(8,128)} custom-call(f32[8,128]{1,0:T(8,128)S(1)} %get-tuple-element.22.marks, f32[2,64,128]{2,1,0:T(8,128)S(1)} %get-tuple-element.38.part, f32[2,64,128]{2,1,0:T(8,128)S(1)} %get-tuple-element.35.mp.params, f32[64,128]{1,0:T(8,128)S(1)} %collective-permute-done.6.got_a, f32[64,128]{1,0:T(8,128)S(1)} %collective-permute-done.7.got_b), custom_call_target="tpu_custom_call" | custom-call | tf_op jit(solution)/shard_map/pallas_call | solution.py:530
  (1 shorter events, 0.0 us)
Async XLA Ops:
  2.3 5.1 %copy-start = (bf16[3,256,256]{2,1,0:T(8,128)(2,1)S(1)}, bf16[3,256,256]{2,1,0:T(8,128)(2,1)}, u32[]{:S(2)}) copy-start(bf16[3,256,256]{2,1,0:T(8,128)(2,1)} %constant.24.clone.rest_9_) | copy-start | bytes 1179652
  2.3 5.1 %copy-start.1 = (bf16[384,384]{1,0:T(8,128)(2,1)S(1)}, bf16[384,384]{1,0:T(8,128)(2,1)}, u32[]{:S(2)}) copy-start(bf16[384,384]{1,0:T(8,128)(2,1)} %constant.23.clone.rest_8_) | copy-start | bytes 884740
  2.3 5.1 %copy-start.2 = (bf16[512,256]{1,0:T(8,128)(2,1)S(1)}, bf16[512,256]{1,0:T(8,128)(2,1)}, u32[]{:S(2)}) copy-start(bf16[512,256]{1,0:T(8,128)(2,1)} %constant.22.clone.rest_7_) | copy-start | bytes 786436
  2.3 5.1 %copy-start.3 = (bf16[512,256]{1,0:T(8,128)(2,1)S(1)}, bf16[512,256]{1,0:T(8,128)(2,1)}, u32[]{:S(2)}) copy-start(bf16[512,256]{1,0:T(8,128)(2,1)} %constant.20.clone.rest_5_) | copy-start | bytes 786436
  2.3 5.1 %copy-start.4 = (f32[2,64,128]{2,1,0:T(8,128)S(1)}, f32[2,64,128]{2,1,0:T(8,128)}, u32[]{:S(2)}) copy-start(f32[2,64,128]{2,1,0:T(8,128)} %params.3) | copy-start | bytes 196612
  2.3 5.1 %copy-start.5 = (bf16[32,16,128]{2,1,0:T(8,128)(2,1)S(1)}, bf16[32,16,128]{2,1,0:T(8,128)(2,1)}, u32[]{:S(2)}) copy-start(bf16[32,16,128]{2,1,0:T(8,128)(2,1)} %constant.21.clone.rest_6_) | copy-start | bytes 393220
  2.4 5.1 %copy-start.6 = (f32[2,64,128]{2,1,0:T(8,128)S(1)}, f32[2,64,128]{2,1,0:T(8,128)}, u32[]{:S(2)}) copy-start(f32[2,64,128]{2,1,0:T(8,128)} %target.3) | copy-start | bytes 196612
  2.4 5.1 %copy-start.7 = (f32[2,64,128]{2,1,0:T(8,128)S(1)}, f32[2,64,128]{2,1,0:T(8,128)}, u32[]{:S(2)}) copy-start(f32[2,64,128]{2,1,0:T(8,128)} %weight.3) | copy-start | bytes 196612
  2.4 5.1 %copy-start.8 = (bf16[80,192]{1,0:T(8,128)(2,1)S(1)}, bf16[80,192]{1,0:T(8,128)(2,1)}, u32[]{:S(2)}) copy-start(bf16[80,192]{1,0:T(8,128)(2,1)} %constant.19.clone.rest_4_) | copy-start | bytes 92164
  2.4 5.1 %copy-start.9 = (bf16[64,240]{1,0:T(8,128)(2,1)S(1)}, bf16[64,240]{1,0:T(8,128)(2,1)}, u32[]{:S(2)}) copy-start(bf16[64,240]{1,0:T(8,128)(2,1)} %constant.18.clone.rest_3_) | copy-start | bytes 92164
  2.4 3.3 %collective-permute-start = (f32[64,128]{1,0:T(8,128)S(1)}, f32[64,128]{1,0:T(8,128)S(1)}, u32[]{:S(2)}, u32[]{:S(2)}) collective-permute-start(f32[64,128]{1,0:T(8,128)S(1)} %get-tuple-element.23), channel_id=1, source_target_pairs={{0,1},{1,0},{2,3},{3,2},{4,5},{5,4},{6,7},{7,6},{8,9},{9,8},{10,11... | collective-permute-start | bytes 98312 | tf_op jit(solution)/shard_map/ppermute | solution.py:557
  3.1 4.2 %collective-permute-start.1 = (f32[64,128]{1,0:T(8,128)S(1)}, f32[64,128]{1,0:T(8,128)S(1)}, u32[]{:S(2)}, u32[]{:S(2)}) collective-permute-start(f32[64,128]{1,0:T(8,128)S(1)} %get-tuple-element.24), channel_id=1, source_target_pairs={{0,16},{1,2},{2,1},{3,4},{4,3},{5,6},{6,5},{7,8},{8,7},{9,10},{10,... | collective-permute-start | bytes 98312 | tf_op jit(solution)/shard_map/ppermute | solution.py:557
  12.2 1.4 %collective-permute-start.2 = (f32[64,128]{1,0:T(8,128)S(1)}, f32[64,128]{1,0:T(8,128)S(1)}, u32[]{:S(2)}, u32[]{:S(2)}) collective-permute-start(f32[64,128]{1,0:T(8,128)S(1)} %get-tuple-element.33), channel_id=1, source_target_pairs={{0,1},{1,0},{2,3},{3,2},{4,5},{5,4},{6,7},{7,6},{8,9},{9,8},{10,11... | collective-permute-start | bytes 98312 | tf_op jit(solution)/shard_map/ppermute | solution.py:557
  12.3 4.3 %collective-permute-start.3 = (f32[64,128]{1,0:T(8,128)S(1)}, f32[64,128]{1,0:T(8,128)S(1)}, u32[]{:S(2)}, u32[]{:S(2)}) collective-permute-start(f32[64,128]{1,0:T(8,128)S(1)} %get-tuple-element.34), channel_id=1, source_target_pairs={{0,16},{1,2},{2,1},{3,4},{4,3},{5,6},{6,5},{7,8},{8,7},{9,10},{10,... | collective-permute-start | bytes 98312 | tf_op jit(solution)/shard_map/ppermute | solution.py:557
  16.6 1.5 %collective-permute-start.4 = (f32[64,128]{1,0:T(8,128)S(1)}, f32[64,128]{1,0:T(8,128)S(1)}, u32[]{:S(2)}, u32[]{:S(2)}) collective-permute-start(f32[64,128]{1,0:T(8,128)S(1)} %get-tuple-element.36), channel_id=1, source_target_pairs={{0,1},{1,0},{2,3},{3,2},{4,5},{5,4},{6,7},{7,6},{8,9},{9,8},{10,11... | collective-permute-start | bytes 98312 | tf_op jit(solution)/shard_map/ppermute | solution.py:557
  16.7 4.3 %collective-permute-start.5 = (f32[64,128]{1,0:T(8,128)S(1)}, f32[64,128]{1,0:T(8,128)S(1)}, u32[]{:S(2)}, u32[]{:S(2)}) collective-permute-start(f32[64,128]{1,0:T(8,128)S(1)} %get-tuple-element.37), channel_id=1, source_target_pairs={{0,16},{1,2},{2,1},{3,4},{4,3},{5,6},{6,5},{7,8},{8,7},{9,10},{10,... | collective-permute-start | bytes 98312 | tf_op jit(solution)/shard_map/ppermute | solution.py:557
  25.7 2.2 %collective-permute-start.6 = (f32[64,128]{1,0:T(8,128)S(1)}, f32[64,128]{1,0:T(8,128)S(1)}, u32[]{:S(2)}, u32[]{:S(2)}) collective-permute-start(f32[64,128]{1,0:T(8,128)S(1)} %get-tuple-element.39), channel_id=1, source_target_pairs={{0,1},{1,0},{2,3},{3,2},{4,5},{5,4},{6,7},{7,6},{8,9},{9,8},{10,11... | collective-permute-start | bytes 98312 | tf_op jit(solution)/shard_map/ppermute | solution.py:557
  25.8 4.3 %collective-permute-start.7 = (f32[64,128]{1,0:T(8,128)S(1)}, f32[64,128]{1,0:T(8,128)S(1)}, u32[]{:S(2)}, u32[]{:S(2)}) collective-permute-start(f32[64,128]{1,0:T(8,128)S(1)} %get-tuple-element.40), channel_id=1, source_target_pairs={{0,16},{1,2},{2,1},{3,4},{4,3},{5,6},{6,5},{7,8},{8,7},{9,10},{10,... | collective-permute-start | bytes 98312 | tf_op jit(solution)/shard_map/ppermute | solution.py:557

commit v5 on v4

--- a/solution.py
+++ b/solution.py
@@ -381,14 +381,38 @@
     send_a[...], send_b[...] = in_order(flags[5], to_next, to_prev)
 
 
-def kernel_update(step, marks, part, params, got_a, got_b, out, send_a, send_b):
-    flags = read_flags(marks, got_a.shape)
-    prev, nxt = in_order(flags[5], got_b[...], got_a[...])
-    g0, g1 = own_gradient(flags, part[0], part[1], prev, nxt)
+def side_gradient(flags, part, got, inward):
+    even = flags[5]
+    zero = jnp.zeros_like(got)
+    ahead, behind = (got, zero) if inward else (zero, got)
+    from_next, from_prev = jnp.where(even, ahead, behind), jnp.where(even, behind, ahead)
+    return own_gradient(flags, part[0], part[1], from_prev, from_next)
+
+
+def kernel_join(marks, part, third, got, out, send):
+    flags = read_flags(marks, got.shape)
+    both, even = flags[0], flags[5]
+    rows = got.shape[0]
+    g0, g1 = side_gradient(flags, part, got[...], True)
+    out[0], out[1] = g0, g1
+    send[:rows] = third[...]
+    send[rows:] = jnp.where(jnp.logical_or(even, jnp.logical_not(both)), g0, g1)
+
+
+def kernel_update(step, marks, part, params, outer, third, got, out, outer_out, send):
+    flags = read_flags(marks, outer.shape)
+    both, l0, l1, r0, r1, even = flags
+    odd, single = jnp.logical_not(even), jnp.logical_not(both)
+    rows = outer.shape[0]
+    g0, g1 = side_gradient(flags, part, got[:rows], False)
     new0 = stepped(step, params[0], g0)
-    new1 = jnp.where(flags[0], stepped(step, params[1], g1), params[1])
+    new1 = jnp.where(both, stepped(step, params[1], g1), params[1])
     out[0], out[1] = new0, new1
-    send_a[...], send_b[...] = in_order(flags[5], jnp.where(flags[0], new1, new0), new0)
+    send[...] = jnp.where(jnp.logical_and(even, both), new1, new0)
+    after = jnp.logical_or(jnp.logical_and(both, r1), jnp.logical_and(single, r0))
+    linked = jnp.logical_or(jnp.logical_and(even, l0), jnp.logical_and(odd, after))
+    beside = got[rows:] + jnp.where(linked, third[...], 0.0)
+    outer_out[...] = stepped(step, outer[...], beside)
 
 
 def kernel_second(tb, names, marks, mp, got_a, got_b, target, weight, *rest):
@@ -553,8 +577,14 @@
     inner = swap_pairs(groups, count, 0)
     outer = swap_pairs(groups, count, 1)
 
+    def swap_inner(v):
+        return lax.ppermute(v, axes, inner)
+
+    def swap_outer(v):
+        return lax.ppermute(v, axes, outer)
+
     def exchange(a, b):
-        return lax.ppermute(a, axes, inner), lax.ppermute(b, axes, outer)
+        return swap_inner(a), swap_outer(b)
 
     whole, tile = mask_params.shape, (rows, cols)
 
@@ -570,14 +600,17 @@
         [whole, tile, tile],
         [field],
     )
-    params, sa, sb = call(
+    part, both_sent = call(
+        kernel_join, [marks, part, sb, swap_inner(sa)], [whole, (2 * rows, cols)]
+    )
+    params, outer_tile, sa = call(
         functools.partial(kernel_update, step),
-        [marks, part, mask_params, *exchange(sa, sb)],
+        [marks, part, mask_params, got[1], sb, swap_outer(both_sent)],
         [whole, tile, tile],
     )
     part, resist, sa, sb = call(
         functools.partial(kernel_second, tb, names),
-        [marks, params, *exchange(sa, sb), target, weight, *arranged, *tables],
+        [marks, params, swap_inner(sa), outer_tile, target, weight, *arranged, *tables],
         [whole, whole, tile, tile],
         [field],
     )

time: 30.9 us -> 29.5 us (0.955)
  starting transfers between devices: 6.34 us -> 5.01 us
    ppermute x8 -> x7, starting transfers between devices: 6.34 us -> 5.01 us  [the longest x3 3.9 us: swap_outer(): return lax.ppermute(v, axes, outer)]
    ppermute x8 -> x7, waiting for transfers between devices: 9.78 us -> 9.65 us  [the longest x3 7.25 us: swap_outer(): return lax.ppermute(v, axes, outer)]
    pallas_call x6 -> x7, Pallas kernels: 12.1 us -> 12.1 us  [call(): pl.pallas_call(body, in_specs=[vmem] * len(ins), out_specs=[pl.BlockSpec(...]
  transfers between devices with their start and end apart: 8 -> 7, of which waited for: 4 -> 5; matrix products, arithmetic and copies ran while one was open for 0% -> 0% of each run, Pallas kernels for 6% -> 7%
where the time goes in v5:
time: 29.5 us; the launch traced here: 29.3 us
  Pallas kernels  13.7 us (46%)
  waiting for transfers between devices  9.65 us (33%)
  starting transfers between devices  5.01 us (17%)
  between operations  0.85 us (3%)
    pallas_call x7, Pallas kernels, call(): pl.pallas_call(body, in_specs=[vmem] * len(ins), out_specs=[pl.BlockSpec(...  12.1 us
    ppermute x3, waiting for transfers between devices, swap_outer(): return lax.ppermute(v, axes, outer)  7.25 us
    ppermute x3, starting transfers between devices, swap_outer(): return lax.ppermute(v, axes, outer)  3.9 us
    ppermute x4, waiting for transfers between devices, swap_inner(): return lax.ppermute(v, axes, inner)  2.39 us
    pallas_call x1, Pallas kernels, choose(): pl.pallas_call(kernel_choose, in_specs=[pl.BlockSpec(memory_space=pltpu.H...  1.64 us
    ppermute x4, starting transfers between devices, swap_inner(): return lax.ppermute(v, axes, inner)  1.11 us
  transfers between devices with their start and end apart: 7, of which 5 were waited for; matrix products, arithmetic and copies ran while one was open for 0% of the time, Pallas kernels for 7%

profile of v5, /device:TPU:21, one launch (start us, length us, event | category | flops | bytes accessed | tf_op | source)
XLA Modules:
  0.0 29.3 jit_solution(4893998617391650013)
XLA Ops:
  0.6 1.6 %shard_map.167 = (f32[8,128]{1,0:T(8,128)S(1)}, f32[64,128]{1,0:T(8,128)S(1)}, f32[64,128]{1,0:T(8,128)S(1)}, f32[3120,65]{1,0:T(8,128)S(1)}, f32[1,24]{1,0:T(1,...) custom-call(s32[2]{0:T(128)} %ids.1, s32[2,2]{1,0:T(2,128)} %links.1, f32[2,64,128]{2,1,0:T(8,128)} %params.3, ...), custom_call_target="tpu_custom_call" | custom-call | tf_op jit(solution)/shard_map/pallas_call | solution.py:537
  2.3 0.0 copy-start
  2.3 0.0 copy-start.1
  2.3 0.0 copy-start.2
  2.3 0.0 copy-start.3
  2.3 0.0 copy-start.4
  2.3 0.0 copy-start.5
  2.4 0.0 copy-start.6
  2.4 0.0 copy-start.7
  2.4 0.0 copy-start.8
  2.4 0.0 copy-start.9
  2.4 0.7 %collective-permute-start = (f32[64,128]{1,0:T(8,128)S(1)}, f32[64,128]{1,0:T(8,128)S(1)}, u32[]{:S(2)}, u32[]{:S(2)}) collective-permute-start(f32[64,128]{1,0:T(8,128)S(1)} %get-tuple-element.25), channel_id=1, source_target_pairs={{0,1},{1,0},{2,3},{3,2},{4,5},{5,4},{6,7},{7,6},{8,9},{9,8},{10,11... | collective-permute-start | bytes 98312 | tf_op jit(solution)/shard_map/ppermute | solution.py:581
  3.1 1.2 %collective-permute-start.1 = (f32[64,128]{1,0:T(8,128)S(1)}, f32[64,128]{1,0:T(8,128)S(1)}, u32[]{:S(2)}, u32[]{:S(2)}) collective-permute-start(f32[64,128]{1,0:T(8,128)S(1)} %get-tuple-element.26), channel_id=1, source_target_pairs={{0,16},{1,2},{2,1},{3,4},{4,3},{5,6},{6,5},{7,8},{8,7},{9,10},{10,... | collective-permute-start | bytes 98312 | tf_op jit(solution)/shard_map/ppermute | solution.py:584
  4.3 1.3 %shard_map.168 = (f32[24,72,128]{2,1,0:T(8,128)S(1)}, f32[24,72,128]{2,1,0:T(8,128)S(1)}, f32[2,72,128]{2,1,0:T(8,128)S(1)}) custom-call(f32[3120,65]{1,0:T(8,128)S(1)} %get-tuple-element.27.kernels, f32[1,24]{1,0:T(1,128)S(1)} %get-tuple-element.28.weights, bf16[4,144,288]{2,1,0:T(8,128)(2,1)S(1)} %get-tuple-element.29.order, ...), custom_call_target="tpu_custom_call" | custom-call | tf_op jit(solution)/shard_map/pallas_call | solution.py:554
  5.7 0.0 collective-permute-done.got_a
  5.7 1.7 %collective-permute-done.1.got_b.outer = f32[64,128]{1,0:T(8,128)S(1)} collective-permute-done((f32[64,128]{1,0:T(8,128)S(1)}, f32[64,128]{1,0:T(8,128)S(1)}, u32[]{:S(2)}, u32[]{:S(2)}) %collective-permute-start.1) | collective-permute-done | bytes 32800 | tf_op jit(solution)/shard_map/ppermute | solution.py:584
  7.4 0.0 copy-done
  7.4 0.0 copy-done.1
  7.4 0.0 copy-done.2
  7.4 0.0 copy-done.3
  7.4 0.0 copy-done.4
  7.4 0.0 copy-done.5
  7.4 0.0 copy-done.6
  7.4 0.0 copy-done.7
  7.4 0.0 copy-done.8
  7.5 0.0 copy-done.9
  7.5 4.7 %shard_map.169 = (f32[2,64,128]{2,1,0:T(8,128)S(1)}, f32[64,128]{1,0:T(8,128)S(1)}, f32[64,128]{1,0:T(8,128)S(1)}) custom-call(f32[8,128]{1,0:T(8,128)S(1)} %get-tuple-element.24.marks, f32[2,64,128]{2,1,0:T(8,128)S(1)} %copy-done.4, f32[64,128]{1,0:T(8,128)S(1)} %collective-permute-done.got_a, f32[64,128]{1,0:T(8,128)S(1)} %collective-permute-done.1.got_b.outer, ...), custom_call_target="tpu_custom_call" | custom-call | tf_op jit(solution)/shard_map/pallas_call | solution.py:554
  12.2 0.1 collective-permute-start.2
  12.3 1.2 %collective-permute-done.2.got = f32[64,128]{1,0:T(8,128)S(1)} collective-permute-done((f32[64,128]{1,0:T(8,128)S(1)}, f32[64,128]{1,0:T(8,128)S(1)}, u32[]{:S(2)}, u32[]{:S(2)}) %collective-permute-start.2) | collective-permute-done | bytes 32800 | tf_op jit(solution)/shard_map/ppermute | solution.py:581
  13.5 1.3 %collective-permute-start.3 = (f32[128,128]{1,0:T(8,128)S(1)}, f32[128,128]{1,0:T(8,128)S(1)}, u32[]{:S(2)}, u32[]{:S(2)}) collective-permute-start(f32[128,128]{1,0:T(8,128)S(1)} %get-tuple-element.38), channel_id=1, source_target_pairs={{0,16},{1,2},{2,1},{3,4},{4,3},{5,6},{6,5},{7,8},{8,7},{9,10},{10,... | collective-permute-start | bytes 196616 | tf_op jit(solution)/shard_map/ppermute | solution.py:584
  14.8 3.3 %collective-permute-done.3.got = f32[128,128]{1,0:T(8,128)S(1)} collective-permute-done((f32[128,128]{1,0:T(8,128)S(1)}, f32[128,128]{1,0:T(8,128)S(1)}, u32[]{:S(2)}, u32[]{:S(2)}) %collective-permute-start.3) | collective-permute-done | bytes 65568 | tf_op jit(solution)/shard_map/ppermute | solution.py:584
  18.2 0.1 collective-permute-start.4
  18.3 1.2 %collective-permute-done.4.got_a = f32[64,128]{1,0:T(8,128)S(1)} collective-permute-done((f32[64,128]{1,0:T(8,128)S(1)}, f32[64,128]{1,0:T(8,128)S(1)}, u32[]{:S(2)}, u32[]{:S(2)}) %collective-permute-start.4) | collective-permute-done | bytes 32800 | tf_op jit(solution)/shard_map/ppermute | solution.py:581
  19.5 4.7 %shard_map.172 = (f32[2,64,128]{2,1,0:T(8,128)S(1)}, f32[2,64,128]{2,1,0:T(8,128)S(1)}, f32[64,128]{1,0:T(8,128)S(1)}, f32[64,128]{1,0:T(8,128)S(1)}) custom-call(f32[8,128]{1,0:T(8,128)S(1)} %get-tuple-element.24.marks, f32[2,64,128]{2,1,0:T(8,128)S(1)} %get-tuple-element.39.mp.params, f32[64,128]{1,0:T(8,128)S(1)} %collective-permute-done.4.got_a, ...), custom_call_target="tpu_custom_call" | custom-call | tf_op jit(solution)/shard_map/pallas_call | solution.py:554
  24.2 0.2 collective-permute-start.5
  24.4 1.4 %collective-permute-start.6 = (f32[64,128]{1,0:T(8,128)S(1)}, f32[64,128]{1,0:T(8,128)S(1)}, u32[]{:S(2)}, u32[]{:S(2)}) collective-permute-start(f32[64,128]{1,0:T(8,128)S(1)} %get-tuple-element.44), channel_id=1, source_target_pairs={{0,16},{1,2},{2,1},{3,4},{4,3},{5,6},{6,5},{7,8},{8,7},{9,10},{10,... | collective-permute-start | bytes 98312 | tf_op jit(solution)/shard_map/ppermute | solution.py:584
  25.8 0.6 %shard_map.174 = f32[2,64,128]{2,1,0:T(8,128)} custom-call(f32[2,64,128]{2,1,0:T(8,128)S(1)} %get-tuple-element.45.image), custom_call_target="tpu_custom_call" | custom-call | tf_op jit(solution)/shard_map/pallas_call | solution.py:554
  26.4 0.0 collective-permute-done.5.got_a
  26.4 2.2 %collective-permute-done.6.got_b = f32[64,128]{1,0:T(8,128)S(1)} collective-permute-done((f32[64,128]{1,0:T(8,128)S(1)}, f32[64,128]{1,0:T(8,128)S(1)}, u32[]{:S(2)}, u32[]{:S(2)}) %collective-permute-start.6) | collective-permute-done | bytes 32800 | tf_op jit(solution)/shard_map/ppermute | solution.py:584
  28.6 0.7 %shard_map.173 = f32[2,64,128]{2,1,0:T(8,128)} custom-call(f32[8,128]{1,0:T(8,128)S(1)} %get-tuple-element.24.marks, f32[2,64,128]{2,1,0:T(8,128)S(1)} %get-tuple-element.42.part, f32[2,64,128]{2,1,0:T(8,128)S(1)} %get-tuple-element.39.mp.params, f32[64,128]{1,0:T(8,128)S(1)} %collective-permute-done.5.got_a, f32[64,128]{1,0:T(8,128)S(1)} %collective-permute-done.6.got_b), custom_call_target="tpu_custom_call" | custom-call | tf_op jit(solution)/shard_map/pallas_call | solution.py:554
  (2 shorter events, 0.1 us)
Async XLA Ops:
  2.3 5.1 %copy-start = (bf16[3,256,256]{2,1,0:T(8,128)(2,1)S(1)}, bf16[3,256,256]{2,1,0:T(8,128)(2,1)}, u32[]{:S(2)}) copy-start(bf16[3,256,256]{2,1,0:T(8,128)(2,1)} %constant.24.clone.rest_9_) | copy-start | bytes 1179652
  2.3 5.1 %copy-start.1 = (bf16[384,384]{1,0:T(8,128)(2,1)S(1)}, bf16[384,384]{1,0:T(8,128)(2,1)}, u32[]{:S(2)}) copy-start(bf16[384,384]{1,0:T(8,128)(2,1)} %constant.23.clone.rest_8_) | copy-start | bytes 884740
  2.3 5.1 %copy-start.2 = (bf16[512,256]{1,0:T(8,128)(2,1)S(1)}, bf16[512,256]{1,0:T(8,128)(2,1)}, u32[]{:S(2)}) copy-start(bf16[512,256]{1,0:T(8,128)(2,1)} %constant.22.clone.rest_7_) | copy-start | bytes 786436
  2.3 5.1 %copy-start.3 = (bf16[512,256]{1,0:T(8,128)(2,1)S(1)}, bf16[512,256]{1,0:T(8,128)(2,1)}, u32[]{:S(2)}) copy-start(bf16[512,256]{1,0:T(8,128)(2,1)} %constant.20.clone.rest_5_) | copy-start | bytes 786436
  2.3 5.1 %copy-start.4 = (f32[2,64,128]{2,1,0:T(8,128)S(1)}, f32[2,64,128]{2,1,0:T(8,128)}, u32[]{:S(2)}) copy-start(f32[2,64,128]{2,1,0:T(8,128)} %params.3) | copy-start | bytes 196612
  2.3 5.1 %copy-start.5 = (bf16[32,16,128]{2,1,0:T(8,128)(2,1)S(1)}, bf16[32,16,128]{2,1,0:T(8,128)(2,1)}, u32[]{:S(2)}) copy-start(bf16[32,16,128]{2,1,0:T(8,128)(2,1)} %constant.21.clone.rest_6_) | copy-start | bytes 393220
  2.4 5.1 %copy-start.6 = (f32[2,64,128]{2,1,0:T(8,128)S(1)}, f32[2,64,128]{2,1,0:T(8,128)}, u32[]{:S(2)}) copy-start(f32[2,64,128]{2,1,0:T(8,128)} %target.3) | copy-start | bytes 196612
  2.4 5.1 %copy-start.7 = (f32[2,64,128]{2,1,0:T(8,128)S(1)}, f32[2,64,128]{2,1,0:T(8,128)}, u32[]{:S(2)}) copy-start(f32[2,64,128]{2,1,0:T(8,128)} %weight.3) | copy-start | bytes 196612
  2.4 5.1 %copy-start.8 = (bf16[80,192]{1,0:T(8,128)(2,1)S(1)}, bf16[80,192]{1,0:T(8,128)(2,1)}, u32[]{:S(2)}) copy-start(bf16[80,192]{1,0:T(8,128)(2,1)} %constant.19.clone.rest_4_) | copy-start | bytes 92164
  2.4 5.1 %copy-start.9 = (bf16[64,240]{1,0:T(8,128)(2,1)S(1)}, bf16[64,240]{1,0:T(8,128)(2,1)}, u32[]{:S(2)}) copy-start(bf16[64,240]{1,0:T(8,128)(2,1)} %constant.18.clone.rest_3_) | copy-start | bytes 92164
  2.4 3.3 %collective-permute-start = (f32[64,128]{1,0:T(8,128)S(1)}, f32[64,128]{1,0:T(8,128)S(1)}, u32[]{:S(2)}, u32[]{:S(2)}) collective-permute-start(f32[64,128]{1,0:T(8,128)S(1)} %get-tuple-element.25), channel_id=1, source_target_pairs={{0,1},{1,0},{2,3},{3,2},{4,5},{5,4},{6,7},{7,6},{8,9},{9,8},{10,11... | collective-permute-start | bytes 98312 | tf_op jit(solution)/shard_map/ppermute | solution.py:581
  3.1 4.2 %collective-permute-start.1 = (f32[64,128]{1,0:T(8,128)S(1)}, f32[64,128]{1,0:T(8,128)S(1)}, u32[]{:S(2)}, u32[]{:S(2)}) collective-permute-start(f32[64,128]{1,0:T(8,128)S(1)} %get-tuple-element.26), channel_id=1, source_target_pairs={{0,16},{1,2},{2,1},{3,4},{4,3},{5,6},{6,5},{7,8},{8,7},{9,10},{10,... | collective-permute-start | bytes 98312 | tf_op jit(solution)/shard_map/ppermute | solution.py:584
  12.2 1.3 %collective-permute-start.2 = (f32[64,128]{1,0:T(8,128)S(1)}, f32[64,128]{1,0:T(8,128)S(1)}, u32[]{:S(2)}, u32[]{:S(2)}) collective-permute-start(f32[64,128]{1,0:T(8,128)S(1)} %get-tuple-element.36), channel_id=1, source_target_pairs={{0,1},{1,0},{2,3},{3,2},{4,5},{5,4},{6,7},{7,6},{8,9},{9,8},{10,11... | collective-permute-start | bytes 98312 | tf_op jit(solution)/shard_map/ppermute | solution.py:581
  13.5 4.7 %collective-permute-start.3 = (f32[128,128]{1,0:T(8,128)S(1)}, f32[128,128]{1,0:T(8,128)S(1)}, u32[]{:S(2)}, u32[]{:S(2)}) collective-permute-start(f32[128,128]{1,0:T(8,128)S(1)} %get-tuple-element.38), channel_id=1, source_target_pairs={{0,16},{1,2},{2,1},{3,4},{4,3},{5,6},{6,5},{7,8},{8,7},{9,10},{10,... | collective-permute-start | bytes 196616 | tf_op jit(solution)/shard_map/ppermute | solution.py:584
  18.2 1.3 %collective-permute-start.4 = (f32[64,128]{1,0:T(8,128)S(1)}, f32[64,128]{1,0:T(8,128)S(1)}, u32[]{:S(2)}, u32[]{:S(2)}) collective-permute-start(f32[64,128]{1,0:T(8,128)S(1)} %get-tuple-element.40), channel_id=1, source_target_pairs={{0,1},{1,0},{2,3},{3,2},{4,5},{5,4},{6,7},{7,6},{8,9},{9,8},{10,11... | collective-permute-start | bytes 98312 | tf_op jit(solution)/shard_map/ppermute | solution.py:581
  24.2 2.2 %collective-permute-start.5 = (f32[64,128]{1,0:T(8,128)S(1)}, f32[64,128]{1,0:T(8,128)S(1)}, u32[]{:S(2)}, u32[]{:S(2)}) collective-permute-start(f32[64,128]{1,0:T(8,128)S(1)} %get-tuple-element.43), channel_id=1, source_target_pairs={{0,1},{1,0},{2,3},{3,2},{4,5},{5,4},{6,7},{7,6},{8,9},{9,8},{10,11... | collective-permute-start | bytes 98312 | tf_op jit(solution)/shard_map/ppermute | solution.py:581
  24.4 4.2 %collective-permute-start.6 = (f32[64,128]{1,0:T(8,128)S(1)}, f32[64,128]{1,0:T(8,128)S(1)}, u32[]{:S(2)}, u32[]{:S(2)}) collective-permute-start(f32[64,128]{1,0:T(8,128)S(1)} %get-tuple-element.44), channel_id=1, source_target_pairs={{0,16},{1,2},{2,1},{3,4},{4,3},{5,6},{6,5},{7,8},{8,7},{9,10},{10,... | collective-permute-start | bytes 98312 | tf_op jit(solution)/shard_map/ppermute | solution.py:584

commit v6 on v5

--- a/solution.py
+++ b/solution.py
@@ -444,17 +444,31 @@
     out[1] = jnp.where(flags[0], stepped(step, params[1], g1), params[1])
 
 
-def kernel_arrange(tb, slots, kernels, weights, order, lanes, out_a, out_b, out_0, padded):
+def kernel_arrange(tb, slots, kernels, *refs):
+    small_far, (out_a, out_b, out_0), small = refs[:3], refs[3:6], refs[6:9]
+    raw, padded, sems, small_sems = refs[9:]
     half, nf = tb.half, tb.nf
     frows, wl = 2 * half + 8, 2 * nf
     bands = kernels.shape[1]
     kcount = out_a.shape[0]
     zb = wl // (2 * slots)
     chunk = RUN * 2 * bands
+    first_moves = [
+        pltpu.make_async_copy(small_far[i], small[i], small_sems.at[i]) for i in range(3)
+    ]
+    moves = []
+    for i in range(kcount // RUN):
+        part = pl.ds(i * chunk, chunk)
+        moves.append(pltpu.make_async_copy(kernels.at[part], raw.at[part], sems.at[i]))
+    for move in moves[:2] + first_moves + moves[2:]:
+        move.start()
     padded[...] = jnp.zeros(padded.shape, F32)
+    weights, order, lanes = small
     inner = lax.rem(lane_of((frows, wl)), zb)
     sign = jnp.where(lane_of((1, wl)) < nf, -1.0, 1.0)
     zeros = [jnp.zeros((frows, wl), F32) for _ in range(2)]
+    for move in first_moves:
+        move.wait()
     roots = jnp.sqrt(weights[...])
 
     def order_rows(i):
@@ -463,7 +477,7 @@
             ks = (i * RUN + j, (i + 1) * RUN + j)
             for n, k in enumerate(ks):
                 window = pl.ds((i + n) * chunk + tb.starts[j], tb.window)
-                padded[k, :, :bands] = kernels[window, :]
+                padded[k, :, :bands] = raw[window, :]
             high, low = split(jnp.concatenate([padded[k] for k in ks], 1))
             v = dot(order[j], jnp.concatenate([high, low], 0))
             for n, k in enumerate(ks):
@@ -485,6 +499,8 @@
 
     waiting = None
     for i in range(0, kcount // RUN, 2):
+        moves[i].wait()
+        moves[i + 1].wait()
         found = order_rows(i)
         if waiting is not None:
             order_lanes(waiting)
@@ -494,26 +510,36 @@
     out_0[1] = -conj(zeros[1], zb)
 
 
-def arrange(tb, slots, parts, ins):
-    bands, kcount = ins[0].shape[1], ins[1].shape[1]
+def arrange(tb, slots, kernels, kernel_weight):
+    kcount, parts, bands = kernels.shape[:3]
     frows, wl = 2 * tb.half + 8, 2 * tb.nf
-    return call(
+    flat = jnp.swapaxes(kernels, 1, 2).reshape(kcount * bands * parts, bands)
+    shapes = [(kcount, frows, wl)] * 2 + [(2, frows, wl)]
+    ins = [flat, kernel_weight[None], jnp.asarray(tb.order), jnp.asarray(tb.lanes)]
+    return pl.pallas_call(
         functools.partial(kernel_arrange, tb, slots),
-        list(ins),
-        [(kcount, frows, wl)] * 2 + [(2, frows, wl)],
-        [pltpu.VMEM((kcount, parts * frows, wl), F32)],
-    )
-
-
-def kernel_choose(ids, links, params, *refs):
-    count = (len(refs) - 7) // 2
-    far, (marks, send_a, send_b) = refs[:count], refs[count : count + 3]
-    near, (ids_s, links_s, params_v, sems) = refs[count + 3 : 2 * count + 3], refs[2 * count + 3 :]
-    pairs = [(ids, ids_s), (links, links_s), (params, params_v), *zip(far, near)]
-    moves = [pltpu.make_async_copy(*pair, sems.at[i]) for i, pair in enumerate(pairs)]
+        in_specs=[pl.BlockSpec(memory_space=pltpu.HBM)] * 4,
+        out_specs=[pl.BlockSpec(memory_space=pltpu.VMEM)] * 3,
+        out_shape=[jax.ShapeDtypeStruct(shape, F32) for shape in shapes],
+        scratch_shapes=[pltpu.VMEM(v.shape, v.dtype) for v in ins[1:]]
+        + [
+            pltpu.VMEM(flat.shape, F32),
+            pltpu.VMEM((kcount, parts * frows, wl), F32),
+            pltpu.SemaphoreType.DMA((kcount // RUN,)),
+            pltpu.SemaphoreType.DMA((3,)),
+        ],
+        compiler_params=pltpu.CompilerParams(vmem_limit_bytes=24 << 20),
+    )(*(pltpu.with_memory_space_constraint(v, pltpu.HBM) for v in ins))
+
+
+def kernel_choose(ids, links, params, marks, send_a, send_b, ids_s, links_s, params_v, sems):
+    moves = [
+        pltpu.make_async_copy(source, target, sems.at[i])
+        for i, (source, target) in enumerate(((ids, ids_s), (links, links_s), (params, params_v)))
+    ]
     for move in moves:
         move.start()
-    for move in moves[:3]:
+    for move in moves:
         move.wait()
     both = ids_s[1] >= 0
     even = lax.rem(lax.axis_index("tile"), 2) == 0
@@ -525,27 +551,24 @@
     for i, flag in enumerate(flags):
         out = jnp.where(row == i, jnp.where(flag, 1.0, 0.0), out)
     marks[...] = out
-    for move in moves[3:]:
-        move.wait()
-
-
-def choose(tile_ids, tile_links, mask_params, far):
+
+
+def choose(*ins):
+    tile_ids, tile_links, mask_params = ins
     tile = mask_params.shape[1:]
-    ins = (tile_ids, tile_links, mask_params, *far)
-    shapes = [jax.ShapeDtypeStruct(s, F32) for s in ((8, tile[1]), tile, tile)]
-    shapes += [jax.ShapeDtypeStruct(v.shape, v.dtype) for v in far]
+    far = pl.BlockSpec(memory_space=pltpu.HBM)
     return pl.pallas_call(
         kernel_choose,
-        in_specs=[pl.BlockSpec(memory_space=pltpu.HBM)] * len(ins),
-        out_specs=[pl.BlockSpec(memory_space=pltpu.VMEM)] * len(shapes),
-        out_shape=shapes,
+        in_specs=[far] * 3,
+        out_specs=[pl.BlockSpec(memory_space=pltpu.VMEM)] * 3,
+        out_shape=[jax.ShapeDtypeStruct(s, F32) for s in ((8, tile[1]), tile, tile)],
         scratch_shapes=[
             pltpu.SMEM(tile_ids.shape, jnp.int32),
             pltpu.SMEM(tile_links.shape, jnp.int32),
             pltpu.VMEM(mask_params.shape, F32),
-            pltpu.SemaphoreType.DMA((len(ins),)),
+            pltpu.SemaphoreType.DMA((3,)),
         ],
-        compiler_params=pltpu.CompilerParams(vmem_limit_bytes=8 << 20),
+        compiler_params=pltpu.CompilerParams(vmem_limit_bytes=4 << 20),
     )(*(pltpu.with_memory_space_constraint(v, pltpu.HBM) for v in ins))
 
 
@@ -588,11 +611,9 @@
 
     whole, tile = mask_params.shape, (rows, cols)
 
-    flat = jnp.swapaxes(kernels, 1, 2).reshape(-1, bands)
-    far = (flat, kernel_weight[None], jnp.asarray(tb.order), jnp.asarray(tb.lanes))
-    marks, sa, sb, *near = choose(tile_ids, tile_links, mask_params, far)
+    marks, sa, sb = choose(tile_ids, tile_links, mask_params)
     got = exchange(sa, sb)
-    arranged = arrange(tb, slots, kernels.shape[1], near)
+    arranged = arrange(tb, slots, kernels, kernel_weight)
     field = pltpu.VMEM((slots, kcount, rows, 2 * cols), F32)
     part, sa, sb = call(
         functools.partial(kernel_first, tb, names),

time: 29.5 us -> 29.7 us (level)
  the two profiles are of different devices: /device:TPU:21 before, /device:TPU:0 now
where the time goes in v6:
time: 29.7 us; the launch traced here: 29.5 us
  Pallas kernels  15.1 us (51%)
  waiting for transfers between devices  7.23 us (24%)
  starting transfers between devices  6.24 us (21%)
  between operations  0.87 us (3%)
    pallas_call x6, Pallas kernels, call(): pl.pallas_call(body, in_specs=[vmem] * len(ins), out_specs=[pl.BlockSpec(...  10.8 us
    ppermute x3, starting transfers between devices, swap_outer(): return lax.ppermute(v, axes, outer)  5.18 us
    ppermute x3, waiting for transfers between devices, swap_outer(): return lax.ppermute(v, axes, outer)  4.97 us
    pallas_call x1, Pallas kernels, arrange(): pl.pallas_call(functools.partial(kernel_arrange, tb, slots), in_specs=[pl...  3.33 us
    ppermute x4, waiting for transfers between devices, swap_inner(): return lax.ppermute(v, axes, inner)  2.26 us
    ppermute x4, starting transfers between devices, swap_inner(): return lax.ppermute(v, axes, inner)  1.06 us
    pallas_call x1, Pallas kernels, choose(): pl.pallas_call(kernel_choose, in_specs=[far] * 3, out_specs=[pl.BlockSpec...  0.98 us
  transfers between devices with their start and end apart: 7, of which 4 were waited for; matrix products, arithmetic and copies ran while one was open for 0% of the time, Pallas kernels for 13%

profile of v6, /device:TPU:0, one launch (start us, length us, event | category | flops | bytes accessed | tf_op | source)
XLA Modules:
  0.0 29.5 jit_solution(14995678488511142796)
XLA Ops:
  0.6 0.0 copy-start
  0.6 0.0 copy-start.1
  0.7 0.0 copy-start.2
  0.7 0.0 copy-start.5
  0.7 0.0 copy-start.3
  0.7 0.0 copy-start.8
  0.7 0.0 copy-start.9
  0.7 0.0 copy-start.4
  0.7 0.0 copy-start.7
  0.7 0.0 copy-start.6
  0.7 1.0 %shard_map.167 = (f32[8,128]{1,0:T(8,128)S(1)}, f32[64,128]{1,0:T(8,128)S(1)}, f32[64,128]{1,0:T(8,128)S(1)}) custom-call(s32[2]{0:T(128)} %ids.1, s32[2,2]{1,0:T(2,128)} %links.1, f32[2,64,128]{2,1,0:T(8,128)} %params.3), custom_call_target="tpu_custom_call" | custom-call | tf_op jit(solution)/shard_map/pallas_call | solution.py:560
  1.7 0.6 %collective-permute-start = (f32[64,128]{1,0:T(8,128)S(1)}, f32[64,128]{1,0:T(8,128)S(1)}, u32[]{:S(2)}, u32[]{:S(2)}) collective-permute-start(f32[64,128]{1,0:T(8,128)S(1)} %get-tuple-element.21), channel_id=1, source_target_pairs={{0,1},{1,0},{2,3},{3,2},{4,5},{5,4},{6,7},{7,6},{8,9},{9,8},{10,11... | collective-permute-start | bytes 98312 | tf_op jit(solution)/shard_map/ppermute | solution.py:604
  2.3 2.6 %collective-permute-start.1 = (f32[64,128]{1,0:T(8,128)S(1)}, f32[64,128]{1,0:T(8,128)S(1)}, u32[]{:S(2)}, u32[]{:S(2)}) collective-permute-start(f32[64,128]{1,0:T(8,128)S(1)} %get-tuple-element.22), channel_id=1, source_target_pairs={{0,16},{1,2},{2,1},{3,4},{4,3},{5,6},{6,5},{7,8},{8,7},{9,10},{10,... | collective-permute-start | bytes 98312 | tf_op jit(solution)/shard_map/ppermute | solution.py:607
  4.8 3.3 %shard_map.168 = (f32[24,72,128]{2,1,0:T(8,128)S(1)}, f32[24,72,128]{2,1,0:T(8,128)S(1)}, f32[2,72,128]{2,1,0:T(8,128)S(1)}) custom-call(f32[3120,65]{1,0:T(8,128)} %bitcast.4, f32[1,24]{1,0:T(1,128)} %bitcast.5, bf16[4,144,288]{2,1,0:T(8,128)(2,1)} %constant.25.clone.refs_1_, bf16[256,256]{1,0:T(8,128)(2,1)} %constant.26.clone.refs_2_), custom_call_target="tpu_custom_call" | custom-call | tf_op jit(solution)/shard_map/pallas_call | solution.py:519
  8.2 0.0 collective-permute-done.got_a
  8.2 0.0 collective-permute-done.1.got_b.outer
  8.2 0.0 copy-done
  8.2 0.0 copy-done.1
  8.2 0.0 copy-done.2
  8.2 0.0 copy-done.5
  8.2 0.0 copy-done.3
  8.3 0.0 copy-done.8
  8.3 0.0 copy-done.9
  8.3 0.0 copy-done.4
  8.3 0.0 copy-done.7
  8.3 0.0 copy-done.6
  8.3 4.7 %shard_map.169 = (f32[2,64,128]{2,1,0:T(8,128)S(1)}, f32[64,128]{1,0:T(8,128)S(1)}, f32[64,128]{1,0:T(8,128)S(1)}) custom-call(f32[8,128]{1,0:T(8,128)S(1)} %get-tuple-element.20.marks, f32[2,64,128]{2,1,0:T(8,128)S(1)} %copy-done.4, f32[64,128]{1,0:T(8,128)S(1)} %collective-permute-done.got_a, f32[64,128]{1,0:T(8,128)S(1)} %collective-permute-done.1.got_b.outer, ...), custom_call_target="tpu_custom_call" | custom-call | tf_op jit(solution)/shard_map/pallas_call | solution.py:577
  13.0 0.2 collective-permute-start.2
  13.2 1.1 %collective-permute-done.2.got = f32[64,128]{1,0:T(8,128)S(1)} collective-permute-done((f32[64,128]{1,0:T(8,128)S(1)}, f32[64,128]{1,0:T(8,128)S(1)}, u32[]{:S(2)}, u32[]{:S(2)}) %collective-permute-start.2) | collective-permute-done | bytes 32800 | tf_op jit(solution)/shard_map/ppermute | solution.py:604
  14.3 1.3 %collective-permute-start.3 = (f32[128,128]{1,0:T(8,128)S(1)}, f32[128,128]{1,0:T(8,128)S(1)}, u32[]{:S(2)}, u32[]{:S(2)}) collective-permute-start(f32[128,128]{1,0:T(8,128)S(1)} %get-tuple-element.30), channel_id=1, source_target_pairs={{0,16},{1,2},{2,1},{3,4},{4,3},{5,6},{6,5},{7,8},{8,7},{9,10},{10,... | collective-permute-start | bytes 196616 | tf_op jit(solution)/shard_map/ppermute | solution.py:607
  15.7 3.0 %collective-permute-done.3.got = f32[128,128]{1,0:T(8,128)S(1)} collective-permute-done((f32[128,128]{1,0:T(8,128)S(1)}, f32[128,128]{1,0:T(8,128)S(1)}, u32[]{:S(2)}, u32[]{:S(2)}) %collective-permute-start.3) | collective-permute-done | bytes 65568 | tf_op jit(solution)/shard_map/ppermute | solution.py:607
  18.7 0.1 collective-permute-start.4
  18.8 1.2 %collective-permute-done.4.got_a = f32[64,128]{1,0:T(8,128)S(1)} collective-permute-done((f32[64,128]{1,0:T(8,128)S(1)}, f32[64,128]{1,0:T(8,128)S(1)}, u32[]{:S(2)}, u32[]{:S(2)}) %collective-permute-start.4) | collective-permute-done | bytes 32800 | tf_op jit(solution)/shard_map/ppermute | solution.py:604
  20.0 4.7 %shard_map.172 = (f32[2,64,128]{2,1,0:T(8,128)S(1)}, f32[2,64,128]{2,1,0:T(8,128)S(1)}, f32[64,128]{1,0:T(8,128)S(1)}, f32[64,128]{1,0:T(8,128)S(1)}) custom-call(f32[8,128]{1,0:T(8,128)S(1)} %get-tuple-element.20.marks, f32[2,64,128]{2,1,0:T(8,128)S(1)} %get-tuple-element.31.mp.params, f32[64,128]{1,0:T(8,128)S(1)} %collective-permute-done.4.got_a, ...), custom_call_target="tpu_custom_call" | custom-call | tf_op jit(solution)/shard_map/pallas_call | solution.py:577
  24.7 0.2 collective-permute-start.5
  24.9 1.3 %collective-permute-start.6 = (f32[64,128]{1,0:T(8,128)S(1)}, f32[64,128]{1,0:T(8,128)S(1)}, u32[]{:S(2)}, u32[]{:S(2)}) collective-permute-start(f32[64,128]{1,0:T(8,128)S(1)} %get-tuple-element.36), channel_id=1, source_target_pairs={{0,16},{1,2},{2,1},{3,4},{4,3},{5,6},{6,5},{7,8},{8,7},{9,10},{10,... | collective-permute-start | bytes 98312 | tf_op jit(solution)/shard_map/ppermute | solution.py:607
  26.2 0.6 %shard_map.174 = f32[2,64,128]{2,1,0:T(8,128)} custom-call(f32[2,64,128]{2,1,0:T(8,128)S(1)} %get-tuple-element.37.image), custom_call_target="tpu_custom_call" | custom-call | tf_op jit(solution)/shard_map/pallas_call | solution.py:577
  26.8 0.0 collective-permute-done.5.got_a
  26.8 2.0 %collective-permute-done.6.got_b = f32[64,128]{1,0:T(8,128)S(1)} collective-permute-done((f32[64,128]{1,0:T(8,128)S(1)}, f32[64,128]{1,0:T(8,128)S(1)}, u32[]{:S(2)}, u32[]{:S(2)}) %collective-permute-start.6) | collective-permute-done | bytes 32800 | tf_op jit(solution)/shard_map/ppermute | solution.py:607
  28.8 0.7 %shard_map.173 = f32[2,64,128]{2,1,0:T(8,128)} custom-call(f32[8,128]{1,0:T(8,128)S(1)} %get-tuple-element.20.marks, f32[2,64,128]{2,1,0:T(8,128)S(1)} %get-tuple-element.34.part, f32[2,64,128]{2,1,0:T(8,128)S(1)} %get-tuple-element.31.mp.params, f32[64,128]{1,0:T(8,128)S(1)} %collective-permute-done.5.got_a, f32[64,128]{1,0:T(8,128)S(1)} %collective-permute-done.6.got_b), custom_call_target="tpu_custom_call" | custom-call | tf_op jit(solution)/shard_map/pallas_call | solution.py:577
  (2 shorter events, 0.1 us)
Async XLA Ops:
  0.6 7.6 %copy-start = (bf16[3,256,256]{2,1,0:T(8,128)(2,1)S(1)}, bf16[3,256,256]{2,1,0:T(8,128)(2,1)}, u32[]{:S(2)}) copy-start(bf16[3,256,256]{2,1,0:T(8,128)(2,1)} %constant.24.clone.rest_9_) | copy-start | bytes 1179652
  0.6 7.6 %copy-start.1 = (bf16[384,384]{1,0:T(8,128)(2,1)S(1)}, bf16[384,384]{1,0:T(8,128)(2,1)}, u32[]{:S(2)}) copy-start(bf16[384,384]{1,0:T(8,128)(2,1)} %constant.23.clone.rest_8_) | copy-start | bytes 884740
  0.7 7.6 %copy-start.2 = (bf16[512,256]{1,0:T(8,128)(2,1)S(1)}, bf16[512,256]{1,0:T(8,128)(2,1)}, u32[]{:S(2)}) copy-start(bf16[512,256]{1,0:T(8,128)(2,1)} %constant.22.clone.rest_7_) | copy-start | bytes 786436
  0.7 7.6 %copy-start.5 = (bf16[32,16,128]{2,1,0:T(8,128)(2,1)S(1)}, bf16[32,16,128]{2,1,0:T(8,128)(2,1)}, u32[]{:S(2)}) copy-start(bf16[32,16,128]{2,1,0:T(8,128)(2,1)} %constant.21.clone.rest_6_) | copy-start | bytes 393220
  0.7 7.6 %copy-start.3 = (bf16[512,256]{1,0:T(8,128)(2,1)S(1)}, bf16[512,256]{1,0:T(8,128)(2,1)}, u32[]{:S(2)}) copy-start(bf16[512,256]{1,0:T(8,128)(2,1)} %constant.20.clone.rest_5_) | copy-start | bytes 786436
  0.7 7.6 %copy-start.8 = (bf16[80,192]{1,0:T(8,128)(2,1)S(1)}, bf16[80,192]{1,0:T(8,128)(2,1)}, u32[]{:S(2)}) copy-start(bf16[80,192]{1,0:T(8,128)(2,1)} %constant.19.clone.rest_4_) | copy-start | bytes 92164
  0.7 7.6 %copy-start.9 = (bf16[64,240]{1,0:T(8,128)(2,1)S(1)}, bf16[64,240]{1,0:T(8,128)(2,1)}, u32[]{:S(2)}) copy-start(bf16[64,240]{1,0:T(8,128)(2,1)} %constant.18.clone.rest_3_) | copy-start | bytes 92164
  0.7 7.6 %copy-start.4 = (f32[2,64,128]{2,1,0:T(8,128)S(1)}, f32[2,64,128]{2,1,0:T(8,128)}, u32[]{:S(2)}) copy-start(f32[2,64,128]{2,1,0:T(8,128)} %params.3) | copy-start | bytes 196612
  0.7 7.6 %copy-start.7 = (f32[2,64,128]{2,1,0:T(8,128)S(1)}, f32[2,64,128]{2,1,0:T(8,128)}, u32[]{:S(2)}) copy-start(f32[2,64,128]{2,1,0:T(8,128)} %weight.3) | copy-start | bytes 196612
  0.7 7.6 %copy-start.6 = (f32[2,64,128]{2,1,0:T(8,128)S(1)}, f32[2,64,128]{2,1,0:T(8,128)}, u32[]{:S(2)}) copy-start(f32[2,64,128]{2,1,0:T(8,128)} %target.3) | copy-start | bytes 196612
  1.7 6.5 %collective-permute-start = (f32[64,128]{1,0:T(8,128)S(1)}, f32[64,128]{1,0:T(8,128)S(1)}, u32[]{:S(2)}, u32[]{:S(2)}) collective-permute-start(f32[64,128]{1,0:T(8,128)S(1)} %get-tuple-element.21), channel_id=1, source_target_pairs={{0,1},{1,0},{2,3},{3,2},{4,5},{5,4},{6,7},{7,6},{8,9},{9,8},{10,11... | collective-permute-start | bytes 98312 | tf_op jit(solution)/shard_map/ppermute | solution.py:604
  2.3 5.9 %collective-permute-start.1 = (f32[64,128]{1,0:T(8,128)S(1)}, f32[64,128]{1,0:T(8,128)S(1)}, u32[]{:S(2)}, u32[]{:S(2)}) collective-permute-start(f32[64,128]{1,0:T(8,128)S(1)} %get-tuple-element.22), channel_id=1, source_target_pairs={{0,16},{1,2},{2,1},{3,4},{4,3},{5,6},{6,5},{7,8},{8,7},{9,10},{10,... | collective-permute-start | bytes 98312 | tf_op jit(solution)/shard_map/ppermute | solution.py:607
  13.0 1.3 %collective-permute-start.2 = (f32[64,128]{1,0:T(8,128)S(1)}, f32[64,128]{1,0:T(8,128)S(1)}, u32[]{:S(2)}, u32[]{:S(2)}) collective-permute-start(f32[64,128]{1,0:T(8,128)S(1)} %get-tuple-element.28), channel_id=1, source_target_pairs={{0,1},{1,0},{2,3},{3,2},{4,5},{5,4},{6,7},{7,6},{8,9},{9,8},{10,11... | collective-permute-start | bytes 98312 | tf_op jit(solution)/shard_map/ppermute | solution.py:604
  14.3 4.3 %collective-permute-start.3 = (f32[128,128]{1,0:T(8,128)S(1)}, f32[128,128]{1,0:T(8,128)S(1)}, u32[]{:S(2)}, u32[]{:S(2)}) collective-permute-start(f32[128,128]{1,0:T(8,128)S(1)} %get-tuple-element.30), channel_id=1, source_target_pairs={{0,16},{1,2},{2,1},{3,4},{4,3},{5,6},{6,5},{7,8},{8,7},{9,10},{10,... | collective-permute-start | bytes 196616 | tf_op jit(solution)/shard_map/ppermute | solution.py:607
  18.7 1.3 %collective-permute-start.4 = (f32[64,128]{1,0:T(8,128)S(1)}, f32[64,128]{1,0:T(8,128)S(1)}, u32[]{:S(2)}, u32[]{:S(2)}) collective-permute-start(f32[64,128]{1,0:T(8,128)S(1)} %get-tuple-element.32), channel_id=1, source_target_pairs={{0,1},{1,0},{2,3},{3,2},{4,5},{5,4},{6,7},{7,6},{8,9},{9,8},{10,11... | collective-permute-start | bytes 98312 | tf_op jit(solution)/shard_map/ppermute | solution.py:604
  24.7 2.1 %collective-permute-start.5 = (f32[64,128]{1,0:T(8,128)S(1)}, f32[64,128]{1,0:T(8,128)S(1)}, u32[]{:S(2)}, u32[]{:S(2)}) collective-permute-start(f32[64,128]{1,0:T(8,128)S(1)} %get-tuple-element.35), channel_id=1, source_target_pairs={{0,1},{1,0},{2,3},{3,2},{4,5},{5,4},{6,7},{7,6},{8,9},{9,8},{10,11... | collective-permute-start | bytes 98312 | tf_op jit(solution)/shard_map/ppermute | solution.py:604
  24.9 3.9 %collective-permute-start.6 = (f32[64,128]{1,0:T(8,128)S(1)}, f32[64,128]{1,0:T(8,128)S(1)}, u32[]{:S(2)}, u32[]{:S(2)}) collective-permute-start(f32[64,128]{1,0:T(8,128)S(1)} %get-tuple-element.36), channel_id=1, source_target_pairs={{0,16},{1,2},{2,1},{3,4},{4,3},{5,6},{6,5},{7,8},{8,7},{9,10},{10,... | collective-permute-start | bytes 98312 | tf_op jit(solution)/shard_map/ppermute | solution.py:607
